TPU v7x, 32 devices: a whole 2x2x4 slice. The times are simulated.
32 devices in a mesh: cond: 4 (over y, x), shard: 8 (over z, core).
Axes of the slice: x: 2, y: 2, z: 4, core: 2. Of those that a mesh axis runs over, the one named last changes fastest.
Arguments:
- expression: bfloat16 [2048, 2048], P(('cond', 'shard')), may hold values from -6 to 6
- responses: bfloat16 [2048, 512], P(('cond', 'shard')), may hold values from -200 to 200
- coef_init: float32 [8192, 512], P(('cond', 'shard')), may hold values from -4 to 4
- dual_init: float32 [8192, 512], P(('cond', 'shard')), may hold values from -3 to 3
- penalty: float32 [2048], P('shard'), may hold values from 0.5 to 4
Outputs:
- coefficients: float32 [8192, 512], P(('cond', 'shard'))
- consensus: float32 [8192, 512], P(('cond', 'shard'))
- duals: float32 [8192, 512], P(('cond', 'shard'))
All inputs are finite; a program needn't handle non-finite values.
Results may differ from a plain program's by a relative error of at most 0.0045.
Values may be sent and summed in bfloat16 or wider, within the bound.
No kernel may reach another device: no remote copies, remote signals or barrier semaphores. Data moves between devices by JAX's collectives and lax.ppermute only.
A program may use at most 64 MiB of HBM per device.

v0:
```python
import jax
import jax.numpy as jnp
from jax import lax
from jax.sharding import PartitionSpec as P

ITERS = 2


rho_weight = 2.0


def shards(expression, responses, coef_init, dual_init, penalty):
    my_rows = coef_init.shape[0]
    row_start = lax.axis_index("shard") * my_rows
    n_cells = expression.shape[0] * lax.axis_size("shard")
    contract = (((0,), (0,)), ((), ()))
    piece_x = lax.all_gather(expression, "shard", axis=0, tiled=True)
    piece_y = lax.all_gather(responses, "shard", axis=0, tiled=True)
    owned = lax.dynamic_slice_in_dim(piece_x, row_start, my_rows, 1)
    gram = lax.dot_general(owned, piece_x, contract, preferred_element_type=jnp.float32)
    cross = lax.dot_general(owned, piece_y, contract, preferred_element_type=jnp.float32)
    gram, cross = (gram, cross)
    gram = gram / n_cells
    cross = cross / n_cells
    diagonal = jnp.diagonal(lax.dynamic_slice_in_dim(gram, row_start, my_rows, 1))
    gram_copy = gram.astype(jnp.bfloat16)
    coef = coef_init
    dual = dual_init
    weights = penalty[:, None]
    consensus = coef
    for step in range(ITERS):
        merged = coef + dual
        norms = jnp.sqrt(lax.psum(merged * merged, "cond"))
        consensus = merged * (1.0 - weights / jnp.maximum(norms, weights))
        dual = merged - consensus
        coef_copy = coef.astype(jnp.bfloat16)
        product = jnp.dot(
            gram_copy,
            lax.all_gather(coef_copy, "shard", axis=0, tiled=True),
            preferred_element_type=jnp.float32,
        )
        coef = coef + (cross + rho_weight * (consensus - dual) - product - rho_weight * coef) / (
            diagonal[:, None] + rho_weight
        )
    return (coef, consensus, dual)


def solution(mesh):
    in_specs = (
        P(("cond", "shard"), None),
        P(("cond", "shard"), None),
        P(("cond", "shard"), None),
        P(("cond", "shard"), None),
        P("shard"),
    )
    out_specs = (P(("cond", "shard"), None), P(("cond", "shard"), None), P(("cond", "shard"), None))
    return jax.shard_map(shards, mesh=mesh, in_specs=in_specs, out_specs=out_specs, check_vma=False)
```

profile of v0, /device:TPU:0, one launch (start us, length us, event | category | flops | bytes accessed | tf_op | source)
XLA Modules:
  0.0 136.4 jit_solution(8652733695643158765)
XLA Ops:
  8.0 0.0 copy-start.1
  8.0 0.0 all-gather.4.cloned.1.call-start
  8.1 0.7 all-gather.4.cloned.1.call-update
  8.7 0.0 all-reduce.3.cloned.1.call-start
  8.8 2.5 %fusion.17 = (f32[256,512]{1,0:T(8,128)}, f32[256,512]{1,0:T(8,128)}, bf16[256,512]{1,0:T(8,128)(2,1)}) fusion(f32[256,512]{1,0:T(8,128)} %param.7, f32[256,512]{1,0:T(8,128)} %param.8), kind=kLoop, calls=%fused_computation.26 | loop fusion | flops 393216 | bytes 2359296 | tf_op jit(solution)/shard_map/mul | solution.py:33
  11.3 0.0 all-reduce.3.cloned.1.call-update
  11.3 0.0 all-gather.6.cloned.1.call-start
  11.4 0.7 all-gather.6.cloned.1.call-update
  12.1 0.0 all-reduce.5.cloned.1.call-start
  12.2 0.0 copy-done.1
  12.2 17.8 %all_gather.13 = bf16[512,512]{1,0:T(8,128)(2,1)S(1)} all-gather(bf16[64,512]{1,0:T(8,128)(2,1)S(1)} %copy-done.1), channel_id=1, replica_groups=mesh['cond'=4,'shard'=8] {'shard'}, dimensions={0}, use_global_device_ids=true | all-gather | bytes 589824 | tf_op jit(solution)/shard_map/all_gather | solution.py:18
  29.9 13.9 %all-gather.4.cloned.1.call-done = bf16[512,2048]{1,0:T(8,128)(2,1)} async-done(((bf16[64,2048]{1,0:T(8,128)(2,1)}), bf16[512,2048]{1,0:T(8,128)(2,1)}) %all-gather.4.cloned.1.call-update) | async-done | bytes 2097168 | tf_op jit(solution)/shard_map/all_gather | solution.py:17
  43.9 2.4 %convolution_multiply_fusion = f32[256,2048]{1,0:T(8,128)S(1)} fusion(bf16[512,2048]{1,0:T(8,128)(2,1)} %all-gather.4.cloned.1.call-done, s32[]{:T(128)S(6)} %select_n.8), kind=kOutput, calls=%fused_computation.1 | convolution fusion | flops 537395200 | bytes 4456452 | tf_op jit(solution)/shard_map/dot_general | solution.py:20
  46.3 0.0 copy-start.2
  46.3 2.3 %gather_fusion = f32[256]{0:T(256)S(1)} fusion(f32[256,256]{1,0:T(8,128)S(1)} %constant_dynamic-slice_fusion, s32[256]{0:T(256)S(1)} %bitcast.5), kind=kCustom, calls=%fused_computation | custom fusion | bytes 4096 | tf_op jit(solution)/shard_map/jit(diagonal)/cond/branch_0_fun/gather | solution.py:25
  48.7 1.3 convolution_multiply_fusion.1
  50.0 10.3 %all-reduce.3.cloned.1.call-done = f32[256,512]{1,0:T(8,128)} async-done(((f32[256,512]{1,0:T(8,128)}), f32[256,512]{1,0:T(8,128)}) %all-reduce.3.cloned.1.call-update) | async-done | bytes 524304 | tf_op jit(solution)/shard_map/psum | solution.py:33
  60.3 14.7 %all-gather.6.cloned.1.call-done = bf16[2048,512]{1,0:T(8,128)(2,1)} async-done(((bf16[256,512]{1,0:T(8,128)(2,1)}), bf16[2048,512]{1,0:T(8,128)(2,1)}) %all-gather.6.cloned.1.call-update) | async-done | bytes 2097168 | tf_op jit(solution)/shard_map/all_gather | solution.py:39
  75.0 0.0 copy-done.2
  75.0 4.2 %fusion.15 = (f32[256,512]{1,0:T(8,128)}, f32[256,512]{1,0:T(8,128)}, bf16[256,512]{1,0:T(8,128)(2,1)}, f32[256,512]{1,0:T(8,128)}) fusion(f32[256,512]{1,0:T(8,128)} %get-tuple-element.8, f32[256,512]{1,0:T(8,128)} %all-reduce.3.cloned.1.call-done, f32[256]{0:T(256)S(1)} %copy-done.2, f32[256,512]{1,0:T(8,128)} %param.7, f32[256]{0:T(256)S(1)} %broadcast_add_fusion, ...), kind=kOutput, calls=%fused_computation.25 | convolution fusion | flops 539492352 | bytes 8128512 | tf_op jit(solution)/shard_map/dot_general | solution.py:37
  79.1 0.0 all-reduce.5.cloned.1.call-update
  79.2 0.0 all-gather.8.cloned.1.call-start
  79.2 0.7 all-gather.8.cloned.1.call-update
  79.9 43.6 %all-reduce.5.cloned.1.call-done = f32[256,512]{1,0:T(8,128)} async-done(((f32[256,512]{1,0:T(8,128)}), f32[256,512]{1,0:T(8,128)}) %all-reduce.5.cloned.1.call-update) | async-done | bytes 524304 | tf_op jit(solution)/shard_map/psum | solution.py:33
  123.5 2.2 %fusion.14 = (f32[256,512]{1,0:T(8,128)S(1)}, f32[256,512]{1,0:T(8,128)}) fusion(f32[256,512]{1,0:T(8,128)} %get-tuple-element.6, f32[256,512]{1,0:T(8,128)} %all-reduce.5.cloned.1.call-done, f32[256]{0:T(256)S(1)} %copy-done.2), kind=kLoop, calls=%fused_computation.24 | loop fusion | flops 655360 | bytes 2098176 | tf_op jit(solution)/shard_map/sub | solution.py:35
  125.8 0.0 copy-start
  125.8 0.0 all-gather.8.cloned.1.call-done
  125.8 3.6 %fusion.4 = f32[256,512]{1,0:T(8,128)} fusion(f32[256,512]{1,0:T(8,128)} %get-tuple-element.11, bf16[2048,512]{1,0:T(8,128)(2,1)} %all-gather.8.cloned.1.call-done, f32[256,512]{1,0:T(8,128)S(1)} %convolution_multiply_fusion.1, f32[256,512]{1,0:T(8,128)} %get-tuple-element.4, f32[256,512]{1,0:T(8,128)S(1)} %get-tuple-element.3, ...), kind=kOutput, calls=%fused_computation.9 | convolution fusion | flops 538443776 | bytes 6816768 | tf_op jit(solution)/shard_map/dot_general | solution.py:37
  129.3 0.0 copy-done
  (3 shorter events, 0.0 us)
Async XLA Ops:
  8.0 4.2 %copy-start.1 = (bf16[64,512]{1,0:T(8,128)(2,1)S(1)}, bf16[64,512]{1,0:T(8,128)(2,1)}, u32[]{:S(2)}) copy-start(bf16[64,512]{1,0:T(8,128)(2,1)} %param.6) | copy-start | bytes 196612
  8.0 35.8 %all-gather.4.cloned.1.call-start = ((), (), s32[]{:S(2)}) async-start(), calls=%async_computation | async-start | bytes 2359296 | tf_op jit(solution)/shard_map/all_gather | solution.py:17
  8.7 51.5 %all-reduce.3.cloned.1.call-start = ((), (), s32[]{:S(2)}) async-start(), calls=%async_computation.1 | async-start | bytes 1048576 | tf_op jit(solution)/shard_map/psum | solution.py:33
  11.3 63.6 %all-gather.6.cloned.1.call-start = ((), (), s32[]{:S(2)}) async-start(), calls=%async_computation.2 | async-start | bytes 2359296 | tf_op jit(solution)/shard_map/all_gather | solution.py:39
  12.1 111.4 %all-reduce.5.cloned.1.call-start = ((), (), s32[]{:S(2)}) async-start(), calls=%async_computation.3 | async-start | bytes 1048576 | tf_op jit(solution)/shard_map/psum | solution.py:33
  46.3 28.7 %copy-start.2 = (f32[256]{0:T(256)S(1)}, f32[256]{0:T(256)}, u32[]{:S(2)}) copy-start(f32[256]{0:T(256)} %param.9) | copy-start | bytes 3076
  79.2 46.6 %all-gather.8.cloned.1.call-start = ((), (), s32[]{:S(2)}) async-start(), calls=%async_computation.4 | async-start | bytes 2359296 | tf_op jit(solution)/shard_map/all_gather | solution.py:39
  125.8 3.6 %copy-start = (f32[256,512]{1,0:T(8,128)}, f32[256,512]{1,0:T(8,128)S(1)}, u32[]{:S(2)}) copy-start(f32[256,512]{1,0:T(8,128)S(1)} %get-tuple-element.3) | copy-start | bytes 1572868
Sparse Core Ops, SparseCore 0:
  10.4 33.3 all-gather.3
  46.0 28.9 all-gather.5
  81.6 28.5 all-gather.7
Sparse Core Ops, SparseCore 1:
  12.8 47.4 all-reduce.2
  79.3 44.2 all-reduce.4
where the time goes:
time: 137 us; the launch traced here: 136 us
  waiting for transfers between devices  84.6 us (62%)
  blocking collectives  17.8 us (13%)
  between operations  15.3 us (11%)
  matrix products  11.4 us (8%)
  other arithmetic  4.75 us (3%)
  local copies, waits for them, and re-layouts  2.38 us (2%)
    psum x2, waiting for transfers between devices, shards(): norms = jnp.sqrt(lax.psum(merged * merged, 'cond'))  53.9 us
    all_gather x1, blocking collectives, shards(): piece_y = lax.all_gather(responses, 'shard', axis=0, tiled=True)  17.8 us
    all_gather x2, waiting for transfers between devices, shards(): lax.all_gather(coef_copy, 'shard', axis=0, tiled=True)  14.7 us
    all_gather x1, waiting for transfers between devices, shards(): piece_x = lax.all_gather(expression, 'shard', axis=0, tiled=True)  13.9 us
    dot_general x2, matrix products, shards(): jnp.dot(gram_copy, lax.all_gather(coef_copy, 'shard', axis=0, tiled=True)...  7.73 us
  transfers between devices with their start and end apart: 5, of which 4 were waited for; matrix products, arithmetic and copies ran while one was open for 8% of the time, Pallas kernels for 0%

commit v1 on v0

v1 whole, which is shorter than its diff:
```python
import jax
import jax.numpy as jnp
from jax import lax
from jax.sharding import PartitionSpec as P

ITERS = 2


rho_weight = 2.0
bf16 = jnp.bfloat16
f32 = jnp.float32


def bits_of(count):
    return count.bit_length() - 1


def swap(value, axis, mask):
    size = lax.axis_size(axis)
    return lax.ppermute(value, axis, [(i, i ^ mask) for i in range(size)])


def cond_sum(squares):
    bits = range(bits_of(lax.axis_size("cond")))
    half = squares.shape[0] // 2
    parts = [squares[:half], squares[half:]]
    for low, high in zip(bits, reversed(bits)):
        parts = [
            part + swap(part.astype(bf16), "cond", 1 << bit).astype(f32)
            for part, bit in zip(parts, (low, high))
        ]
    return jnp.concatenate(parts)


def shards(expression, responses, coef_init, dual_init, penalty):
    cells, targets = responses.shape
    mine = coef_init.shape[0]
    chips = lax.axis_size("shard") // 2
    n_bits = bits_of(chips)
    n_cells = cells * lax.axis_size("shard")
    me = lax.axis_index("shard")
    chip, core = me // 2, me % 2

    by_chip = expression.reshape(cells, chips, 2, mine)
    own, other = [], []
    for k in range(chips):
        rows = lax.dynamic_index_in_dim(by_chip, chip ^ k, 1, keepdims=False)
        pair = jnp.stack([
            lax.dynamic_index_in_dim(rows, core, 1, keepdims=False),
            lax.dynamic_index_in_dim(rows, 1 - core, 1, keepdims=False),
        ])
        if k > 0:
            pair = swap(pair, "shard", 2 * k)
        own.append(pair[0])
        other.append(pair[1])
    own = jnp.concatenate(own)
    other = jnp.concatenate(other)
    across = swap(other, "shard", 1)

    squares = jnp.sum(jnp.square(own.astype(f32)), 0) + jnp.sum(jnp.square(across.astype(f32)), 0)
    step_size = 1.0 / (squares / n_cells + rho_weight)[:, None]

    coef = coef_init
    dual = dual_init
    weights = penalty[:, None]
    consensus = coef
    for step in range(ITERS):
        merged = coef + dual
        coef_copy = coef.astype(bf16)
        coef_other = swap(coef_copy, "shard", 1)
        total = jnp.dot(own, coef_copy, preferred_element_type=f32) + jnp.dot(
            other, coef_other, preferred_element_type=f32
        )
        total = total.reshape(chips, cells, targets)
        total = jnp.concatenate([total[:1] - responses.astype(f32), total[1:]])
        total = total.reshape([2] * n_bits + [cells, targets])
        for bit in range(n_bits - 1):
            axis = n_bits - 1 - bit
            keep = lax.index_in_dim(total, 0, axis, keepdims=False)
            send = lax.index_in_dim(total, 1, axis, keepdims=False)
            total = keep + swap(send.astype(bf16), "shard", 2 << bit).astype(f32)
        if n_bits > 0:
            last = swap(total[::-1].astype(bf16), "shard", 1 << n_bits)
            total = total + last.astype(f32)
        residual = total.astype(bf16)
        for bit in reversed(range(n_bits - 1)):
            residual = jnp.stack([residual, swap(residual, "shard", 2 << bit)], n_bits - 1 - bit)
        residual = residual.reshape(chips * cells, targets)
        residual_other = swap(residual, "shard", 1)
        contract = (((0,), (0,)), ((), ()))
        product = lax.dot_general(own, residual, contract, preferred_element_type=f32) + lax.dot_general(
            across, residual_other, contract, preferred_element_type=f32
        )

        norms = jnp.sqrt(cond_sum(merged * merged))
        consensus = merged * (1.0 - weights / jnp.maximum(norms, weights))
        dual = merged - consensus
        coef = coef + (rho_weight * (consensus - dual) - product / n_cells - rho_weight * coef) * step_size
    return (coef, consensus, dual)


def solution(mesh):
    in_specs = (
        P(("cond", "shard"), None),
        P(("cond", "shard"), None),
        P(("cond", "shard"), None),
        P(("cond", "shard"), None),
        P("shard"),
    )
    out_specs = (P(("cond", "shard"), None), P(("cond", "shard"), None), P(("cond", "shard"), None))
    return jax.shard_map(shards, mesh=mesh, in_specs=in_specs, out_specs=out_specs, check_vma=False)
```

time: 137 us -> 63.1 us (0.46)
  waiting for transfers between devices: 84.6 us -> 35 us
  starting transfers between devices: 0.21 us -> 19.1 us
  blocking collectives: 17.8 us -> 0 us
  between operations: 15.3 us -> 1.18 us
  matrix products: 11.4 us -> 3 us
  other arithmetic: 4.75 us -> 1.15 us
    psum x2 -> x0, waiting for transfers between devices: 53.9 us -> none  [shards(): norms = jnp.sqrt(lax.psum(merged * merged, 'cond'))]
    ppermute x0 -> x22, waiting for transfers between devices: none -> 35 us  [swap(): return lax.ppermute(value, axis, [(i, i ^ mask) for i in range(size)])]
    all_gather x3 -> x0, waiting for transfers between devices: 28.7 us -> none  [the longest x2 14.7 us: shards(): lax.all_gather(coef_copy, 'shard', axis=0, tiled=True)]
    ppermute x0 -> x22, starting transfers between devices: none -> 19.1 us  [swap(): return lax.ppermute(value, axis, [(i, i ^ mask) for i in range(size)])]
    all_gather x1 -> x0, blocking collectives: 17.8 us -> none  [shards(): piece_y = lax.all_gather(responses, 'shard', axis=0, tiled=True)]
    dot_general x4 -> x8, matrix products: 11.4 us -> 3 us  [the longest x2 1.62 us: shards(): lax.dot_general(own, residual, contract, preferred_element_type=f32)]
    mul x1, other arithmetic: 2.52 us -> 0.14 us  [shards(): norms = jnp.sqrt(cond_sum(merged * merged))]
    gather x1 -> x0, local copies, waits for them, and re-layouts: 2.34 us -> none  [shards(): jnp.diagonal(lax.dynamic_slice_in_dim(gram, row_start, my_rows, 1))]
  transfers between devices with their start and end apart: 5 -> 22, of which waited for: 4 -> 13; matrix products, arithmetic and copies ran while one was open for 8% -> 2% of each run, Pallas kernels for 0% -> 0%
where the time goes in v1:
time: 63.1 us; the launch traced here: 62.9 us
  waiting for transfers between devices  35 us (55%)
  starting transfers between devices  19.1 us (30%)
  local copies, waits for them, and re-layouts  3.5 us (6%)
  matrix products  3 us (5%)
  between operations  1.18 us (2%)
  other arithmetic  1.15 us (2%)
    ppermute x22, waiting for transfers between devices, swap(): return lax.ppermute(value, axis, [(i, i ^ mask) for i in range(size)])  35 us
    ppermute x22, starting transfers between devices, swap(): return lax.ppermute(value, axis, [(i, i ^ mask) for i in range(size)])  19.1 us
    dot_general x2, matrix products, shards(): lax.dot_general(own, residual, contract, preferred_element_type=f32)  1.62 us
    unnamed x17, local copies, waits for them, and re-layouts  1.54 us
  transfers between devices with their start and end apart: 22, of which 13 were waited for; matrix products, arithmetic and copies ran while one was open for 2% of the time, Pallas kernels for 0%

profile of v1, /device:TPU:0, one launch (start us, length us, event | category | flops | bytes accessed | tf_op | source)
XLA Modules:
  0.0 62.9 jit_solution(17169742812117193442)
XLA Ops:
  0.7 1.1 %reshape.63 = bf16[64,4,2,256]{3,2,1,0:T(2,128)(2,1)S(1)} reshape(bf16[64,2048]{1,0:T(8,128)(2,1)} %param.5) | data formatting | bytes 524288 | tf_op jit(solution)/shard_map/reshape | solution.py:44
  1.8 0.6 constant_dynamic-slice_fusion.7
  2.5 3.1 %collective-permute-start.4 = (bf16[2,64,256]{2,1,0:T(8,128)(2,1)S(1)}, bf16[2,64,256]{2,1,0:T(8,128)(2,1)S(1)}, u32[]{:S(2)}, u32[]{:S(2)}) collective-permute-start(bf16[2,64,256]{2,1,0:T(8,128)(2,1)S(1)} %pad_maximum_fusion.6), channel_id=1, source_target_pairs={{0,2},{1,3},{2,0},{3,1},{4,6},{5,7},{6,4},{7,5},{8,10},{9,11},{10,... | collective-permute-start | bytes 196616 | tf_op jit(solution)/shard_map/ppermute | solution.py:20
  5.6 2.7 %collective-permute-start.5 = (bf16[2,64,256]{2,1,0:T(8,128)(2,1)S(1)}, bf16[2,64,256]{2,1,0:T(8,128)(2,1)S(1)}, u32[]{:S(2)}, u32[]{:S(2)}) collective-permute-start(bf16[2,64,256]{2,1,0:T(8,128)(2,1)S(1)} %pad_maximum_fusion.7), channel_id=1, source_target_pairs={{0,4},{1,5},{2,6},{3,7},{4,0},{5,1},{6,2},{7,3},{8,12},{9,13},{10,... | collective-permute-start | bytes 196616 | tf_op jit(solution)/shard_map/ppermute | solution.py:20
  8.3 0.1 collective-permute-start.6
  8.4 0.1 fusion.36
  8.6 4.3 %collective-permute-done.5 = bf16[2,64,256]{2,1,0:T(8,128)(2,1)S(1)} collective-permute-done((bf16[2,64,256]{2,1,0:T(8,128)(2,1)S(1)}, bf16[2,64,256]{2,1,0:T(8,128)(2,1)S(1)}, u32[]{:S(2)}, u32[]{:S(2)}) %collective-permute-start.5) | collective-permute-done | bytes 65568 | tf_op jit(solution)/shard_map/ppermute | solution.py:20
  12.9 1.5 %collective-permute-done.6 = bf16[2,64,256]{2,1,0:T(8,128)(2,1)S(1)} collective-permute-done((bf16[2,64,256]{2,1,0:T(8,128)(2,1)S(1)}, bf16[2,64,256]{2,1,0:T(8,128)(2,1)S(1)}, u32[]{:S(2)}, u32[]{:S(2)}) %collective-permute-start.6) | collective-permute-done | bytes 65568 | tf_op jit(solution)/shard_map/ppermute | solution.py:20
  14.4 0.2 fusion.31
  14.6 0.2 convolution_add_fusion.3
  14.9 0.8 %copy-done.4 = bf16[64,512]{1,0:T(8,128)(2,1)S(1)} copy-done((bf16[64,512]{1,0:T(8,128)(2,1)S(1)}, bf16[64,512]{1,0:T(8,128)(2,1)}, u32[]{:S(2)}) %copy-start.4) | copy-done | bytes 65560
  15.8 0.1 collective-permute-start.8
  15.9 5.0 %collective-permute-done.8 = bf16[2,64,512]{2,1,0:T(8,128)(2,1)S(1)} collective-permute-done((bf16[2,64,512]{2,1,0:T(8,128)(2,1)S(1)}, bf16[2,64,512]{2,1,0:T(8,128)(2,1)S(1)}, u32[]{:S(2)}, u32[]{:S(2)}) %collective-permute-start.8) | collective-permute-done | bytes 131104 | tf_op jit(solution)/shard_map/ppermute | solution.py:20
  20.9 1.7 %collective-permute-start.9 = (bf16[2,64,512]{2,1,0:T(8,128)(2,1)S(1)}, bf16[2,64,512]{2,1,0:T(8,128)(2,1)S(1)}, u32[]{:S(2)}, u32[]{:S(2)}) collective-permute-start(bf16[2,64,512]{2,1,0:T(8,128)(2,1)S(1)} %rev.11), channel_id=1, source_target_pairs={{0,4},{1,5},{2,6},{3,7},{4,0},{5,1},{6,2},{7,3},{8,12},{9,13},{10,... | collective-permute-start | bytes 393224 | tf_op jit(solution)/shard_map/ppermute | solution.py:20
  22.7 1.5 %collective-permute-start = (bf16[128,512]{1,0:T(8,128)(2,1)S(1)}, bf16[128,512]{1,0:T(8,128)(2,1)S(1)}, u32[]{:S(2)}, u32[]{:S(2)}) collective-permute-start(bf16[128,512]{1,0:T(8,128)(2,1)S(1)} %get-tuple-element.20), channel_id=1, source_target_pairs={{0,8},{8,0},{16,24},{24,16},{1,9},{9,1},{17,25},{25,17},{2,10},{10... | collective-permute-start | bytes 393224 | tf_op jit(solution)/shard_map/ppermute | solution.py:20
  24.2 1.5 %collective-permute-start.2 = (bf16[128,512]{1,0:T(8,128)(2,1)S(1)}, bf16[128,512]{1,0:T(8,128)(2,1)S(1)}, u32[]{:S(2)}, u32[]{:S(2)}) collective-permute-start(bf16[128,512]{1,0:T(8,128)(2,1)S(1)} %get-tuple-element.21), channel_id=1, source_target_pairs={{0,16},{8,24},{16,0},{24,8},{1,17},{9,25},{17,1},{25,9},{2,18},{10... | collective-permute-start | bytes 393224 | tf_op jit(solution)/shard_map/ppermute | solution.py:20
  25.7 0.1 collective-permute-start.11
  25.9 1.8 %collective-permute-done.9 = bf16[2,64,512]{2,1,0:T(8,128)(2,1)S(1)} collective-permute-done((bf16[2,64,512]{2,1,0:T(8,128)(2,1)S(1)}, bf16[2,64,512]{2,1,0:T(8,128)(2,1)S(1)}, u32[]{:S(2)}, u32[]{:S(2)}) %collective-permute-start.9) | collective-permute-done | bytes 131104 | tf_op jit(solution)/shard_map/ppermute | solution.py:20
  27.8 1.4 %collective-permute-done.2 = bf16[128,512]{1,0:T(8,128)(2,1)S(1)} collective-permute-done((bf16[128,512]{1,0:T(8,128)(2,1)S(1)}, bf16[128,512]{1,0:T(8,128)(2,1)S(1)}, u32[]{:S(2)}, u32[]{:S(2)}) %collective-permute-start.2) | collective-permute-done | bytes 131104 | tf_op jit(solution)/shard_map/ppermute | solution.py:20
  29.2 0.1 fusion.20
  29.3 2.2 %collective-permute-start.1 = (bf16[128,512]{1,0:T(8,128)(2,1)S(1)}, bf16[128,512]{1,0:T(8,128)(2,1)S(1)}, u32[]{:S(2)}, u32[]{:S(2)}) collective-permute-start(bf16[128,512]{1,0:T(8,128)(2,1)S(1)} %get-tuple-element.18), channel_id=1, source_target_pairs={{0,16},{8,24},{16,0},{24,8},{1,17},{9,25},{17,1},{25,9},{2,18},{10... | collective-permute-start | bytes 393224 | tf_op jit(solution)/shard_map/ppermute | solution.py:20
  31.5 0.5 collective-permute-start.3
  32.1 0.7 %collective-permute-done.10 = bf16[2,64,512]{2,1,0:T(8,128)(2,1)S(1)} collective-permute-done((bf16[2,64,512]{2,1,0:T(8,128)(2,1)S(1)}, bf16[2,64,512]{2,1,0:T(8,128)(2,1)S(1)}, u32[]{:S(2)}, u32[]{:S(2)}) %collective-permute-start.10) | collective-permute-done | bytes 131104 | tf_op jit(solution)/shard_map/ppermute | solution.py:20
  32.8 0.1 collective-permute-start.12
  32.9 1.5 %collective-permute-done.1 = bf16[128,512]{1,0:T(8,128)(2,1)S(1)} collective-permute-done((bf16[128,512]{1,0:T(8,128)(2,1)S(1)}, bf16[128,512]{1,0:T(8,128)(2,1)S(1)}, u32[]{:S(2)}, u32[]{:S(2)}) %collective-permute-start.1) | collective-permute-done | bytes 131104 | tf_op jit(solution)/shard_map/ppermute | solution.py:20
  34.5 2.0 %collective-permute-done.3 = bf16[128,512]{1,0:T(8,128)(2,1)S(1)} collective-permute-done((bf16[128,512]{1,0:T(8,128)(2,1)S(1)}, bf16[128,512]{1,0:T(8,128)(2,1)S(1)}, u32[]{:S(2)}, u32[]{:S(2)}) %collective-permute-start.3) | collective-permute-done | bytes 131104 | tf_op jit(solution)/shard_map/ppermute | solution.py:20
  36.5 0.1 convert_add_fusion.6
  36.6 0.2 fusion.39
  36.8 0.7 %copy-done.5 = f32[256]{0:T(256)S(1)} copy-done((f32[256]{0:T(256)S(1)}, f32[256]{0:T(256)}, u32[]{:S(2)}) %copy-start.5) | copy-done | bytes 1048
  37.5 0.5 fusion.34
  38.1 1.5 %collective-permute-done.17 = bf16[256,512]{1,0:T(8,128)(2,1)S(1)} collective-permute-done((bf16[256,512]{1,0:T(8,128)(2,1)S(1)}, bf16[256,512]{1,0:T(8,128)(2,1)S(1)}, u32[]{:S(2)}, u32[]{:S(2)}) %collective-permute-start.17) | collective-permute-done | bytes 262176 | tf_op jit(solution)/shard_map/ppermute | solution.py:20
  39.6 0.2 fusion.30
  39.9 0.2 convolution_add_fusion.1
  40.3 1.6 %collective-permute-start.13 = (bf16[128,512]{1,0:T(8,128)(2,1)S(1)}, bf16[128,512]{1,0:T(8,128)(2,1)S(1)}, u32[]{:S(2)}, u32[]{:S(2)}) collective-permute-start(bf16[128,512]{1,0:T(8,128)(2,1)S(1)} %get-tuple-element.13), channel_id=1, source_target_pairs={{0,8},{8,0},{16,24},{24,16},{1,9},{9,1},{17,25},{25,17},{2,10},{10... | collective-permute-start | bytes 393224 | tf_op jit(solution)/shard_map/ppermute | solution.py:20
  41.9 0.5 collective-permute-start.15
  42.4 3.5 %collective-permute-done.18 = bf16[2,64,512]{2,1,0:T(8,128)(2,1)S(1)} collective-permute-done((bf16[2,64,512]{2,1,0:T(8,128)(2,1)S(1)}, bf16[2,64,512]{2,1,0:T(8,128)(2,1)S(1)}, u32[]{:S(2)}, u32[]{:S(2)}) %collective-permute-start.18) | collective-permute-done | bytes 131104 | tf_op jit(solution)/shard_map/ppermute | solution.py:20
  45.9 1.7 %collective-permute-start.19 = (bf16[2,64,512]{2,1,0:T(8,128)(2,1)S(1)}, bf16[2,64,512]{2,1,0:T(8,128)(2,1)S(1)}, u32[]{:S(2)}, u32[]{:S(2)}) collective-permute-start(bf16[2,64,512]{2,1,0:T(8,128)(2,1)S(1)} %rev.10), channel_id=1, source_target_pairs={{0,4},{1,5},{2,6},{3,7},{4,0},{5,1},{6,2},{7,3},{8,12},{9,13},{10,... | collective-permute-start | bytes 393224 | tf_op jit(solution)/shard_map/ppermute | solution.py:20
  47.7 0.1 collective-permute-start.14
  47.8 1.2 %collective-permute-start.16 = (bf16[128,512]{1,0:T(8,128)(2,1)S(1)}, bf16[128,512]{1,0:T(8,128)(2,1)S(1)}, u32[]{:S(2)}, u32[]{:S(2)}) collective-permute-start(bf16[128,512]{1,0:T(8,128)(2,1)S(1)} %get-tuple-element.12), channel_id=1, source_target_pairs={{0,8},{8,0},{16,24},{24,16},{1,9},{9,1},{17,25},{25,17},{2,10},{10... | collective-permute-start | bytes 393224 | tf_op jit(solution)/shard_map/ppermute | solution.py:20
  49.0 5.4 %collective-permute-done.19 = bf16[2,64,512]{2,1,0:T(8,128)(2,1)S(1)} collective-permute-done((bf16[2,64,512]{2,1,0:T(8,128)(2,1)S(1)}, bf16[2,64,512]{2,1,0:T(8,128)(2,1)S(1)}, u32[]{:S(2)}, u32[]{:S(2)}) %collective-permute-start.19) | collective-permute-done | bytes 131104 | tf_op jit(solution)/shard_map/ppermute | solution.py:20
  54.4 0.1 collective-permute-start.20
  54.5 0.1 convert_add_fusion.2
  54.6 5.2 %collective-permute-done.20 = bf16[2,64,512]{2,1,0:T(8,128)(2,1)S(1)} collective-permute-done((bf16[2,64,512]{2,1,0:T(8,128)(2,1)S(1)}, bf16[2,64,512]{2,1,0:T(8,128)(2,1)S(1)}, u32[]{:S(2)}, u32[]{:S(2)}) %collective-permute-start.20) | collective-permute-done | bytes 131104 | tf_op jit(solution)/shard_map/ppermute | solution.py:20
  59.9 0.1 collective-permute-start.21
  60.0 0.2 fusion.32
  60.3 1.3 %collective-permute-done.21 = bf16[256,512]{1,0:T(8,128)(2,1)S(1)} collective-permute-done((bf16[256,512]{1,0:T(8,128)(2,1)S(1)}, bf16[256,512]{1,0:T(8,128)(2,1)S(1)}, u32[]{:S(2)}, u32[]{:S(2)}) %collective-permute-start.21) | collective-permute-done | bytes 262176 | tf_op jit(solution)/shard_map/ppermute | solution.py:20
  61.5 0.2 fusion.40
  61.8 1.1 %fusion.4 = f32[256,512]{1,0:T(8,128)} fusion(f32[256,512]{1,0:T(8,128)S(1)} %get-tuple-element.37, f32[256,512]{1,0:T(8,128)S(1)} %fusion.40, bf16[256,512]{1,0:T(8,128)(2,1)S(1)} %bitcast.77, f32[256,512]{1,0:T(8,128)S(1)} %get-tuple-element.4, f32[256,512]{1,0:T(8,128)S(1)} %get-tuple-element.3, f32[256]{0:T(256)S(1)} %add_divide_fusion, ...), kind=kOutput, calls=%fused_computation.5 | convolution fusion | flops 68812800 | bytes 3015680 | tf_op jit(solution)/shard_map/dot_general | solution.py:91
  (59 shorter events, 1.1 us)
Async XLA Ops:
  1.8 6.5 %copy-start.3 = (f32[256,512]{1,0:T(8,128)S(1)}, f32[256,512]{1,0:T(8,128)}, u32[]{:S(2)}) copy-start(f32[256,512]{1,0:T(8,128)} %param.7) | copy-start | bytes 1572868
  2.4 5.9 %copy-start.2 = (f32[256,512]{1,0:T(8,128)S(1)}, f32[256,512]{1,0:T(8,128)}, u32[]{:S(2)}) copy-start(f32[256,512]{1,0:T(8,128)} %param.8) | copy-start | bytes 1572868
  2.5 6.2 %collective-permute-start.4 = (bf16[2,64,256]{2,1,0:T(8,128)(2,1)S(1)}, bf16[2,64,256]{2,1,0:T(8,128)(2,1)S(1)}, u32[]{:S(2)}, u32[]{:S(2)}) collective-permute-start(bf16[2,64,256]{2,1,0:T(8,128)(2,1)S(1)} %pad_maximum_fusion.6), channel_id=1, source_target_pairs={{0,2},{1,3},{2,0},{3,1},{4,6},{5,7},{6,4},{7,5},{8,10},{9,11},{10,... | collective-permute-start | bytes 196616 | tf_op jit(solution)/shard_map/ppermute | solution.py:20
  5.6 7.3 %collective-permute-start.5 = (bf16[2,64,256]{2,1,0:T(8,128)(2,1)S(1)}, bf16[2,64,256]{2,1,0:T(8,128)(2,1)S(1)}, u32[]{:S(2)}, u32[]{:S(2)}) collective-permute-start(bf16[2,64,256]{2,1,0:T(8,128)(2,1)S(1)} %pad_maximum_fusion.7), channel_id=1, source_target_pairs={{0,4},{1,5},{2,6},{3,7},{4,0},{5,1},{6,2},{7,3},{8,12},{9,13},{10,... | collective-permute-start | bytes 196616 | tf_op jit(solution)/shard_map/ppermute | solution.py:20
  8.3 6.1 %collective-permute-start.6 = (bf16[2,64,256]{2,1,0:T(8,128)(2,1)S(1)}, bf16[2,64,256]{2,1,0:T(8,128)(2,1)S(1)}, u32[]{:S(2)}, u32[]{:S(2)}) collective-permute-start(bf16[2,64,256]{2,1,0:T(8,128)(2,1)S(1)} %pad_maximum_fusion.8), channel_id=1, source_target_pairs={{0,6},{1,7},{2,4},{3,5},{4,2},{5,3},{6,0},{7,1},{8,14},{9,15},{10,... | collective-permute-start | bytes 196616 | tf_op jit(solution)/shard_map/ppermute | solution.py:20
  8.5 5.9 %collective-permute-start.7 = (bf16[256,512]{1,0:T(8,128)(2,1)S(1)}, bf16[256,512]{1,0:T(8,128)(2,1)S(1)}, u32[]{:S(2)}, u32[]{:S(2)}) collective-permute-start(bf16[256,512]{1,0:T(8,128)(2,1)S(1)} %get-tuple-element.22), channel_id=1, source_target_pairs={{0,1},{1,0},{2,3},{3,2},{4,5},{5,4},{6,7},{7,6},{8,9},{9,8},{10,11... | collective-permute-start | bytes 786440 | tf_op jit(solution)/shard_map/ppermute | solution.py:20
  14.9 0.8 %copy-start.4 = (bf16[64,512]{1,0:T(8,128)(2,1)S(1)}, bf16[64,512]{1,0:T(8,128)(2,1)}, u32[]{:S(2)}) copy-start(bf16[64,512]{1,0:T(8,128)(2,1)} %param.6) | copy-start | bytes 196612
  15.8 5.0 %collective-permute-start.8 = (bf16[2,64,512]{2,1,0:T(8,128)(2,1)S(1)}, bf16[2,64,512]{2,1,0:T(8,128)(2,1)S(1)}, u32[]{:S(2)}, u32[]{:S(2)}) collective-permute-start(bf16[2,64,512]{2,1,0:T(8,128)(2,1)S(1)} %fusion.26), channel_id=1, source_target_pairs={{0,2},{1,3},{2,0},{3,1},{4,6},{5,7},{6,4},{7,5},{8,10},{9,11},{10,... | collective-permute-start | bytes 393224 | tf_op jit(solution)/shard_map/ppermute | solution.py:20
  20.9 6.8 %collective-permute-start.9 = (bf16[2,64,512]{2,1,0:T(8,128)(2,1)S(1)}, bf16[2,64,512]{2,1,0:T(8,128)(2,1)S(1)}, u32[]{:S(2)}, u32[]{:S(2)}) collective-permute-start(bf16[2,64,512]{2,1,0:T(8,128)(2,1)S(1)} %rev.11), channel_id=1, source_target_pairs={{0,4},{1,5},{2,6},{3,7},{4,0},{5,1},{6,2},{7,3},{8,12},{9,13},{10,... | collective-permute-start | bytes 393224 | tf_op jit(solution)/shard_map/ppermute | solution.py:20
  22.7 5.1 %collective-permute-start = (bf16[128,512]{1,0:T(8,128)(2,1)S(1)}, bf16[128,512]{1,0:T(8,128)(2,1)S(1)}, u32[]{:S(2)}, u32[]{:S(2)}) collective-permute-start(bf16[128,512]{1,0:T(8,128)(2,1)S(1)} %get-tuple-element.20), channel_id=1, source_target_pairs={{0,8},{8,0},{16,24},{24,16},{1,9},{9,1},{17,25},{25,17},{2,10},{10... | collective-permute-start | bytes 393224 | tf_op jit(solution)/shard_map/ppermute | solution.py:20
  24.2 5.0 %collective-permute-start.2 = (bf16[128,512]{1,0:T(8,128)(2,1)S(1)}, bf16[128,512]{1,0:T(8,128)(2,1)S(1)}, u32[]{:S(2)}, u32[]{:S(2)}) collective-permute-start(bf16[128,512]{1,0:T(8,128)(2,1)S(1)} %get-tuple-element.21), channel_id=1, source_target_pairs={{0,16},{8,24},{16,0},{24,8},{1,17},{9,25},{17,1},{25,9},{2,18},{10... | collective-permute-start | bytes 393224 | tf_op jit(solution)/shard_map/ppermute | solution.py:20
  25.7 6.3 %collective-permute-start.11 = (bf16[256,256]{1,0:T(8,128)(2,1)S(1)}, bf16[256,256]{1,0:T(8,128)(2,1)S(1)}, u32[]{:S(2)}, u32[]{:S(2)}) collective-permute-start(bf16[256,256]{1,0:T(8,128)(2,1)S(1)} %pad_maximum_fusion.5), channel_id=1, source_target_pairs={{0,1},{1,0},{2,3},{3,2},{4,5},{5,4},{6,7},{7,6},{8,9},{9,8},{10,11... | collective-permute-start | bytes 393224 | tf_op jit(solution)/shard_map/ppermute | solution.py:20
  27.7 5.0 %collective-permute-start.10 = (bf16[2,64,512]{2,1,0:T(8,128)(2,1)S(1)}, bf16[2,64,512]{2,1,0:T(8,128)(2,1)S(1)}, u32[]{:S(2)}, u32[]{:S(2)}) collective-permute-start(bf16[2,64,512]{2,1,0:T(8,128)(2,1)S(1)} %add_convert_fusion.1), channel_id=1, source_target_pairs={{0,2},{1,3},{2,0},{3,1},{4,6},{5,7},{6,4},{7,5},{8,10},{9,11},{10,... | collective-permute-start | bytes 393224 | tf_op jit(solution)/shard_map/ppermute | solution.py:20
  29.3 5.2 %collective-permute-start.1 = (bf16[128,512]{1,0:T(8,128)(2,1)S(1)}, bf16[128,512]{1,0:T(8,128)(2,1)S(1)}, u32[]{:S(2)}, u32[]{:S(2)}) collective-permute-start(bf16[128,512]{1,0:T(8,128)(2,1)S(1)} %get-tuple-element.18), channel_id=1, source_target_pairs={{0,16},{8,24},{16,0},{24,8},{1,17},{9,25},{17,1},{25,9},{2,18},{10... | collective-permute-start | bytes 393224 | tf_op jit(solution)/shard_map/ppermute | solution.py:20
  31.5 5.0 %collective-permute-start.3 = (bf16[128,512]{1,0:T(8,128)(2,1)S(1)}, bf16[128,512]{1,0:T(8,128)(2,1)S(1)}, u32[]{:S(2)}, u32[]{:S(2)}) collective-permute-start(bf16[128,512]{1,0:T(8,128)(2,1)S(1)} %get-tuple-element.19), channel_id=1, source_target_pairs={{0,8},{8,0},{16,24},{24,16},{1,9},{9,1},{17,25},{25,17},{2,10},{10... | collective-permute-start | bytes 393224 | tf_op jit(solution)/shard_map/ppermute | solution.py:20
  32.8 3.8 %collective-permute-start.12 = (bf16[256,512]{1,0:T(8,128)(2,1)S(1)}, bf16[256,512]{1,0:T(8,128)(2,1)S(1)}, u32[]{:S(2)}, u32[]{:S(2)}) collective-permute-start(bf16[256,512]{1,0:T(8,128)(2,1)S(1)} %bitcast.88), channel_id=1, source_target_pairs={{0,1},{1,0},{2,3},{3,2},{4,5},{5,4},{6,7},{7,6},{8,9},{9,8},{10,11... | collective-permute-start | bytes 786440 | tf_op jit(solution)/shard_map/ppermute | solution.py:20
  36.8 0.7 %copy-start.5 = (f32[256]{0:T(256)S(1)}, f32[256]{0:T(256)}, u32[]{:S(2)}) copy-start(f32[256]{0:T(256)} %param.9) | copy-start | bytes 3076
  38.0 1.6 %collective-permute-start.17 = (bf16[256,512]{1,0:T(8,128)(2,1)S(1)}, bf16[256,512]{1,0:T(8,128)(2,1)S(1)}, u32[]{:S(2)}, u32[]{:S(2)}) collective-permute-start(bf16[256,512]{1,0:T(8,128)(2,1)S(1)} %get-tuple-element.15), channel_id=1, source_target_pairs={{0,1},{1,0},{2,3},{3,2},{4,5},{5,4},{6,7},{7,6},{8,9},{9,8},{10,11... | collective-permute-start | bytes 786440 | tf_op jit(solution)/shard_map/ppermute | solution.py:20
  40.2 5.6 %collective-permute-start.18 = (bf16[2,64,512]{2,1,0:T(8,128)(2,1)S(1)}, bf16[2,64,512]{2,1,0:T(8,128)(2,1)S(1)}, u32[]{:S(2)}, u32[]{:S(2)}) collective-permute-start(bf16[2,64,512]{2,1,0:T(8,128)(2,1)S(1)} %fusion.27), channel_id=1, source_target_pairs={{0,2},{1,3},{2,0},{3,1},{4,6},{5,7},{6,4},{7,5},{8,10},{9,11},{10,... | collective-permute-start | bytes 393224 | tf_op jit(solution)/shard_map/ppermute | solution.py:20
  40.3 7.2 %collective-permute-start.13 = (bf16[128,512]{1,0:T(8,128)(2,1)S(1)}, bf16[128,512]{1,0:T(8,128)(2,1)S(1)}, u32[]{:S(2)}, u32[]{:S(2)}) collective-permute-start(bf16[128,512]{1,0:T(8,128)(2,1)S(1)} %get-tuple-element.13), channel_id=1, source_target_pairs={{0,8},{8,0},{16,24},{24,16},{1,9},{9,1},{17,25},{25,17},{2,10},{10... | collective-permute-start | bytes 393224 | tf_op jit(solution)/shard_map/ppermute | solution.py:20
  41.9 5.7 %collective-permute-start.15 = (bf16[128,512]{1,0:T(8,128)(2,1)S(1)}, bf16[128,512]{1,0:T(8,128)(2,1)S(1)}, u32[]{:S(2)}, u32[]{:S(2)}) collective-permute-start(bf16[128,512]{1,0:T(8,128)(2,1)S(1)} %get-tuple-element.14), channel_id=1, source_target_pairs={{0,16},{8,24},{16,0},{24,8},{1,17},{9,25},{17,1},{25,9},{2,18},{10... | collective-permute-start | bytes 393224 | tf_op jit(solution)/shard_map/ppermute | solution.py:20
  45.9 8.5 %collective-permute-start.19 = (bf16[2,64,512]{2,1,0:T(8,128)(2,1)S(1)}, bf16[2,64,512]{2,1,0:T(8,128)(2,1)S(1)}, u32[]{:S(2)}, u32[]{:S(2)}) collective-permute-start(bf16[2,64,512]{2,1,0:T(8,128)(2,1)S(1)} %rev.10), channel_id=1, source_target_pairs={{0,4},{1,5},{2,6},{3,7},{4,0},{5,1},{6,2},{7,3},{8,12},{9,13},{10,... | collective-permute-start | bytes 393224 | tf_op jit(solution)/shard_map/ppermute | solution.py:20
  47.7 6.9 %collective-permute-start.14 = (bf16[128,512]{1,0:T(8,128)(2,1)S(1)}, bf16[128,512]{1,0:T(8,128)(2,1)S(1)}, u32[]{:S(2)}, u32[]{:S(2)}) collective-permute-start(bf16[128,512]{1,0:T(8,128)(2,1)S(1)} %get-tuple-element.11), channel_id=1, source_target_pairs={{0,16},{8,24},{16,0},{24,8},{1,17},{9,25},{17,1},{25,9},{2,18},{10... | collective-permute-start | bytes 393224 | tf_op jit(solution)/shard_map/ppermute | solution.py:20
  47.8 6.7 %collective-permute-start.16 = (bf16[128,512]{1,0:T(8,128)(2,1)S(1)}, bf16[128,512]{1,0:T(8,128)(2,1)S(1)}, u32[]{:S(2)}, u32[]{:S(2)}) collective-permute-start(bf16[128,512]{1,0:T(8,128)(2,1)S(1)} %get-tuple-element.12), channel_id=1, source_target_pairs={{0,8},{8,0},{16,24},{24,16},{1,9},{9,1},{17,25},{25,17},{2,10},{10... | collective-permute-start | bytes 393224 | tf_op jit(solution)/shard_map/ppermute | solution.py:20
  54.4 5.4 %collective-permute-start.20 = (bf16[2,64,512]{2,1,0:T(8,128)(2,1)S(1)}, bf16[2,64,512]{2,1,0:T(8,128)(2,1)S(1)}, u32[]{:S(2)}, u32[]{:S(2)}) collective-permute-start(bf16[2,64,512]{2,1,0:T(8,128)(2,1)S(1)} %add_convert_fusion), channel_id=1, source_target_pairs={{0,2},{1,3},{2,0},{3,1},{4,6},{5,7},{6,4},{7,5},{8,10},{9,11},{10,... | collective-permute-start | bytes 393224 | tf_op jit(solution)/shard_map/ppermute | solution.py:20
  59.9 1.6 %collective-permute-start.21 = (bf16[256,512]{1,0:T(8,128)(2,1)S(1)}, bf16[256,512]{1,0:T(8,128)(2,1)S(1)}, u32[]{:S(2)}, u32[]{:S(2)}) collective-permute-start(bf16[256,512]{1,0:T(8,128)(2,1)S(1)} %bitcast.76), channel_id=1, source_target_pairs={{0,1},{1,0},{2,3},{3,2},{4,5},{5,4},{6,7},{7,6},{8,9},{9,8},{10,11... | collective-permute-start | bytes 786440 | tf_op jit(solution)/shard_map/ppermute | solution.py:20
  60.2 2.6 %copy-start = (f32[256,512]{1,0:T(8,128)}, f32[256,512]{1,0:T(8,128)S(1)}, u32[]{:S(2)}) copy-start(f32[256,512]{1,0:T(8,128)S(1)} %get-tuple-element.3) | copy-start | bytes 1572868
  60.3 2.6 %copy-start.1 = (f32[256,512]{1,0:T(8,128)}, f32[256,512]{1,0:T(8,128)S(1)}, u32[]{:S(2)}) copy-start(f32[256,512]{1,0:T(8,128)S(1)} %get-tuple-element.4) | copy-start | bytes 1572868

commit v2 on v0

v2 whole, which is shorter than its diff:
```python
import jax
import jax.numpy as jnp
from jax import lax
from jax.sharding import PartitionSpec as P

ITERS = 2


rho_weight = 2.0
bf16 = jnp.bfloat16
f32 = jnp.float32


def swap(value, axis, mask, what):
    size = lax.axis_size(axis)
    with jax.named_scope(what):
        return lax.ppermute(value, axis, [(i, i ^ mask) for i in range(size)])


def together(*values):
    return lax.optimization_barrier(values)


def shards(expression, responses, coef_init, dual_init, penalty):
    cells, targets = responses.shape
    mine = coef_init.shape[0]
    chips = lax.axis_size("shard") // 2
    cond_bits = lax.axis_size("cond").bit_length() - 1
    n_cells = cells * lax.axis_size("shard")
    me = lax.axis_index("shard")
    chip, core = me // 2, me % 2
    far_first = list(reversed(range(1, chips)))
    contract = (((0,), (0,)), ((), ()))

    def dot(x, c):
        return jnp.dot(x, c, preferred_element_type=f32)

    def columns(k, side):
        start = ((chip ^ k) * 2 + (core ^ side)) * mine
        return lax.dynamic_slice_in_dim(expression, start, mine, 1)

    coef_copy = coef_init.astype(bf16)
    coef_other = swap(coef_copy, "shard", 1, "coef_core")
    pairs = [jnp.stack([columns(k, 0), columns(k, 1)]) for k in range(chips)]
    for k in far_first:
        pairs[k] = swap(pairs[k], "shard", 2 * k, f"cells{k}")
    weights = jnp.broadcast_to(penalty[:, None], coef_init.shape)
    response_rows = responses.astype(f32)
    pairs, weights, response_rows = together(pairs, weights, response_rows)
    own = jnp.concatenate([p[0] for p in pairs])
    other = jnp.concatenate([p[1] for p in pairs])

    coef = coef_init
    dual = dual_init
    for step in range(ITERS):
        merged = coef + dual
        squares = merged * merged
        if cond_bits > 0:
            squares = squares + swap(squares.astype(bf16), "cond", 1, "squares0").astype(f32)
        if step > 0:
            coef_copy = coef.astype(bf16)
            coef_other = swap(coef_copy, "shard", 1, "coef_core")
        fitted = (dot(own, coef_copy) + dot(other, coef_other)).reshape(chips, cells, targets)
        total = fitted[0] - response_rows
        leaving = fitted.astype(bf16)
        leaving, total, held, squares = together(leaving, total, other, squares) if step == 0 else (*together(leaving, total), other, squares)
        arrived = [swap(leaving[k], "shard", 2 * k, f"fit{k}") for k in far_first]
        for bit in range(1, cond_bits):
            squares = squares + swap(squares.astype(bf16), "cond", 1 << bit, f"squares{bit}").astype(f32)
        for part in arrived:
            total = total + part.astype(f32)
        residual = [total.astype(bf16)] * chips
        for k in far_first:
            residual[k] = swap(residual[0], "shard", 2 * k, f"residual{k}")
        if step == 0:
            across = swap(held, "shard", 1, "cells_core")
            diagonal = jnp.sum(jnp.square(own.astype(f32)), 0) + jnp.sum(jnp.square(across.astype(f32)), 0)
            step_size = 1.0 / (diagonal / n_cells + rho_weight)[:, None]
            residual, squares, step_size, across = together(residual, squares, step_size, across)
        else:
            residual, squares = together(residual, squares)
        residual = jnp.concatenate(residual)
        residual_other = swap(residual, "shard", 1, "residual_core")
        product = lax.dot_general(own, residual, contract, preferred_element_type=f32) + lax.dot_general(
            across, residual_other, contract, preferred_element_type=f32
        )

        norms = jnp.sqrt(squares)
        consensus = merged * (1.0 - weights / jnp.maximum(norms, weights))
        dual = merged - consensus
        coef = coef + (rho_weight * (consensus - dual) - product / n_cells - rho_weight * coef) * step_size
    return (coef, consensus, dual)


def solution(mesh):
    in_specs = (
        P(("cond", "shard"), None),
        P(("cond", "shard"), None),
        P(("cond", "shard"), None),
        P(("cond", "shard"), None),
        P("shard"),
    )
    out_specs = (P(("cond", "shard"), None), P(("cond", "shard"), None), P(("cond", "shard"), None))
    return jax.shard_map(shards, mesh=mesh, in_specs=in_specs, out_specs=out_specs, check_vma=False)
```

time: 137 us -> 57.5 us (0.42)
  waiting for transfers between devices: 84.6 us -> 20.3 us
  starting transfers between devices: 0.21 us -> 30.7 us
  blocking collectives: 17.8 us -> 0 us
  between operations: 15.3 us -> 1.07 us
  matrix products: 11.4 us -> 3.02 us
  other arithmetic: 4.75 us -> 1.01 us
    psum x2 -> x0, waiting for transfers between devices: 53.9 us -> none  [shards(): norms = jnp.sqrt(lax.psum(merged * merged, 'cond'))]
    ppermute x0 -> x24, starting transfers between devices: none -> 30.7 us  [swap(): return lax.ppermute(value, axis, [(i, i ^ mask) for i in range(size)])]
    all_gather x3 -> x0, waiting for transfers between devices: 28.7 us -> none  [the longest x2 14.7 us: shards(): lax.all_gather(coef_copy, 'shard', axis=0, tiled=True)]
    ppermute x0 -> x24, waiting for transfers between devices: none -> 20.3 us  [swap(): return lax.ppermute(value, axis, [(i, i ^ mask) for i in range(size)])]
    all_gather x1 -> x0, blocking collectives: 17.8 us -> none  [shards(): piece_y = lax.all_gather(responses, 'shard', axis=0, tiled=True)]
    dot_general x4 -> x8, matrix products: 11.4 us -> 3.02 us  [the longest x2 1.66 us: shards(): lax.dot_general(own, residual, contract, preferred_element_type=f32)]
    mul x1 -> x0, other arithmetic: 2.52 us -> none  [shards(): norms = jnp.sqrt(lax.psum(merged * merged, 'cond'))]
    gather x1 -> x0, local copies, waits for them, and re-layouts: 2.34 us -> none  [shards(): jnp.diagonal(lax.dynamic_slice_in_dim(gram, row_start, my_rows, 1))]
  transfers between devices with their start and end apart: 5 -> 24, of which waited for: 4 -> 17; matrix products, arithmetic and copies ran while one was open for 8% -> 3% of each run, Pallas kernels for 0% -> 0%
where the time goes in v2:
time: 57.5 us; the launch traced here: 57.3 us
  starting transfers between devices  30.7 us (53%)
  waiting for transfers between devices  20.3 us (35%)
  matrix products  3.02 us (5%)
  local copies, waits for them, and re-layouts  1.21 us (2%)
  between operations  1.07 us (2%)
  other arithmetic  1.01 us (2%)
    ppermute x24, starting transfers between devices, swap(): return lax.ppermute(value, axis, [(i, i ^ mask) for i in range(size)])  30.7 us
    ppermute x24, waiting for transfers between devices, swap(): return lax.ppermute(value, axis, [(i, i ^ mask) for i in range(size)])  20.3 us
    dot_general x2, matrix products, shards(): lax.dot_general(own, residual, contract, preferred_element_type=f32)  1.66 us
  transfers between devices with their start and end apart: 24, of which 17 were waited for; matrix products, arithmetic and copies ran while one was open for 3% of the time, Pallas kernels for 0%

profile of v2, /device:TPU:0, one launch (start us, length us, event | category | flops | bytes accessed | tf_op | source)
XLA Modules:
  0.0 57.3 jit_solution(476292206375657932)
XLA Ops:
  0.7 1.0 %dynamic-slice_bitcast_fusion.1 = (bf16[1,64,256]{2,1,0:T(8,128)(2,1)S(1)}, bf16[1,64,256]{2,1,0:T(8,128)(2,1)S(1)}, bf16[1,64,256]{2,1,0:T(8,128)(2,1)S(1)}, bf...) fusion(bf16[64,2048]{1,0:T(8,128)(2,1)} %param.5, ...), kind=kLoop, calls=%fused_computation.56 | loop fusion | bytes 524320 | tf_op jit(solution)/shard_map/stack | solution.py:44
  1.7 3.1 %collective-permute-start = (bf16[2,64,256]{2,1,0:T(8,128)(2,1)S(1)}, bf16[2,64,256]{2,1,0:T(8,128)(2,1)S(1)}, u32[]{:S(2)}, u32[]{:S(2)}) collective-permute-start(bf16[2,64,256]{2,1,0:T(8,128)(2,1)S(1)} %pad_maximum_fusion.3), channel_id=1, source_target_pairs={{0,2},{1,3},{2,0},{3,1},{4,6},{5,7},{6,4},{7,5},{8,10},{9,11},{10,... | collective-permute-start | bytes 196616 | tf_op jit(solution)/shard_map/cells1/ppermute | solution.py:17
  4.8 2.6 %collective-permute-start.1 = (bf16[2,64,256]{2,1,0:T(8,128)(2,1)S(1)}, bf16[2,64,256]{2,1,0:T(8,128)(2,1)S(1)}, u32[]{:S(2)}, u32[]{:S(2)}) collective-permute-start(bf16[2,64,256]{2,1,0:T(8,128)(2,1)S(1)} %pad_maximum_fusion.4), channel_id=1, source_target_pairs={{0,4},{1,5},{2,6},{3,7},{4,0},{5,1},{6,2},{7,3},{8,12},{9,13},{10,... | collective-permute-start | bytes 196616 | tf_op jit(solution)/shard_map/cells2/ppermute | solution.py:17
  7.6 0.1 multiply_convert_fusion.1
  7.7 1.7 %collective-permute-start.4 = (bf16[256,512]{1,0:T(8,128)(2,1)S(1)}, bf16[256,512]{1,0:T(8,128)(2,1)S(1)}, u32[]{:S(2)}, u32[]{:S(2)}) collective-permute-start(bf16[256,512]{1,0:T(8,128)(2,1)S(1)} %get-tuple-element.55), channel_id=1, source_target_pairs={{0,8},{8,0},{16,24},{24,16},{1,9},{9,1},{17,25},{25,17},{2,10},{10... | collective-permute-start | bytes 786440 | tf_op jit(solution)/shard_map/squares0/ppermute | solution.py:17
  9.5 2.6 %collective-permute-done.1 = bf16[2,64,256]{2,1,0:T(8,128)(2,1)S(1)} collective-permute-done((bf16[2,64,256]{2,1,0:T(8,128)(2,1)S(1)}, bf16[2,64,256]{2,1,0:T(8,128)(2,1)S(1)}, u32[]{:S(2)}, u32[]{:S(2)}) %collective-permute-start.1) | collective-permute-done | bytes 65568 | tf_op jit(solution)/shard_map/cells2/ppermute | solution.py:17
  12.1 1.5 %collective-permute-done.2 = bf16[2,64,256]{2,1,0:T(8,128)(2,1)S(1)} collective-permute-done((bf16[2,64,256]{2,1,0:T(8,128)(2,1)S(1)}, bf16[2,64,256]{2,1,0:T(8,128)(2,1)S(1)}, u32[]{:S(2)}, u32[]{:S(2)}) %collective-permute-start.2) | collective-permute-done | bytes 65568 | tf_op jit(solution)/shard_map/cells3/ppermute | solution.py:17
  13.6 0.1 broadcast_in_dim.2
  13.8 0.2 fusion.18
  14.0 0.2 fusion.22
  14.3 1.0 %collective-permute-done.4 = bf16[256,512]{1,0:T(8,128)(2,1)S(1)} collective-permute-done((bf16[256,512]{1,0:T(8,128)(2,1)S(1)}, bf16[256,512]{1,0:T(8,128)(2,1)S(1)}, u32[]{:S(2)}, u32[]{:S(2)}) %collective-permute-start.4) | collective-permute-done | bytes 262176 | tf_op jit(solution)/shard_map/squares0/ppermute | solution.py:17
  15.4 3.6 %collective-permute-start.5 = (bf16[64,512]{1,0:T(8,128)(2,1)S(1)}, bf16[64,512]{1,0:T(8,128)(2,1)S(1)}, u32[]{:S(2)}, u32[]{:S(2)}) collective-permute-start(bf16[64,512]{1,0:T(8,128)(2,1)S(1)} %get-tuple-element.62), channel_id=1, source_target_pairs={{0,6},{1,7},{2,4},{3,5},{4,2},{5,3},{6,0},{7,1},{8,14},{9,15},{10,... | collective-permute-start | bytes 196616 | tf_op jit(solution)/shard_map/fit3/ppermute | solution.py:17
  18.9 0.9 %collective-permute-start.6 = (bf16[64,512]{1,0:T(8,128)(2,1)S(1)}, bf16[64,512]{1,0:T(8,128)(2,1)S(1)}, u32[]{:S(2)}, u32[]{:S(2)}) collective-permute-start(bf16[64,512]{1,0:T(8,128)(2,1)S(1)} %get-tuple-element.64), channel_id=1, source_target_pairs={{0,4},{1,5},{2,6},{3,7},{4,0},{5,1},{6,2},{7,3},{8,12},{9,13},{10,... | collective-permute-start | bytes 196616 | tf_op jit(solution)/shard_map/fit2/ppermute | solution.py:17
  20.0 1.6 %collective-permute-start.11 = (bf16[256,512]{1,0:T(8,128)(2,1)S(1)}, bf16[256,512]{1,0:T(8,128)(2,1)S(1)}, u32[]{:S(2)}, u32[]{:S(2)}) collective-permute-start(bf16[256,512]{1,0:T(8,128)(2,1)S(1)} %convert_element_type.85), channel_id=1, source_target_pairs={{0,16},{8,24},{16,0},{24,8},{1,17},{9,25},{17,1},{25,9},{2,18},{10... | collective-permute-start | bytes 786440 | tf_op jit(solution)/shard_map/squares1/ppermute | solution.py:17
  21.6 0.2 collective-permute-done.5
  21.7 1.5 %collective-permute-done.7 = bf16[64,512]{1,0:T(8,128)(2,1)S(1)} collective-permute-done((bf16[64,512]{1,0:T(8,128)(2,1)S(1)}, bf16[64,512]{1,0:T(8,128)(2,1)S(1)}, u32[]{:S(2)}, u32[]{:S(2)}) %collective-permute-start.7) | collective-permute-done | bytes 65568 | tf_op jit(solution)/shard_map/fit1/ppermute | solution.py:17
  23.2 0.9 %collective-permute-done.6 = bf16[64,512]{1,0:T(8,128)(2,1)S(1)} collective-permute-done((bf16[64,512]{1,0:T(8,128)(2,1)S(1)}, bf16[64,512]{1,0:T(8,128)(2,1)S(1)}, u32[]{:S(2)}, u32[]{:S(2)}) %collective-permute-start.6) | collective-permute-done | bytes 65568 | tf_op jit(solution)/shard_map/fit2/ppermute | solution.py:17
  24.2 1.7 %collective-permute-start.10 = (bf16[64,512]{1,0:T(8,128)(2,1)S(1)}, bf16[64,512]{1,0:T(8,128)(2,1)S(1)}, u32[]{:S(2)}, u32[]{:S(2)}) collective-permute-start(bf16[64,512]{1,0:T(8,128)(2,1)S(1)} %add_convert_fusion.1), channel_id=1, source_target_pairs={{0,6},{1,7},{2,4},{3,5},{4,2},{5,3},{6,0},{7,1},{8,14},{9,15},{10,... | collective-permute-start | bytes 196616 | tf_op jit(solution)/shard_map/residual3/ppermute | solution.py:17
  25.8 1.9 %collective-permute-start.9 = (bf16[64,512]{1,0:T(8,128)(2,1)S(1)}, bf16[64,512]{1,0:T(8,128)(2,1)S(1)}, u32[]{:S(2)}, u32[]{:S(2)}) collective-permute-start(bf16[64,512]{1,0:T(8,128)(2,1)S(1)} %add_convert_fusion.1), channel_id=1, source_target_pairs={{0,4},{1,5},{2,6},{3,7},{4,0},{5,1},{6,2},{7,3},{8,12},{9,13},{10,... | collective-permute-start | bytes 196616 | tf_op jit(solution)/shard_map/residual2/ppermute | solution.py:17
  27.7 0.9 %collective-permute-start.8 = (bf16[64,512]{1,0:T(8,128)(2,1)S(1)}, bf16[64,512]{1,0:T(8,128)(2,1)S(1)}, u32[]{:S(2)}, u32[]{:S(2)}) collective-permute-start(bf16[64,512]{1,0:T(8,128)(2,1)S(1)} %add_convert_fusion.1), channel_id=1, source_target_pairs={{0,2},{1,3},{2,0},{3,1},{4,6},{5,7},{6,4},{7,5},{8,10},{9,11},{10,... | collective-permute-start | bytes 196616 | tf_op jit(solution)/shard_map/residual1/ppermute | solution.py:17
  28.7 0.1 collective-permute-done.11
  28.8 1.9 %collective-permute-done.10 = bf16[64,512]{1,0:T(8,128)(2,1)S(1)} collective-permute-done((bf16[64,512]{1,0:T(8,128)(2,1)S(1)}, bf16[64,512]{1,0:T(8,128)(2,1)S(1)}, u32[]{:S(2)}, u32[]{:S(2)}) %collective-permute-start.10) | collective-permute-done | bytes 65568 | tf_op jit(solution)/shard_map/residual3/ppermute | solution.py:17
  30.7 1.5 %collective-permute-done.9 = bf16[64,512]{1,0:T(8,128)(2,1)S(1)} collective-permute-done((bf16[64,512]{1,0:T(8,128)(2,1)S(1)}, bf16[64,512]{1,0:T(8,128)(2,1)S(1)}, u32[]{:S(2)}, u32[]{:S(2)}) %collective-permute-start.9) | collective-permute-done | bytes 65568 | tf_op jit(solution)/shard_map/residual2/ppermute | solution.py:17
  32.3 0.2 collective-permute-done.8
  32.6 1.5 %collective-permute-done.13 = bf16[256,512]{1,0:T(8,128)(2,1)S(1)} collective-permute-done((bf16[256,512]{1,0:T(8,128)(2,1)S(1)}, bf16[256,512]{1,0:T(8,128)(2,1)S(1)}, u32[]{:S(2)}, u32[]{:S(2)}) %collective-permute-start.13) | collective-permute-done | bytes 262176 | tf_op jit(solution)/shard_map/residual_core/ppermute | solution.py:17
  34.1 0.2 fusion.24
  34.3 0.6 multiply_convert_fusion
  34.9 0.2 collective-permute-start.14
  35.1 1.5 %collective-permute-start.21 = (bf16[256,512]{1,0:T(8,128)(2,1)S(1)}, bf16[256,512]{1,0:T(8,128)(2,1)S(1)}, u32[]{:S(2)}, u32[]{:S(2)}) collective-permute-start(bf16[256,512]{1,0:T(8,128)(2,1)S(1)} %get-tuple-element.53), channel_id=1, source_target_pairs={{0,8},{8,0},{16,24},{24,16},{1,9},{9,1},{17,25},{25,17},{2,10},{10... | collective-permute-start | bytes 786440 | tf_op jit(solution)/shard_map/squares0/ppermute | solution.py:17
  36.6 0.2 fusion.17
  36.8 0.2 fusion.23
  37.1 1.7 %collective-permute-start.15 = (bf16[64,512]{1,0:T(8,128)(2,1)S(1)}, bf16[64,512]{1,0:T(8,128)(2,1)S(1)}, u32[]{:S(2)}, u32[]{:S(2)}) collective-permute-start(bf16[64,512]{1,0:T(8,128)(2,1)S(1)} %get-tuple-element.59), channel_id=1, source_target_pairs={{0,6},{1,7},{2,4},{3,5},{4,2},{5,3},{6,0},{7,1},{8,14},{9,15},{10,... | collective-permute-start | bytes 196616 | tf_op jit(solution)/shard_map/fit3/ppermute | solution.py:17
  38.8 2.8 %collective-permute-start.16 = (bf16[64,512]{1,0:T(8,128)(2,1)S(1)}, bf16[64,512]{1,0:T(8,128)(2,1)S(1)}, u32[]{:S(2)}, u32[]{:S(2)}) collective-permute-start(bf16[64,512]{1,0:T(8,128)(2,1)S(1)} %get-tuple-element.61), channel_id=1, source_target_pairs={{0,4},{1,5},{2,6},{3,7},{4,0},{5,1},{6,2},{7,3},{8,12},{9,13},{10,... | collective-permute-start | bytes 196616 | tf_op jit(solution)/shard_map/fit2/ppermute | solution.py:17
  41.6 2.1 %collective-permute-done.21 = bf16[256,512]{1,0:T(8,128)(2,1)S(1)} collective-permute-done((bf16[256,512]{1,0:T(8,128)(2,1)S(1)}, bf16[256,512]{1,0:T(8,128)(2,1)S(1)}, u32[]{:S(2)}, u32[]{:S(2)}) %collective-permute-start.21) | collective-permute-done | bytes 262176 | tf_op jit(solution)/shard_map/squares0/ppermute | solution.py:17
  43.7 0.1 fusion.14
  43.8 1.8 %collective-permute-start.22 = (bf16[256,512]{1,0:T(8,128)(2,1)S(1)}, bf16[256,512]{1,0:T(8,128)(2,1)S(1)}, u32[]{:S(2)}, u32[]{:S(2)}) collective-permute-start(bf16[256,512]{1,0:T(8,128)(2,1)S(1)} %fusion.14), channel_id=1, source_target_pairs={{0,16},{8,24},{16,0},{24,8},{1,17},{9,25},{17,1},{25,9},{2,18},{10... | collective-permute-start | bytes 786440 | tf_op jit(solution)/shard_map/squares1/ppermute | solution.py:17
  45.6 0.3 collective-permute-done.16
  46.0 1.9 %collective-permute-start.20 = (bf16[64,512]{1,0:T(8,128)(2,1)S(1)}, bf16[64,512]{1,0:T(8,128)(2,1)S(1)}, u32[]{:S(2)}, u32[]{:S(2)}) collective-permute-start(bf16[64,512]{1,0:T(8,128)(2,1)S(1)} %add_convert_fusion), channel_id=1, source_target_pairs={{0,6},{1,7},{2,4},{3,5},{4,2},{5,3},{6,0},{7,1},{8,14},{9,15},{10,... | collective-permute-start | bytes 196616 | tf_op jit(solution)/shard_map/residual3/ppermute | solution.py:17
  47.8 0.2 collective-permute-start.19
  48.0 2.4 %collective-permute-start.18 = (bf16[64,512]{1,0:T(8,128)(2,1)S(1)}, bf16[64,512]{1,0:T(8,128)(2,1)S(1)}, u32[]{:S(2)}, u32[]{:S(2)}) collective-permute-start(bf16[64,512]{1,0:T(8,128)(2,1)S(1)} %add_convert_fusion), channel_id=1, source_target_pairs={{0,2},{1,3},{2,0},{3,1},{4,6},{5,7},{6,4},{7,5},{8,10},{9,11},{10,... | collective-permute-start | bytes 196616 | tf_op jit(solution)/shard_map/residual1/ppermute | solution.py:17
  50.4 1.2 %collective-permute-done.22 = bf16[256,512]{1,0:T(8,128)(2,1)S(1)} collective-permute-done((bf16[256,512]{1,0:T(8,128)(2,1)S(1)}, bf16[256,512]{1,0:T(8,128)(2,1)S(1)}, u32[]{:S(2)}, u32[]{:S(2)}) %collective-permute-start.22) | collective-permute-done | bytes 262176 | tf_op jit(solution)/shard_map/squares1/ppermute | solution.py:17
  51.6 0.1 convert_add_fusion
  51.7 0.7 %collective-permute-done.20 = bf16[64,512]{1,0:T(8,128)(2,1)S(1)} collective-permute-done((bf16[64,512]{1,0:T(8,128)(2,1)S(1)}, bf16[64,512]{1,0:T(8,128)(2,1)S(1)}, u32[]{:S(2)}, u32[]{:S(2)}) %collective-permute-start.20) | collective-permute-done | bytes 65568 | tf_op jit(solution)/shard_map/residual3/ppermute | solution.py:17
  52.5 1.9 %collective-permute-done.19 = bf16[64,512]{1,0:T(8,128)(2,1)S(1)} collective-permute-done((bf16[64,512]{1,0:T(8,128)(2,1)S(1)}, bf16[64,512]{1,0:T(8,128)(2,1)S(1)}, u32[]{:S(2)}, u32[]{:S(2)}) %collective-permute-start.19) | collective-permute-done | bytes 65568 | tf_op jit(solution)/shard_map/residual2/ppermute | solution.py:17
  54.4 0.3 fusion.19
  54.7 1.2 %collective-permute-done.23 = bf16[256,512]{1,0:T(8,128)(2,1)S(1)} collective-permute-done((bf16[256,512]{1,0:T(8,128)(2,1)S(1)}, bf16[256,512]{1,0:T(8,128)(2,1)S(1)}, u32[]{:S(2)}, u32[]{:S(2)}) %collective-permute-start.23) | collective-permute-done | bytes 262176 | tf_op jit(solution)/shard_map/residual_core/ppermute | solution.py:17
  56.0 0.2 fusion.25
  56.2 1.1 %fusion.4 = f32[256,512]{1,0:T(8,128)} fusion(f32[256,512]{1,0:T(8,128)S(1)} %get-tuple-element.83, f32[256,512]{1,0:T(8,128)S(1)} %fusion.25, bf16[256,512]{1,0:T(8,128)(2,1)S(1)} %constant_dynamic-update-slice_fusion.4, f32[256,512]{1,0:T(8,128)S(1)} %get-tuple-element.52, f32[256,512]{1,0:T(8,128)S(1)} %get-tuple-element.51, f32[256]{0:T(256)S(1)} %add_divide_fusion, ...), kind=kOutput, calls=%fused_computation.5 | convolution fusion | flops 68812800 | bytes 3015680 | tf_op jit(solution)/shard_map/dot_general | solution.py:84
  (54 shorter events, 0.9 us)
Async XLA Ops:
  0.6 6.9 %copy-start.2 = (f32[256,512]{1,0:T(8,128)S(1)}, f32[256,512]{1,0:T(8,128)}, u32[]{:S(2)}) copy-start(f32[256,512]{1,0:T(8,128)} %param.8) | copy-start | bytes 1572868
  0.6 6.9 %copy-start.3 = (f32[256,512]{1,0:T(8,128)S(1)}, f32[256,512]{1,0:T(8,128)}, u32[]{:S(2)}) copy-start(f32[256,512]{1,0:T(8,128)} %param.7) | copy-start | bytes 1572868
  1.7 7.8 %collective-permute-start = (bf16[2,64,256]{2,1,0:T(8,128)(2,1)S(1)}, bf16[2,64,256]{2,1,0:T(8,128)(2,1)S(1)}, u32[]{:S(2)}, u32[]{:S(2)}) collective-permute-start(bf16[2,64,256]{2,1,0:T(8,128)(2,1)S(1)} %pad_maximum_fusion.3), channel_id=1, source_target_pairs={{0,2},{1,3},{2,0},{3,1},{4,6},{5,7},{6,4},{7,5},{8,10},{9,11},{10,... | collective-permute-start | bytes 196616 | tf_op jit(solution)/shard_map/cells1/ppermute | solution.py:17
  4.8 7.3 %collective-permute-start.1 = (bf16[2,64,256]{2,1,0:T(8,128)(2,1)S(1)}, bf16[2,64,256]{2,1,0:T(8,128)(2,1)S(1)}, u32[]{:S(2)}, u32[]{:S(2)}) collective-permute-start(bf16[2,64,256]{2,1,0:T(8,128)(2,1)S(1)} %pad_maximum_fusion.4), channel_id=1, source_target_pairs={{0,4},{1,5},{2,6},{3,7},{4,0},{5,1},{6,2},{7,3},{8,12},{9,13},{10,... | collective-permute-start | bytes 196616 | tf_op jit(solution)/shard_map/cells2/ppermute | solution.py:17
  7.5 2.0 %copy-start.4 = (bf16[64,512]{1,0:T(8,128)(2,1)S(1)}, bf16[64,512]{1,0:T(8,128)(2,1)}, u32[]{:S(2)}) copy-start(bf16[64,512]{1,0:T(8,128)(2,1)} %param.6) | copy-start | bytes 196612
  7.5 6.1 %collective-permute-start.2 = (bf16[2,64,256]{2,1,0:T(8,128)(2,1)S(1)}, bf16[2,64,256]{2,1,0:T(8,128)(2,1)S(1)}, u32[]{:S(2)}, u32[]{:S(2)}) collective-permute-start(bf16[2,64,256]{2,1,0:T(8,128)(2,1)S(1)} %pad_maximum_fusion.5), channel_id=1, source_target_pairs={{0,6},{1,7},{2,4},{3,5},{4,2},{5,3},{6,0},{7,1},{8,14},{9,15},{10,... | collective-permute-start | bytes 196616 | tf_op jit(solution)/shard_map/cells3/ppermute | solution.py:17
  7.7 7.6 %collective-permute-start.4 = (bf16[256,512]{1,0:T(8,128)(2,1)S(1)}, bf16[256,512]{1,0:T(8,128)(2,1)S(1)}, u32[]{:S(2)}, u32[]{:S(2)}) collective-permute-start(bf16[256,512]{1,0:T(8,128)(2,1)S(1)} %get-tuple-element.55), channel_id=1, source_target_pairs={{0,8},{8,0},{16,24},{24,16},{1,9},{9,1},{17,25},{25,17},{2,10},{10... | collective-permute-start | bytes 786440 | tf_op jit(solution)/shard_map/squares0/ppermute | solution.py:17
  9.5 4.5 %collective-permute-start.3 = (bf16[256,512]{1,0:T(8,128)(2,1)S(1)}, bf16[256,512]{1,0:T(8,128)(2,1)S(1)}, u32[]{:S(2)}, u32[]{:S(2)}) collective-permute-start(bf16[256,512]{1,0:T(8,128)(2,1)S(1)} %get-tuple-element.58), channel_id=1, source_target_pairs={{0,1},{1,0},{2,3},{3,2},{4,5},{5,4},{6,7},{7,6},{8,9},{9,8},{10,11... | collective-permute-start | bytes 786440 | tf_op jit(solution)/shard_map/coef_core/ppermute | solution.py:17
  9.5 4.1 %copy-start.5 = (f32[256]{0:T(256)S(1)}, f32[256]{0:T(256)}, u32[]{:S(2)}) copy-start(f32[256]{0:T(256)} %param.9) | copy-start | bytes 3076
  15.4 6.4 %collective-permute-start.5 = (bf16[64,512]{1,0:T(8,128)(2,1)S(1)}, bf16[64,512]{1,0:T(8,128)(2,1)S(1)}, u32[]{:S(2)}, u32[]{:S(2)}) collective-permute-start(bf16[64,512]{1,0:T(8,128)(2,1)S(1)} %get-tuple-element.62), channel_id=1, source_target_pairs={{0,6},{1,7},{2,4},{3,5},{4,2},{5,3},{6,0},{7,1},{8,14},{9,15},{10,... | collective-permute-start | bytes 196616 | tf_op jit(solution)/shard_map/fit3/ppermute | solution.py:17
  18.9 4.3 %collective-permute-start.7 = (bf16[64,512]{1,0:T(8,128)(2,1)S(1)}, bf16[64,512]{1,0:T(8,128)(2,1)S(1)}, u32[]{:S(2)}, u32[]{:S(2)}) collective-permute-start(bf16[64,512]{1,0:T(8,128)(2,1)S(1)} %get-tuple-element.63), channel_id=1, source_target_pairs={{0,2},{1,3},{2,0},{3,1},{4,6},{5,7},{6,4},{7,5},{8,10},{9,11},{10,... | collective-permute-start | bytes 196616 | tf_op jit(solution)/shard_map/fit1/ppermute | solution.py:17
  18.9 5.2 %collective-permute-start.6 = (bf16[64,512]{1,0:T(8,128)(2,1)S(1)}, bf16[64,512]{1,0:T(8,128)(2,1)S(1)}, u32[]{:S(2)}, u32[]{:S(2)}) collective-permute-start(bf16[64,512]{1,0:T(8,128)(2,1)S(1)} %get-tuple-element.64), channel_id=1, source_target_pairs={{0,4},{1,5},{2,6},{3,7},{4,0},{5,1},{6,2},{7,3},{8,12},{9,13},{10,... | collective-permute-start | bytes 196616 | tf_op jit(solution)/shard_map/fit2/ppermute | solution.py:17
  19.9 8.7 %collective-permute-start.12 = (bf16[256,256]{1,0:T(8,128)(2,1)S(1)}, bf16[256,256]{1,0:T(8,128)(2,1)S(1)}, u32[]{:S(2)}, u32[]{:S(2)}) collective-permute-start(bf16[256,256]{1,0:T(8,128)(2,1)S(1)} %pad_maximum_fusion.1), channel_id=1, source_target_pairs={{0,1},{1,0},{2,3},{3,2},{4,5},{5,4},{6,7},{7,6},{8,9},{9,8},{10,11... | collective-permute-start | bytes 393224 | tf_op jit(solution)/shard_map/cells_core/ppermute | solution.py:17
  20.0 8.8 %collective-permute-start.11 = (bf16[256,512]{1,0:T(8,128)(2,1)S(1)}, bf16[256,512]{1,0:T(8,128)(2,1)S(1)}, u32[]{:S(2)}, u32[]{:S(2)}) collective-permute-start(bf16[256,512]{1,0:T(8,128)(2,1)S(1)} %convert_element_type.85), channel_id=1, source_target_pairs={{0,16},{8,24},{16,0},{24,8},{1,17},{9,25},{17,1},{25,9},{2,18},{10... | collective-permute-start | bytes 786440 | tf_op jit(solution)/shard_map/squares1/ppermute | solution.py:17
  24.2 6.6 %collective-permute-start.10 = (bf16[64,512]{1,0:T(8,128)(2,1)S(1)}, bf16[64,512]{1,0:T(8,128)(2,1)S(1)}, u32[]{:S(2)}, u32[]{:S(2)}) collective-permute-start(bf16[64,512]{1,0:T(8,128)(2,1)S(1)} %add_convert_fusion.1), channel_id=1, source_target_pairs={{0,6},{1,7},{2,4},{3,5},{4,2},{5,3},{6,0},{7,1},{8,14},{9,15},{10,... | collective-permute-start | bytes 196616 | tf_op jit(solution)/shard_map/residual3/ppermute | solution.py:17
  25.8 6.4 %collective-permute-start.9 = (bf16[64,512]{1,0:T(8,128)(2,1)S(1)}, bf16[64,512]{1,0:T(8,128)(2,1)S(1)}, u32[]{:S(2)}, u32[]{:S(2)}) collective-permute-start(bf16[64,512]{1,0:T(8,128)(2,1)S(1)} %add_convert_fusion.1), channel_id=1, source_target_pairs={{0,4},{1,5},{2,6},{3,7},{4,0},{5,1},{6,2},{7,3},{8,12},{9,13},{10,... | collective-permute-start | bytes 196616 | tf_op jit(solution)/shard_map/residual2/ppermute | solution.py:17
  27.7 4.7 %collective-permute-start.8 = (bf16[64,512]{1,0:T(8,128)(2,1)S(1)}, bf16[64,512]{1,0:T(8,128)(2,1)S(1)}, u32[]{:S(2)}, u32[]{:S(2)}) collective-permute-start(bf16[64,512]{1,0:T(8,128)(2,1)S(1)} %add_convert_fusion.1), channel_id=1, source_target_pairs={{0,2},{1,3},{2,0},{3,1},{4,6},{5,7},{6,4},{7,5},{8,10},{9,11},{10,... | collective-permute-start | bytes 196616 | tf_op jit(solution)/shard_map/residual1/ppermute | solution.py:17
  32.5 1.6 %collective-permute-start.13 = (bf16[256,512]{1,0:T(8,128)(2,1)S(1)}, bf16[256,512]{1,0:T(8,128)(2,1)S(1)}, u32[]{:S(2)}, u32[]{:S(2)}) collective-permute-start(bf16[256,512]{1,0:T(8,128)(2,1)S(1)} %constant_dynamic-update-slice_fusion), channel_id=1, source_target_pairs={{0,1},{1,0},{2,3},{3,2},{4,5},{5,4},{6,7},{7,6},{8,9},{9,8},{10,11... | collective-permute-start | bytes 786440 | tf_op jit(solution)/shard_map/residual_core/ppermute | solution.py:17
  34.9 1.9 %collective-permute-start.14 = (bf16[256,512]{1,0:T(8,128)(2,1)S(1)}, bf16[256,512]{1,0:T(8,128)(2,1)S(1)}, u32[]{:S(2)}, u32[]{:S(2)}) collective-permute-start(bf16[256,512]{1,0:T(8,128)(2,1)S(1)} %get-tuple-element.57), channel_id=1, source_target_pairs={{0,1},{1,0},{2,3},{3,2},{4,5},{5,4},{6,7},{7,6},{8,9},{9,8},{10,11... | collective-permute-start | bytes 786440 | tf_op jit(solution)/shard_map/coef_core/ppermute | solution.py:17
  35.1 8.6 %collective-permute-start.21 = (bf16[256,512]{1,0:T(8,128)(2,1)S(1)}, bf16[256,512]{1,0:T(8,128)(2,1)S(1)}, u32[]{:S(2)}, u32[]{:S(2)}) collective-permute-start(bf16[256,512]{1,0:T(8,128)(2,1)S(1)} %get-tuple-element.53), channel_id=1, source_target_pairs={{0,8},{8,0},{16,24},{24,16},{1,9},{9,1},{17,25},{25,17},{2,10},{10... | collective-permute-start | bytes 786440 | tf_op jit(solution)/shard_map/squares0/ppermute | solution.py:17
  37.1 8.5 %collective-permute-start.15 = (bf16[64,512]{1,0:T(8,128)(2,1)S(1)}, bf16[64,512]{1,0:T(8,128)(2,1)S(1)}, u32[]{:S(2)}, u32[]{:S(2)}) collective-permute-start(bf16[64,512]{1,0:T(8,128)(2,1)S(1)} %get-tuple-element.59), channel_id=1, source_target_pairs={{0,6},{1,7},{2,4},{3,5},{4,2},{5,3},{6,0},{7,1},{8,14},{9,15},{10,... | collective-permute-start | bytes 196616 | tf_op jit(solution)/shard_map/fit3/ppermute | solution.py:17
  38.8 6.8 %collective-permute-start.17 = (bf16[64,512]{1,0:T(8,128)(2,1)S(1)}, bf16[64,512]{1,0:T(8,128)(2,1)S(1)}, u32[]{:S(2)}, u32[]{:S(2)}) collective-permute-start(bf16[64,512]{1,0:T(8,128)(2,1)S(1)} %get-tuple-element.60), channel_id=1, source_target_pairs={{0,2},{1,3},{2,0},{3,1},{4,6},{5,7},{6,4},{7,5},{8,10},{9,11},{10,... | collective-permute-start | bytes 196616 | tf_op jit(solution)/shard_map/fit1/ppermute | solution.py:17
  38.8 7.1 %collective-permute-start.16 = (bf16[64,512]{1,0:T(8,128)(2,1)S(1)}, bf16[64,512]{1,0:T(8,128)(2,1)S(1)}, u32[]{:S(2)}, u32[]{:S(2)}) collective-permute-start(bf16[64,512]{1,0:T(8,128)(2,1)S(1)} %get-tuple-element.61), channel_id=1, source_target_pairs={{0,4},{1,5},{2,6},{3,7},{4,0},{5,1},{6,2},{7,3},{8,12},{9,13},{10,... | collective-permute-start | bytes 196616 | tf_op jit(solution)/shard_map/fit2/ppermute | solution.py:17
  43.8 7.9 %collective-permute-start.22 = (bf16[256,512]{1,0:T(8,128)(2,1)S(1)}, bf16[256,512]{1,0:T(8,128)(2,1)S(1)}, u32[]{:S(2)}, u32[]{:S(2)}) collective-permute-start(bf16[256,512]{1,0:T(8,128)(2,1)S(1)} %fusion.14), channel_id=1, source_target_pairs={{0,16},{8,24},{16,0},{24,8},{1,17},{9,25},{17,1},{25,9},{2,18},{10... | collective-permute-start | bytes 786440 | tf_op jit(solution)/shard_map/squares1/ppermute | solution.py:17
  46.0 6.5 %collective-permute-start.20 = (bf16[64,512]{1,0:T(8,128)(2,1)S(1)}, bf16[64,512]{1,0:T(8,128)(2,1)S(1)}, u32[]{:S(2)}, u32[]{:S(2)}) collective-permute-start(bf16[64,512]{1,0:T(8,128)(2,1)S(1)} %add_convert_fusion), channel_id=1, source_target_pairs={{0,6},{1,7},{2,4},{3,5},{4,2},{5,3},{6,0},{7,1},{8,14},{9,15},{10,... | collective-permute-start | bytes 196616 | tf_op jit(solution)/shard_map/residual3/ppermute | solution.py:17
  47.8 6.5 %collective-permute-start.19 = (bf16[64,512]{1,0:T(8,128)(2,1)S(1)}, bf16[64,512]{1,0:T(8,128)(2,1)S(1)}, u32[]{:S(2)}, u32[]{:S(2)}) collective-permute-start(bf16[64,512]{1,0:T(8,128)(2,1)S(1)} %add_convert_fusion), channel_id=1, source_target_pairs={{0,4},{1,5},{2,6},{3,7},{4,0},{5,1},{6,2},{7,3},{8,12},{9,13},{10,... | collective-permute-start | bytes 196616 | tf_op jit(solution)/shard_map/residual2/ppermute | solution.py:17
  48.0 6.3 %collective-permute-start.18 = (bf16[64,512]{1,0:T(8,128)(2,1)S(1)}, bf16[64,512]{1,0:T(8,128)(2,1)S(1)}, u32[]{:S(2)}, u32[]{:S(2)}) collective-permute-start(bf16[64,512]{1,0:T(8,128)(2,1)S(1)} %add_convert_fusion), channel_id=1, source_target_pairs={{0,2},{1,3},{2,0},{3,1},{4,6},{5,7},{6,4},{7,5},{8,10},{9,11},{10,... | collective-permute-start | bytes 196616 | tf_op jit(solution)/shard_map/residual1/ppermute | solution.py:17
  54.4 1.6 %collective-permute-start.23 = (bf16[256,512]{1,0:T(8,128)(2,1)S(1)}, bf16[256,512]{1,0:T(8,128)(2,1)S(1)}, u32[]{:S(2)}, u32[]{:S(2)}) collective-permute-start(bf16[256,512]{1,0:T(8,128)(2,1)S(1)} %constant_dynamic-update-slice_fusion.4), channel_id=1, source_target_pairs={{0,1},{1,0},{2,3},{3,2},{4,5},{5,4},{6,7},{7,6},{8,9},{9,8},{10,11... | collective-permute-start | bytes 786440 | tf_op jit(solution)/shard_map/residual_core/ppermute | solution.py:17
  54.7 2.6 %copy-start = (f32[256,512]{1,0:T(8,128)}, f32[256,512]{1,0:T(8,128)S(1)}, u32[]{:S(2)}) copy-start(f32[256,512]{1,0:T(8,128)S(1)} %get-tuple-element.51) | copy-start | bytes 1572868
  54.7 2.6 %copy-start.1 = (f32[256,512]{1,0:T(8,128)}, f32[256,512]{1,0:T(8,128)S(1)}, u32[]{:S(2)}) copy-start(f32[256,512]{1,0:T(8,128)S(1)} %get-tuple-element.52) | copy-start | bytes 1572868

commit v3 on v2

v3 whole, which is shorter than its diff:
```python
import jax
import jax.numpy as jnp
from jax import lax
from jax.sharding import PartitionSpec as P

ITERS = 2


rho_weight = 2.0
bf16 = jnp.bfloat16
f32 = jnp.float32


def bits_of(size):
    return size.bit_length() - 1


def mirrored(mask, bits):
    return sum(((mask >> b) & 1) << (bits - 1 - b) for b in range(bits))


def core_swap(value, what):
    with jax.named_scope(what):
        return lax.ppermute(value, "shard", [(i, i ^ 1) for i in range(lax.axis_size("shard"))])


def chip_swap(value, mask, what):
    with jax.named_scope(what):
        return lax.ppermute(value, "shard", [(i, i ^ (2 * mask)) for i in range(lax.axis_size("shard"))])


def cond_swap(value, mask, what):
    conds, size = lax.axis_size("cond"), lax.axis_size("shard")
    masks = (mask, mirrored(mask, bits_of(conds)))
    pairs = [(c * size + i, (c ^ masks[i % 2]) * size + i) for c in range(conds) for i in range(size)]
    with jax.named_scope(what):
        return lax.ppermute(value, ("cond", "shard"), pairs)


def together(*values):
    return lax.optimization_barrier(values)


def shards(expression, responses, coef_init, dual_init, penalty):
    cells, targets = responses.shape
    mine = coef_init.shape[0]
    chips = lax.axis_size("shard") // 2
    cond_bits = bits_of(lax.axis_size("cond"))
    n_cells = cells * lax.axis_size("shard")
    me = lax.axis_index("shard")
    chip, core = me // 2, me % 2
    far_first = list(reversed(range(1, chips)))
    contract = (((0,), (0,)), ((), ()))

    def dot(x, c):
        return jnp.dot(x, c, preferred_element_type=f32)

    def columns(k, side):
        start = ((chip ^ k) * 2 + (core ^ side)) * mine
        return lax.dynamic_slice_in_dim(expression, start, mine, 1)

    coef_copy = coef_init.astype(bf16)
    coef_other = core_swap(coef_copy, "coef_core")
    pairs = [jnp.stack([columns(k, 0), columns(k, 1)]) for k in range(chips)]
    for k in far_first:
        pairs[k] = chip_swap(pairs[k], k, f"cells{k}")
    weights = jnp.broadcast_to(penalty[:, None], coef_init.shape)
    response_rows = responses.astype(f32)
    order = [0] + far_first
    *ordered, weights, response_rows = together(*[pairs[k] for k in order], weights, response_rows)
    for k, pair in zip(order, ordered):
        pairs[k] = pair
    own = jnp.concatenate([pairs[k][0] for k in order])
    other = jnp.concatenate([pairs[k][1] for k in order])

    coef = coef_init
    dual = dual_init
    for step in range(ITERS):
        merged = coef + dual
        squares = merged * merged
        if cond_bits > 0:
            squares = squares + cond_swap(squares.astype(bf16), 1, "squares0").astype(f32)
        if step > 0:
            coef_copy = coef.astype(bf16)
            coef_other = core_swap(coef_copy, "coef_core")
        fitted = (dot(own, coef_copy) + dot(other, coef_other)).reshape(chips, cells, targets)
        total = fitted[0] - response_rows
        leaving = fitted.astype(bf16)
        held = other
        if step == 0:
            leaving, total, held, squares = together(leaving, total, held, squares)
        arrived = [chip_swap(leaving[order.index(k)], k, f"fit{k}") for k in far_first]
        for bit in range(1, cond_bits):
            squares = squares + cond_swap(squares.astype(bf16), 1 << bit, f"squares{bit}").astype(f32)
        for part in arrived:
            total = total + part.astype(f32)
        residual = [total.astype(bf16)] * chips
        for k in far_first:
            residual[k] = chip_swap(residual[0], k, f"residual{k}")
        if step == 0:
            across = core_swap(held, "cells_core")
            diagonal = jnp.sum(jnp.square(own.astype(f32)), 0) + jnp.sum(jnp.square(across.astype(f32)), 0)
            step_size = 1.0 / (diagonal / n_cells + rho_weight)[:, None]
            residual, squares, step_size, across = together(residual, squares, step_size, across)
        else:
            residual, squares = together(residual, squares)
        residual = jnp.concatenate([residual[k] for k in order])
        residual_other = core_swap(residual, "residual_core")
        product = lax.dot_general(own, residual, contract, preferred_element_type=f32) + lax.dot_general(
            across, residual_other, contract, preferred_element_type=f32
        )

        norms = jnp.sqrt(squares)
        consensus = merged * (1.0 - weights / jnp.maximum(norms, weights))
        dual = merged - consensus
        coef = coef + (rho_weight * (consensus - dual) - product / n_cells - rho_weight * coef) * step_size
    return (coef, consensus, dual)


def solution(mesh):
    in_specs = (
        P(("cond", "shard"), None),
        P(("cond", "shard"), None),
        P(("cond", "shard"), None),
        P(("cond", "shard"), None),
        P("shard"),
    )
    out_specs = (P(("cond", "shard"), None), P(("cond", "shard"), None), P(("cond", "shard"), None))
    return jax.shard_map(shards, mesh=mesh, in_specs=in_specs, out_specs=out_specs, check_vma=False)
```

time: 57.5 us -> 56.1 us (0.976)
  waiting for transfers between devices: 20.3 us -> 18.8 us
    ppermute x24, waiting for transfers between devices: 20.3 us -> 18.8 us  [the longest x15 15 us: chip_swap(): lax.ppermute(value, 'shard', [(i, i ^ 2 * mask) for i in range(lax.axis_s...]
  transfers between devices with their start and end apart: 24 -> 24, of which waited for: 17 -> 14; matrix products, arithmetic and copies ran while one was open for 3% -> 3% of each run, Pallas kernels for 0% -> 0%
where the time goes in v3:
time: 56.1 us; the launch traced here: 56 us
  starting transfers between devices  30.9 us (55%)
  waiting for transfers between devices  18.8 us (34%)
  matrix products  3.04 us (5%)
  local copies, waits for them, and re-layouts  1.22 us (2%)
  between operations  1.07 us (2%)
  other arithmetic  1 us (2%)
    ppermute x15, starting transfers between devices, chip_swap(): lax.ppermute(value, 'shard', [(i, i ^ 2 * mask) for i in range(lax.axis_s...  23.7 us
    ppermute x15, waiting for transfers between devices, chip_swap(): lax.ppermute(value, 'shard', [(i, i ^ 2 * mask) for i in range(lax.axis_s...  15 us
    ppermute x4, starting transfers between devices, cond_swap(): return lax.ppermute(value, ('cond', 'shard'), pairs)  6.81 us
    ppermute x5, waiting for transfers between devices, core_swap(): lax.ppermute(value, 'shard', [(i, i ^ 1) for i in range(lax.axis_size('sh...  2.77 us
    dot_general x2, matrix products, shards(): lax.dot_general(own, residual, contract, preferred_element_type=f32)  1.66 us
  transfers between devices with their start and end apart: 24, of which 14 were waited for; matrix products, arithmetic and copies ran while one was open for 3% of the time, Pallas kernels for 0%

profile of v3, /device:TPU:0, one launch (start us, length us, event | category | flops | bytes accessed | tf_op | source)
XLA Modules:
  0.0 56.0 jit_solution(11692508939588179025)
XLA Ops:
  0.7 1.0 %dynamic-slice_bitcast_fusion.1 = (bf16[1,64,256]{2,1,0:T(8,128)(2,1)S(1)}, bf16[1,64,256]{2,1,0:T(8,128)(2,1)S(1)}, bf16[1,64,256]{2,1,0:T(8,128)(2,1)S(1)}, bf...) fusion(bf16[64,2048]{1,0:T(8,128)(2,1)} %param.5, ...), kind=kLoop, calls=%fused_computation.56 | loop fusion | bytes 524320 | tf_op jit(solution)/shard_map/stack | solution.py:64
  1.7 5.1 %collective-permute-start = (bf16[2,64,256]{2,1,0:T(8,128)(2,1)S(1)}, bf16[2,64,256]{2,1,0:T(8,128)(2,1)S(1)}, u32[]{:S(2)}, u32[]{:S(2)}) collective-permute-start(bf16[2,64,256]{2,1,0:T(8,128)(2,1)S(1)} %pad_maximum_fusion.3), channel_id=1, source_target_pairs={{0,6},{1,7},{2,4},{3,5},{4,2},{5,3},{6,0},{7,1},{8,14},{9,15},{10,... | collective-permute-start | bytes 196616 | tf_op jit(solution)/shard_map/cells3/ppermute | solution.py:29
  6.9 0.6 %collective-permute-start.2 = (bf16[2,64,256]{2,1,0:T(8,128)(2,1)S(1)}, bf16[2,64,256]{2,1,0:T(8,128)(2,1)S(1)}, u32[]{:S(2)}, u32[]{:S(2)}) collective-permute-start(bf16[2,64,256]{2,1,0:T(8,128)(2,1)S(1)} %pad_maximum_fusion.5), channel_id=1, source_target_pairs={{0,2},{1,3},{2,0},{3,1},{4,6},{5,7},{6,4},{7,5},{8,10},{9,11},{10,... | collective-permute-start | bytes 196616 | tf_op jit(solution)/shard_map/cells1/ppermute | solution.py:29
  7.6 0.1 multiply_convert_fusion.1
  7.7 1.8 %collective-permute-start.4 = (bf16[256,512]{1,0:T(8,128)(2,1)S(1)}, bf16[256,512]{1,0:T(8,128)(2,1)S(1)}, u32[]{:S(2)}, u32[]{:S(2)}) collective-permute-start(bf16[256,512]{1,0:T(8,128)(2,1)S(1)} %get-tuple-element.51), channel_id=1, source_target_pairs={{0,8},{1,17},{2,10},{3,19},{4,12},{5,21},{6,14},{7,23},{8,0},{9,25... | collective-permute-start | bytes 786440 | tf_op jit(solution)/shard_map/squares0/ppermute | solution.py:37
  9.5 2.9 %collective-permute-done.1 = bf16[2,64,256]{2,1,0:T(8,128)(2,1)S(1)} collective-permute-done((bf16[2,64,256]{2,1,0:T(8,128)(2,1)S(1)}, bf16[2,64,256]{2,1,0:T(8,128)(2,1)S(1)}, u32[]{:S(2)}, u32[]{:S(2)}) %collective-permute-start.1) | collective-permute-done | bytes 65568 | tf_op jit(solution)/shard_map/cells2/ppermute | solution.py:29
  12.4 0.1 broadcast_in_dim.2
  12.6 0.2 fusion.22
  12.8 0.2 fusion.27
  13.1 1.0 %collective-permute-done.4 = bf16[256,512]{1,0:T(8,128)(2,1)S(1)} collective-permute-done((bf16[256,512]{1,0:T(8,128)(2,1)S(1)}, bf16[256,512]{1,0:T(8,128)(2,1)S(1)}, u32[]{:S(2)}, u32[]{:S(2)}) %collective-permute-start.4) | collective-permute-done | bytes 262176 | tf_op jit(solution)/shard_map/squares0/ppermute | solution.py:37
  14.2 3.9 %collective-permute-start.5 = (bf16[64,512]{1,0:T(8,128)(2,1)S(1)}, bf16[64,512]{1,0:T(8,128)(2,1)S(1)}, u32[]{:S(2)}, u32[]{:S(2)}) collective-permute-start(bf16[64,512]{1,0:T(8,128)(2,1)S(1)} %get-tuple-element.58), channel_id=1, source_target_pairs={{0,6},{1,7},{2,4},{3,5},{4,2},{5,3},{6,0},{7,1},{8,14},{9,15},{10,... | collective-permute-start | bytes 196616 | tf_op jit(solution)/shard_map/fit3/ppermute | solution.py:29
  18.1 0.6 %collective-permute-start.6 = (bf16[64,512]{1,0:T(8,128)(2,1)S(1)}, bf16[64,512]{1,0:T(8,128)(2,1)S(1)}, u32[]{:S(2)}, u32[]{:S(2)}) collective-permute-start(bf16[64,512]{1,0:T(8,128)(2,1)S(1)} %get-tuple-element.60), channel_id=1, source_target_pairs={{0,4},{1,5},{2,6},{3,7},{4,0},{5,1},{6,2},{7,3},{8,12},{9,13},{10,... | collective-permute-start | bytes 196616 | tf_op jit(solution)/shard_map/fit2/ppermute | solution.py:29
  18.9 1.7 %collective-permute-start.11 = (bf16[256,512]{1,0:T(8,128)(2,1)S(1)}, bf16[256,512]{1,0:T(8,128)(2,1)S(1)}, u32[]{:S(2)}, u32[]{:S(2)}) collective-permute-start(bf16[256,512]{1,0:T(8,128)(2,1)S(1)} %convert_element_type.83), channel_id=1, source_target_pairs={{0,16},{1,9},{2,18},{3,11},{4,20},{5,13},{6,22},{7,15},{8,24},{9,1... | collective-permute-start | bytes 786440 | tf_op jit(solution)/shard_map/squares1/ppermute | solution.py:37
  20.7 1.7 %collective-permute-done.7 = bf16[64,512]{1,0:T(8,128)(2,1)S(1)} collective-permute-done((bf16[64,512]{1,0:T(8,128)(2,1)S(1)}, bf16[64,512]{1,0:T(8,128)(2,1)S(1)}, u32[]{:S(2)}, u32[]{:S(2)}) %collective-permute-start.7) | collective-permute-done | bytes 65568 | tf_op jit(solution)/shard_map/fit1/ppermute | solution.py:29
  22.4 0.9 %collective-permute-done.6 = bf16[64,512]{1,0:T(8,128)(2,1)S(1)} collective-permute-done((bf16[64,512]{1,0:T(8,128)(2,1)S(1)}, bf16[64,512]{1,0:T(8,128)(2,1)S(1)}, u32[]{:S(2)}, u32[]{:S(2)}) %collective-permute-start.6) | collective-permute-done | bytes 65568 | tf_op jit(solution)/shard_map/fit2/ppermute | solution.py:29
  23.3 1.7 %collective-permute-start.10 = (bf16[64,512]{1,0:T(8,128)(2,1)S(1)}, bf16[64,512]{1,0:T(8,128)(2,1)S(1)}, u32[]{:S(2)}, u32[]{:S(2)}) collective-permute-start(bf16[64,512]{1,0:T(8,128)(2,1)S(1)} %add_convert_fusion), channel_id=1, source_target_pairs={{0,6},{1,7},{2,4},{3,5},{4,2},{5,3},{6,0},{7,1},{8,14},{9,15},{10,... | collective-permute-start | bytes 196616 | tf_op jit(solution)/shard_map/residual3/ppermute | solution.py:29
  25.0 1.9 %collective-permute-start.9 = (bf16[64,512]{1,0:T(8,128)(2,1)S(1)}, bf16[64,512]{1,0:T(8,128)(2,1)S(1)}, u32[]{:S(2)}, u32[]{:S(2)}) collective-permute-start(bf16[64,512]{1,0:T(8,128)(2,1)S(1)} %add_convert_fusion), channel_id=1, source_target_pairs={{0,4},{1,5},{2,6},{3,7},{4,0},{5,1},{6,2},{7,3},{8,12},{9,13},{10,... | collective-permute-start | bytes 196616 | tf_op jit(solution)/shard_map/residual2/ppermute | solution.py:29
  26.9 0.9 %collective-permute-start.8 = (bf16[64,512]{1,0:T(8,128)(2,1)S(1)}, bf16[64,512]{1,0:T(8,128)(2,1)S(1)}, u32[]{:S(2)}, u32[]{:S(2)}) collective-permute-start(bf16[64,512]{1,0:T(8,128)(2,1)S(1)} %add_convert_fusion), channel_id=1, source_target_pairs={{0,2},{1,3},{2,0},{3,1},{4,6},{5,7},{6,4},{7,5},{8,10},{9,11},{10,... | collective-permute-start | bytes 196616 | tf_op jit(solution)/shard_map/residual1/ppermute | solution.py:29
  27.8 0.1 convert_add_fusion.2
  27.9 2.0 %collective-permute-done.10 = bf16[64,512]{1,0:T(8,128)(2,1)S(1)} collective-permute-done((bf16[64,512]{1,0:T(8,128)(2,1)S(1)}, bf16[64,512]{1,0:T(8,128)(2,1)S(1)}, u32[]{:S(2)}, u32[]{:S(2)}) %collective-permute-start.10) | collective-permute-done | bytes 65568 | tf_op jit(solution)/shard_map/residual3/ppermute | solution.py:29
  29.9 1.5 %collective-permute-done.9 = bf16[64,512]{1,0:T(8,128)(2,1)S(1)} collective-permute-done((bf16[64,512]{1,0:T(8,128)(2,1)S(1)}, bf16[64,512]{1,0:T(8,128)(2,1)S(1)}, u32[]{:S(2)}, u32[]{:S(2)}) %collective-permute-start.9) | collective-permute-done | bytes 65568 | tf_op jit(solution)/shard_map/residual2/ppermute | solution.py:29
  31.4 0.2 collective-permute-done.8
  31.6 0.1 collective-permute-start.13
  31.7 1.5 %collective-permute-done.13 = bf16[256,512]{1,0:T(8,128)(2,1)S(1)} collective-permute-done((bf16[256,512]{1,0:T(8,128)(2,1)S(1)}, bf16[256,512]{1,0:T(8,128)(2,1)S(1)}, u32[]{:S(2)}, u32[]{:S(2)}) %collective-permute-start.13) | collective-permute-done | bytes 262176 | tf_op jit(solution)/shard_map/residual_core/ppermute | solution.py:24
  33.3 0.2 fusion.29
  33.5 0.6 multiply_convert_fusion
  34.1 0.2 collective-permute-start.14
  34.3 1.7 %collective-permute-start.21 = (bf16[256,512]{1,0:T(8,128)(2,1)S(1)}, bf16[256,512]{1,0:T(8,128)(2,1)S(1)}, u32[]{:S(2)}, u32[]{:S(2)}) collective-permute-start(bf16[256,512]{1,0:T(8,128)(2,1)S(1)} %get-tuple-element.49), channel_id=1, source_target_pairs={{0,8},{1,17},{2,10},{3,19},{4,12},{5,21},{6,14},{7,23},{8,0},{9,25... | collective-permute-start | bytes 786440 | tf_op jit(solution)/shard_map/squares0/ppermute | solution.py:37
  36.0 0.2 fusion.21
  36.2 0.2 fusion.28
  36.5 1.3 %collective-permute-start.15 = (bf16[64,512]{1,0:T(8,128)(2,1)S(1)}, bf16[64,512]{1,0:T(8,128)(2,1)S(1)}, u32[]{:S(2)}, u32[]{:S(2)}) collective-permute-start(bf16[64,512]{1,0:T(8,128)(2,1)S(1)} %get-tuple-element.55), channel_id=1, source_target_pairs={{0,6},{1,7},{2,4},{3,5},{4,2},{5,3},{6,0},{7,1},{8,14},{9,15},{10,... | collective-permute-start | bytes 196616 | tf_op jit(solution)/shard_map/fit3/ppermute | solution.py:29
  37.8 3.2 %collective-permute-start.16 = (bf16[64,512]{1,0:T(8,128)(2,1)S(1)}, bf16[64,512]{1,0:T(8,128)(2,1)S(1)}, u32[]{:S(2)}, u32[]{:S(2)}) collective-permute-start(bf16[64,512]{1,0:T(8,128)(2,1)S(1)} %get-tuple-element.57), channel_id=1, source_target_pairs={{0,4},{1,5},{2,6},{3,7},{4,0},{5,1},{6,2},{7,3},{8,12},{9,13},{10,... | collective-permute-start | bytes 196616 | tf_op jit(solution)/shard_map/fit2/ppermute | solution.py:29
  41.0 0.1 fusion.14
  41.0 1.6 %collective-permute-start.22 = (bf16[256,512]{1,0:T(8,128)(2,1)S(1)}, bf16[256,512]{1,0:T(8,128)(2,1)S(1)}, u32[]{:S(2)}, u32[]{:S(2)}) collective-permute-start(bf16[256,512]{1,0:T(8,128)(2,1)S(1)} %fusion.14), channel_id=1, source_target_pairs={{0,16},{1,9},{2,18},{3,11},{4,20},{5,13},{6,22},{7,15},{8,24},{9,1... | collective-permute-start | bytes 786440 | tf_op jit(solution)/shard_map/squares1/ppermute | solution.py:37
  42.6 0.7 %collective-permute-done.15 = bf16[64,512]{1,0:T(8,128)(2,1)S(1)} collective-permute-done((bf16[64,512]{1,0:T(8,128)(2,1)S(1)}, bf16[64,512]{1,0:T(8,128)(2,1)S(1)}, u32[]{:S(2)}, u32[]{:S(2)}) %collective-permute-start.15) | collective-permute-done | bytes 65568 | tf_op jit(solution)/shard_map/fit3/ppermute | solution.py:29
  43.4 1.1 %collective-permute-done.17 = bf16[64,512]{1,0:T(8,128)(2,1)S(1)} collective-permute-done((bf16[64,512]{1,0:T(8,128)(2,1)S(1)}, bf16[64,512]{1,0:T(8,128)(2,1)S(1)}, u32[]{:S(2)}, u32[]{:S(2)}) %collective-permute-start.17) | collective-permute-done | bytes 65568 | tf_op jit(solution)/shard_map/fit1/ppermute | solution.py:29
  44.5 0.6 %collective-permute-done.16 = bf16[64,512]{1,0:T(8,128)(2,1)S(1)} collective-permute-done((bf16[64,512]{1,0:T(8,128)(2,1)S(1)}, bf16[64,512]{1,0:T(8,128)(2,1)S(1)}, u32[]{:S(2)}, u32[]{:S(2)}) %collective-permute-start.16) | collective-permute-done | bytes 65568 | tf_op jit(solution)/shard_map/fit2/ppermute | solution.py:29
  45.1 1.6 %collective-permute-start.20 = (bf16[64,512]{1,0:T(8,128)(2,1)S(1)}, bf16[64,512]{1,0:T(8,128)(2,1)S(1)}, u32[]{:S(2)}, u32[]{:S(2)}) collective-permute-start(bf16[64,512]{1,0:T(8,128)(2,1)S(1)} %fusion.18), channel_id=1, source_target_pairs={{0,6},{1,7},{2,4},{3,5},{4,2},{5,3},{6,0},{7,1},{8,14},{9,15},{10,... | collective-permute-start | bytes 196616 | tf_op jit(solution)/shard_map/residual3/ppermute | solution.py:29
  46.7 0.4 collective-permute-start.19
  47.2 2.4 %collective-permute-start.18 = (bf16[64,512]{1,0:T(8,128)(2,1)S(1)}, bf16[64,512]{1,0:T(8,128)(2,1)S(1)}, u32[]{:S(2)}, u32[]{:S(2)}) collective-permute-start(bf16[64,512]{1,0:T(8,128)(2,1)S(1)} %fusion.18), channel_id=1, source_target_pairs={{0,2},{1,3},{2,0},{3,1},{4,6},{5,7},{6,4},{7,5},{8,10},{9,11},{10,... | collective-permute-start | bytes 196616 | tf_op jit(solution)/shard_map/residual1/ppermute | solution.py:29
  49.6 0.1 convert_add_fusion
  49.7 1.9 %collective-permute-done.20 = bf16[64,512]{1,0:T(8,128)(2,1)S(1)} collective-permute-done((bf16[64,512]{1,0:T(8,128)(2,1)S(1)}, bf16[64,512]{1,0:T(8,128)(2,1)S(1)}, u32[]{:S(2)}, u32[]{:S(2)}) %collective-permute-start.20) | collective-permute-done | bytes 65568 | tf_op jit(solution)/shard_map/residual3/ppermute | solution.py:29
  51.6 1.4 %collective-permute-done.19 = bf16[64,512]{1,0:T(8,128)(2,1)S(1)} collective-permute-done((bf16[64,512]{1,0:T(8,128)(2,1)S(1)}, bf16[64,512]{1,0:T(8,128)(2,1)S(1)}, u32[]{:S(2)}, u32[]{:S(2)}) %collective-permute-start.19) | collective-permute-done | bytes 65568 | tf_op jit(solution)/shard_map/residual2/ppermute | solution.py:29
  53.0 0.1 collective-permute-start.23
  53.1 0.3 fusion.23
  53.4 1.2 %collective-permute-done.23 = bf16[256,512]{1,0:T(8,128)(2,1)S(1)} collective-permute-done((bf16[256,512]{1,0:T(8,128)(2,1)S(1)}, bf16[256,512]{1,0:T(8,128)(2,1)S(1)}, u32[]{:S(2)}, u32[]{:S(2)}) %collective-permute-start.23) | collective-permute-done | bytes 262176 | tf_op jit(solution)/shard_map/residual_core/ppermute | solution.py:24
  54.6 0.2 fusion.30
  54.9 1.1 %fusion.4 = f32[256,512]{1,0:T(8,128)} fusion(f32[256,512]{1,0:T(8,128)S(1)} %get-tuple-element.79, f32[256,512]{1,0:T(8,128)S(1)} %fusion.30, bf16[256,512]{1,0:T(8,128)(2,1)S(1)} %constant_dynamic-update-slice_fusion.4, f32[256,512]{1,0:T(8,128)S(1)} %get-tuple-element.48, f32[256,512]{1,0:T(8,128)S(1)} %get-tuple-element.47, f32[256]{0:T(256)S(1)} %add_divide_fusion, ...), kind=kOutput, calls=%fused_computation.5 | convolution fusion | flops 68812800 | bytes 3015680 | tf_op jit(solution)/shard_map/dot_general | solution.py:109
  (53 shorter events, 0.7 us)
Async XLA Ops:
  0.6 6.9 %copy-start.2 = (f32[256,512]{1,0:T(8,128)S(1)}, f32[256,512]{1,0:T(8,128)}, u32[]{:S(2)}) copy-start(f32[256,512]{1,0:T(8,128)} %param.8) | copy-start | bytes 1572868
  0.6 6.9 %copy-start.3 = (f32[256,512]{1,0:T(8,128)S(1)}, f32[256,512]{1,0:T(8,128)}, u32[]{:S(2)}) copy-start(f32[256,512]{1,0:T(8,128)} %param.7) | copy-start | bytes 1572868
  1.7 7.8 %collective-permute-start = (bf16[2,64,256]{2,1,0:T(8,128)(2,1)S(1)}, bf16[2,64,256]{2,1,0:T(8,128)(2,1)S(1)}, u32[]{:S(2)}, u32[]{:S(2)}) collective-permute-start(bf16[2,64,256]{2,1,0:T(8,128)(2,1)S(1)} %pad_maximum_fusion.3), channel_id=1, source_target_pairs={{0,6},{1,7},{2,4},{3,5},{4,2},{5,3},{6,0},{7,1},{8,14},{9,15},{10,... | collective-permute-start | bytes 196616 | tf_op jit(solution)/shard_map/cells3/ppermute | solution.py:29
  6.8 5.6 %collective-permute-start.1 = (bf16[2,64,256]{2,1,0:T(8,128)(2,1)S(1)}, bf16[2,64,256]{2,1,0:T(8,128)(2,1)S(1)}, u32[]{:S(2)}, u32[]{:S(2)}) collective-permute-start(bf16[2,64,256]{2,1,0:T(8,128)(2,1)S(1)} %pad_maximum_fusion.4), channel_id=1, source_target_pairs={{0,4},{1,5},{2,6},{3,7},{4,0},{5,1},{6,2},{7,3},{8,12},{9,13},{10,... | collective-permute-start | bytes 196616 | tf_op jit(solution)/shard_map/cells2/ppermute | solution.py:29
  6.9 2.5 %copy-start.4 = (bf16[64,512]{1,0:T(8,128)(2,1)S(1)}, bf16[64,512]{1,0:T(8,128)(2,1)}, u32[]{:S(2)}) copy-start(bf16[64,512]{1,0:T(8,128)(2,1)} %param.6) | copy-start | bytes 196612
  6.9 5.5 %collective-permute-start.2 = (bf16[2,64,256]{2,1,0:T(8,128)(2,1)S(1)}, bf16[2,64,256]{2,1,0:T(8,128)(2,1)S(1)}, u32[]{:S(2)}, u32[]{:S(2)}) collective-permute-start(bf16[2,64,256]{2,1,0:T(8,128)(2,1)S(1)} %pad_maximum_fusion.5), channel_id=1, source_target_pairs={{0,2},{1,3},{2,0},{3,1},{4,6},{5,7},{6,4},{7,5},{8,10},{9,11},{10,... | collective-permute-start | bytes 196616 | tf_op jit(solution)/shard_map/cells1/ppermute | solution.py:29
  7.7 6.4 %collective-permute-start.4 = (bf16[256,512]{1,0:T(8,128)(2,1)S(1)}, bf16[256,512]{1,0:T(8,128)(2,1)S(1)}, u32[]{:S(2)}, u32[]{:S(2)}) collective-permute-start(bf16[256,512]{1,0:T(8,128)(2,1)S(1)} %get-tuple-element.51), channel_id=1, source_target_pairs={{0,8},{1,17},{2,10},{3,19},{4,12},{5,21},{6,14},{7,23},{8,0},{9,25... | collective-permute-start | bytes 786440 | tf_op jit(solution)/shard_map/squares0/ppermute | solution.py:37
  9.5 3.4 %collective-permute-start.3 = (bf16[256,512]{1,0:T(8,128)(2,1)S(1)}, bf16[256,512]{1,0:T(8,128)(2,1)S(1)}, u32[]{:S(2)}, u32[]{:S(2)}) collective-permute-start(bf16[256,512]{1,0:T(8,128)(2,1)S(1)} %get-tuple-element.54), channel_id=1, source_target_pairs={{0,1},{1,0},{2,3},{3,2},{4,5},{5,4},{6,7},{7,6},{8,9},{9,8},{10,11... | collective-permute-start | bytes 786440 | tf_op jit(solution)/shard_map/coef_core/ppermute | solution.py:24
  9.5 3.0 %copy-start.5 = (f32[256]{0:T(256)S(1)}, f32[256]{0:T(256)}, u32[]{:S(2)}) copy-start(f32[256]{0:T(256)} %param.9) | copy-start | bytes 3076
  14.2 6.4 %collective-permute-start.5 = (bf16[64,512]{1,0:T(8,128)(2,1)S(1)}, bf16[64,512]{1,0:T(8,128)(2,1)S(1)}, u32[]{:S(2)}, u32[]{:S(2)}) collective-permute-start(bf16[64,512]{1,0:T(8,128)(2,1)S(1)} %get-tuple-element.58), channel_id=1, source_target_pairs={{0,6},{1,7},{2,4},{3,5},{4,2},{5,3},{6,0},{7,1},{8,14},{9,15},{10,... | collective-permute-start | bytes 196616 | tf_op jit(solution)/shard_map/fit3/ppermute | solution.py:29
  18.1 4.3 %collective-permute-start.7 = (bf16[64,512]{1,0:T(8,128)(2,1)S(1)}, bf16[64,512]{1,0:T(8,128)(2,1)S(1)}, u32[]{:S(2)}, u32[]{:S(2)}) collective-permute-start(bf16[64,512]{1,0:T(8,128)(2,1)S(1)} %get-tuple-element.59), channel_id=1, source_target_pairs={{0,2},{1,3},{2,0},{3,1},{4,6},{5,7},{6,4},{7,5},{8,10},{9,11},{10,... | collective-permute-start | bytes 196616 | tf_op jit(solution)/shard_map/fit1/ppermute | solution.py:29
  18.1 5.2 %collective-permute-start.6 = (bf16[64,512]{1,0:T(8,128)(2,1)S(1)}, bf16[64,512]{1,0:T(8,128)(2,1)S(1)}, u32[]{:S(2)}, u32[]{:S(2)}) collective-permute-start(bf16[64,512]{1,0:T(8,128)(2,1)S(1)} %get-tuple-element.60), channel_id=1, source_target_pairs={{0,4},{1,5},{2,6},{3,7},{4,0},{5,1},{6,2},{7,3},{8,12},{9,13},{10,... | collective-permute-start | bytes 196616 | tf_op jit(solution)/shard_map/fit2/ppermute | solution.py:29
  18.8 9.0 %collective-permute-start.12 = (bf16[256,256]{1,0:T(8,128)(2,1)S(1)}, bf16[256,256]{1,0:T(8,128)(2,1)S(1)}, u32[]{:S(2)}, u32[]{:S(2)}) collective-permute-start(bf16[256,256]{1,0:T(8,128)(2,1)S(1)} %pad_maximum_fusion.1), channel_id=1, source_target_pairs={{0,1},{1,0},{2,3},{3,2},{4,5},{5,4},{6,7},{7,6},{8,9},{9,8},{10,11... | collective-permute-start | bytes 393224 | tf_op jit(solution)/shard_map/cells_core/ppermute | solution.py:24
  18.9 8.9 %collective-permute-start.11 = (bf16[256,512]{1,0:T(8,128)(2,1)S(1)}, bf16[256,512]{1,0:T(8,128)(2,1)S(1)}, u32[]{:S(2)}, u32[]{:S(2)}) collective-permute-start(bf16[256,512]{1,0:T(8,128)(2,1)S(1)} %convert_element_type.83), channel_id=1, source_target_pairs={{0,16},{1,9},{2,18},{3,11},{4,20},{5,13},{6,22},{7,15},{8,24},{9,1... | collective-permute-start | bytes 786440 | tf_op jit(solution)/shard_map/squares1/ppermute | solution.py:37
  23.3 6.6 %collective-permute-start.10 = (bf16[64,512]{1,0:T(8,128)(2,1)S(1)}, bf16[64,512]{1,0:T(8,128)(2,1)S(1)}, u32[]{:S(2)}, u32[]{:S(2)}) collective-permute-start(bf16[64,512]{1,0:T(8,128)(2,1)S(1)} %add_convert_fusion), channel_id=1, source_target_pairs={{0,6},{1,7},{2,4},{3,5},{4,2},{5,3},{6,0},{7,1},{8,14},{9,15},{10,... | collective-permute-start | bytes 196616 | tf_op jit(solution)/shard_map/residual3/ppermute | solution.py:29
  25.0 6.4 %collective-permute-start.9 = (bf16[64,512]{1,0:T(8,128)(2,1)S(1)}, bf16[64,512]{1,0:T(8,128)(2,1)S(1)}, u32[]{:S(2)}, u32[]{:S(2)}) collective-permute-start(bf16[64,512]{1,0:T(8,128)(2,1)S(1)} %add_convert_fusion), channel_id=1, source_target_pairs={{0,4},{1,5},{2,6},{3,7},{4,0},{5,1},{6,2},{7,3},{8,12},{9,13},{10,... | collective-permute-start | bytes 196616 | tf_op jit(solution)/shard_map/residual2/ppermute | solution.py:29
  26.9 4.7 %collective-permute-start.8 = (bf16[64,512]{1,0:T(8,128)(2,1)S(1)}, bf16[64,512]{1,0:T(8,128)(2,1)S(1)}, u32[]{:S(2)}, u32[]{:S(2)}) collective-permute-start(bf16[64,512]{1,0:T(8,128)(2,1)S(1)} %add_convert_fusion), channel_id=1, source_target_pairs={{0,2},{1,3},{2,0},{3,1},{4,6},{5,7},{6,4},{7,5},{8,10},{9,11},{10,... | collective-permute-start | bytes 196616 | tf_op jit(solution)/shard_map/residual1/ppermute | solution.py:29
  31.6 1.6 %collective-permute-start.13 = (bf16[256,512]{1,0:T(8,128)(2,1)S(1)}, bf16[256,512]{1,0:T(8,128)(2,1)S(1)}, u32[]{:S(2)}, u32[]{:S(2)}) collective-permute-start(bf16[256,512]{1,0:T(8,128)(2,1)S(1)} %constant_dynamic-update-slice_fusion), channel_id=1, source_target_pairs={{0,1},{1,0},{2,3},{3,2},{4,5},{5,4},{6,7},{7,6},{8,9},{9,8},{10,11... | collective-permute-start | bytes 786440 | tf_op jit(solution)/shard_map/residual_core/ppermute | solution.py:24
  34.1 2.2 %collective-permute-start.14 = (bf16[256,512]{1,0:T(8,128)(2,1)S(1)}, bf16[256,512]{1,0:T(8,128)(2,1)S(1)}, u32[]{:S(2)}, u32[]{:S(2)}) collective-permute-start(bf16[256,512]{1,0:T(8,128)(2,1)S(1)} %get-tuple-element.53), channel_id=1, source_target_pairs={{0,1},{1,0},{2,3},{3,2},{4,5},{5,4},{6,7},{7,6},{8,9},{9,8},{10,11... | collective-permute-start | bytes 786440 | tf_op jit(solution)/shard_map/coef_core/ppermute | solution.py:24
  34.3 6.7 %collective-permute-start.21 = (bf16[256,512]{1,0:T(8,128)(2,1)S(1)}, bf16[256,512]{1,0:T(8,128)(2,1)S(1)}, u32[]{:S(2)}, u32[]{:S(2)}) collective-permute-start(bf16[256,512]{1,0:T(8,128)(2,1)S(1)} %get-tuple-element.49), channel_id=1, source_target_pairs={{0,8},{1,17},{2,10},{3,19},{4,12},{5,21},{6,14},{7,23},{8,0},{9,25... | collective-permute-start | bytes 786440 | tf_op jit(solution)/shard_map/squares0/ppermute | solution.py:37
  36.5 6.8 %collective-permute-start.15 = (bf16[64,512]{1,0:T(8,128)(2,1)S(1)}, bf16[64,512]{1,0:T(8,128)(2,1)S(1)}, u32[]{:S(2)}, u32[]{:S(2)}) collective-permute-start(bf16[64,512]{1,0:T(8,128)(2,1)S(1)} %get-tuple-element.55), channel_id=1, source_target_pairs={{0,6},{1,7},{2,4},{3,5},{4,2},{5,3},{6,0},{7,1},{8,14},{9,15},{10,... | collective-permute-start | bytes 196616 | tf_op jit(solution)/shard_map/fit3/ppermute | solution.py:29
  37.8 6.7 %collective-permute-start.17 = (bf16[64,512]{1,0:T(8,128)(2,1)S(1)}, bf16[64,512]{1,0:T(8,128)(2,1)S(1)}, u32[]{:S(2)}, u32[]{:S(2)}) collective-permute-start(bf16[64,512]{1,0:T(8,128)(2,1)S(1)} %get-tuple-element.56), channel_id=1, source_target_pairs={{0,2},{1,3},{2,0},{3,1},{4,6},{5,7},{6,4},{7,5},{8,10},{9,11},{10,... | collective-permute-start | bytes 196616 | tf_op jit(solution)/shard_map/fit1/ppermute | solution.py:29
  37.8 7.3 %collective-permute-start.16 = (bf16[64,512]{1,0:T(8,128)(2,1)S(1)}, bf16[64,512]{1,0:T(8,128)(2,1)S(1)}, u32[]{:S(2)}, u32[]{:S(2)}) collective-permute-start(bf16[64,512]{1,0:T(8,128)(2,1)S(1)} %get-tuple-element.57), channel_id=1, source_target_pairs={{0,4},{1,5},{2,6},{3,7},{4,0},{5,1},{6,2},{7,3},{8,12},{9,13},{10,... | collective-permute-start | bytes 196616 | tf_op jit(solution)/shard_map/fit2/ppermute | solution.py:29
  41.0 8.5 %collective-permute-start.22 = (bf16[256,512]{1,0:T(8,128)(2,1)S(1)}, bf16[256,512]{1,0:T(8,128)(2,1)S(1)}, u32[]{:S(2)}, u32[]{:S(2)}) collective-permute-start(bf16[256,512]{1,0:T(8,128)(2,1)S(1)} %fusion.14), channel_id=1, source_target_pairs={{0,16},{1,9},{2,18},{3,11},{4,20},{5,13},{6,22},{7,15},{8,24},{9,1... | collective-permute-start | bytes 786440 | tf_op jit(solution)/shard_map/squares1/ppermute | solution.py:37
  45.1 6.5 %collective-permute-start.20 = (bf16[64,512]{1,0:T(8,128)(2,1)S(1)}, bf16[64,512]{1,0:T(8,128)(2,1)S(1)}, u32[]{:S(2)}, u32[]{:S(2)}) collective-permute-start(bf16[64,512]{1,0:T(8,128)(2,1)S(1)} %fusion.18), channel_id=1, source_target_pairs={{0,6},{1,7},{2,4},{3,5},{4,2},{5,3},{6,0},{7,1},{8,14},{9,15},{10,... | collective-permute-start | bytes 196616 | tf_op jit(solution)/shard_map/residual3/ppermute | solution.py:29
  46.7 6.3 %collective-permute-start.19 = (bf16[64,512]{1,0:T(8,128)(2,1)S(1)}, bf16[64,512]{1,0:T(8,128)(2,1)S(1)}, u32[]{:S(2)}, u32[]{:S(2)}) collective-permute-start(bf16[64,512]{1,0:T(8,128)(2,1)S(1)} %fusion.18), channel_id=1, source_target_pairs={{0,4},{1,5},{2,6},{3,7},{4,0},{5,1},{6,2},{7,3},{8,12},{9,13},{10,... | collective-permute-start | bytes 196616 | tf_op jit(solution)/shard_map/residual2/ppermute | solution.py:29
  47.2 5.8 %collective-permute-start.18 = (bf16[64,512]{1,0:T(8,128)(2,1)S(1)}, bf16[64,512]{1,0:T(8,128)(2,1)S(1)}, u32[]{:S(2)}, u32[]{:S(2)}) collective-permute-start(bf16[64,512]{1,0:T(8,128)(2,1)S(1)} %fusion.18), channel_id=1, source_target_pairs={{0,2},{1,3},{2,0},{3,1},{4,6},{5,7},{6,4},{7,5},{8,10},{9,11},{10,... | collective-permute-start | bytes 196616 | tf_op jit(solution)/shard_map/residual1/ppermute | solution.py:29
  53.0 1.6 %collective-permute-start.23 = (bf16[256,512]{1,0:T(8,128)(2,1)S(1)}, bf16[256,512]{1,0:T(8,128)(2,1)S(1)}, u32[]{:S(2)}, u32[]{:S(2)}) collective-permute-start(bf16[256,512]{1,0:T(8,128)(2,1)S(1)} %constant_dynamic-update-slice_fusion.4), channel_id=1, source_target_pairs={{0,1},{1,0},{2,3},{3,2},{4,5},{5,4},{6,7},{7,6},{8,9},{9,8},{10,11... | collective-permute-start | bytes 786440 | tf_op jit(solution)/shard_map/residual_core/ppermute | solution.py:24
  53.4 2.6 %copy-start = (f32[256,512]{1,0:T(8,128)}, f32[256,512]{1,0:T(8,128)S(1)}, u32[]{:S(2)}) copy-start(f32[256,512]{1,0:T(8,128)S(1)} %get-tuple-element.47) | copy-start | bytes 1572868
  53.4 2.6 %copy-start.1 = (f32[256,512]{1,0:T(8,128)}, f32[256,512]{1,0:T(8,128)S(1)}, u32[]{:S(2)}) copy-start(f32[256,512]{1,0:T(8,128)S(1)} %get-tuple-element.48) | copy-start | bytes 1572868

commit v4 on v3

--- a/solution.py
+++ b/solution.py
@@ -66,10 +66,19 @@
         pairs[k] = chip_swap(pairs[k], k, f"cells{k}")
     weights = jnp.broadcast_to(penalty[:, None], coef_init.shape)
     response_rows = responses.astype(f32)
+
+    def fit(k):
+        return dot(pairs[k][0], coef_copy) + dot(pairs[k][1], coef_other)
+
+    total = fit(0)
+    leaving = {}
+    before = ()
+    for k in far_first:
+        if before:
+            pairs[k], *_ = together(pairs[k], *before)
+        leaving[k] = fit(k).astype(bf16)
+        before = (leaving[k],)
     order = [0] + far_first
-    *ordered, weights, response_rows = together(*[pairs[k] for k in order], weights, response_rows)
-    for k, pair in zip(order, ordered):
-        pairs[k] = pair
     own = jnp.concatenate([pairs[k][0] for k in order])
     other = jnp.concatenate([pairs[k][1] for k in order])
 
@@ -83,15 +92,15 @@
         if step > 0:
             coef_copy = coef.astype(bf16)
             coef_other = core_swap(coef_copy, "coef_core")
-        fitted = (dot(own, coef_copy) + dot(other, coef_other)).reshape(chips, cells, targets)
-        total = fitted[0] - response_rows
-        leaving = fitted.astype(bf16)
-        held = other
-        if step == 0:
-            leaving, total, held, squares = together(leaving, total, held, squares)
-        arrived = [chip_swap(leaving[order.index(k)], k, f"fit{k}") for k in far_first]
+            fitted = (dot(own, coef_copy) + dot(other, coef_other)).reshape(chips, cells, targets)
+            total = fitted[0]
+            leaving = {k: fitted[order.index(k)].astype(bf16) for k in far_first}
+        else:
+            held, squares, weights, response_rows, *_ = together(other, squares, weights, response_rows, *before)
+        arrived = [chip_swap(leaving[k], k, f"fit{k}") for k in far_first]
         for bit in range(1, cond_bits):
             squares = squares + cond_swap(squares.astype(bf16), 1 << bit, f"squares{bit}").astype(f32)
+        total = total - response_rows
         for part in arrived:
             total = total + part.astype(f32)
         residual = [total.astype(bf16)] * chips

time: 56.1 us -> 54.9 us (0.979)
  waiting for transfers between devices: 18.8 us -> 16.2 us
  local copies, waits for them, and re-layouts: 1.22 us -> 2.52 us
  matrix products: 3.04 us -> 3.9 us
  starting transfers between devices: 30.9 us -> 30.1 us
    ppermute x15, waiting for transfers between devices: 15 us -> 12.3 us  [chip_swap(): lax.ppermute(value, 'shard', [(i, i ^ 2 * mask) for i in range(lax.axis_s...]
    unnamed x18, local copies, waits for them, and re-layouts: 0.07 us -> 1.39 us
    another operation x1 -> x0, local copies, waits for them, and re-layouts: 0.98 us -> none  [shards(): pairs = [jnp.stack([columns(k, 0), columns(k, 1)]) for k in range(chips)]]
    dynamic_slice x0 -> x1, local copies, waits for them, and re-layouts: none -> 0.98 us  [columns(): return lax.dynamic_slice_in_dim(expression, start, mine, 1)]
    ppermute x4, starting transfers between devices: 6.81 us -> 5.9 us  [cond_swap(): return lax.ppermute(value, ('cond', 'shard'), pairs)]
    dot_general x4 -> x10, matrix products: 0.9 us -> 1.76 us  [dot(): return jnp.dot(x, c, preferred_element_type=f32)]
    ppermute x5, waiting for transfers between devices: 2.77 us -> 3.6 us  [core_swap(): lax.ppermute(value, 'shard', [(i, i ^ 1) for i in range(lax.axis_size('sh...]
    ppermute x4, waiting for transfers between devices: 1.05 us -> 0.27 us  [cond_swap(): return lax.ppermute(value, ('cond', 'shard'), pairs)]
  transfers between devices with their start and end apart: 24 -> 24, of which waited for: 14 -> 13; matrix products, arithmetic and copies ran while one was open for 3% -> 5% of each run, Pallas kernels for 0% -> 0%
where the time goes in v4:
time: 54.9 us; the launch traced here: 54.7 us
  starting transfers between devices  30.1 us (55%)
  waiting for transfers between devices  16.2 us (30%)
  matrix products  3.9 us (7%)
  local copies, waits for them, and re-layouts  2.52 us (5%)
  between operations  1.08 us (2%)
  other arithmetic  0.94 us (2%)
    ppermute x15, starting transfers between devices, chip_swap(): lax.ppermute(value, 'shard', [(i, i ^ 2 * mask) for i in range(lax.axis_s...  23.7 us
    ppermute x15, waiting for transfers between devices, chip_swap(): lax.ppermute(value, 'shard', [(i, i ^ 2 * mask) for i in range(lax.axis_s...  12.3 us
    ppermute x4, starting transfers between devices, cond_swap(): return lax.ppermute(value, ('cond', 'shard'), pairs)  5.9 us
    ppermute x5, waiting for transfers between devices, core_swap(): lax.ppermute(value, 'shard', [(i, i ^ 1) for i in range(lax.axis_size('sh...  3.6 us
    dot_general x10, matrix products, dot(): return jnp.dot(x, c, preferred_element_type=f32)  1.76 us
    dot_general x2, matrix products, shards(): lax.dot_general(own, residual, contract, preferred_element_type=f32)  1.66 us
    unnamed x18, local copies, waits for them, and re-layouts  1.39 us
  transfers between devices with their start and end apart: 24, of which 13 were waited for; matrix products, arithmetic and copies ran while one was open for 5% of the time, Pallas kernels for 0%

profile of v4, /device:TPU:0, one launch (start us, length us, event | category | flops | bytes accessed | tf_op | source)
XLA Modules:
  0.0 54.7 jit_solution(9562533480734185599)
XLA Ops:
  0.7 1.0 %constant_dynamic-slice_fusion = (bf16[64,256]{1,0:T(8,128)(2,1)S(1)}, bf16[1,64,256]{2,1,0:T(8,128)(2,1)S(1)}, bf16[1,64,256]{2,1,0:T(8,128)(2,1)S(1)}, bf16[1,...) fusion(bf16[64,2048]{1,0:T(8,128)(2,1)} %param.5, ...), kind=kLoop, calls=%fused_computation.72 | loop fusion | bytes 524320 | tf_op jit(solution)/shard_map/dynamic_slice | solution.py:60
  1.7 5.1 %collective-permute-start = (bf16[2,64,256]{2,1,0:T(8,128)(2,1)S(1)}, bf16[2,64,256]{2,1,0:T(8,128)(2,1)S(1)}, u32[]{:S(2)}, u32[]{:S(2)}) collective-permute-start(bf16[2,64,256]{2,1,0:T(8,128)(2,1)S(1)} %pad_maximum_fusion.2), channel_id=1, source_target_pairs={{0,6},{1,7},{2,4},{3,5},{4,2},{5,3},{6,0},{7,1},{8,14},{9,15},{10,... | collective-permute-start | bytes 196616 | tf_op jit(solution)/shard_map/cells3/ppermute | solution.py:29
  6.9 0.6 %collective-permute-start.3 = (bf16[2,64,256]{2,1,0:T(8,128)(2,1)S(1)}, bf16[2,64,256]{2,1,0:T(8,128)(2,1)S(1)}, u32[]{:S(2)}, u32[]{:S(2)}) collective-permute-start(bf16[2,64,256]{2,1,0:T(8,128)(2,1)S(1)} %pad_maximum_fusion.4), channel_id=1, source_target_pairs={{0,2},{1,3},{2,0},{3,1},{4,6},{5,7},{6,4},{7,5},{8,10},{9,11},{10,... | collective-permute-start | bytes 196616 | tf_op jit(solution)/shard_map/cells1/ppermute | solution.py:29
  7.6 0.1 multiply_convert_fusion.1
  7.7 1.8 %collective-permute-start.4 = (bf16[256,512]{1,0:T(8,128)(2,1)S(1)}, bf16[256,512]{1,0:T(8,128)(2,1)S(1)}, u32[]{:S(2)}, u32[]{:S(2)}) collective-permute-start(bf16[256,512]{1,0:T(8,128)(2,1)S(1)} %get-tuple-element.43), channel_id=1, source_target_pairs={{0,8},{1,17},{2,10},{3,19},{4,12},{5,21},{6,14},{7,23},{8,0},{9,25... | collective-permute-start | bytes 786440 | tf_op jit(solution)/shard_map/squares0/ppermute | solution.py:37
  9.5 0.2 fusion.38
  9.6 0.7 %copy-done.4 = bf16[64,512]{1,0:T(8,128)(2,1)S(1)} copy-done((bf16[64,512]{1,0:T(8,128)(2,1)S(1)}, bf16[64,512]{1,0:T(8,128)(2,1)}, u32[]{:S(2)}) %copy-start.4) | copy-done | bytes 65560
  10.3 0.7 %collective-permute-done.2 = bf16[256,512]{1,0:T(8,128)(2,1)S(1)} collective-permute-done((bf16[256,512]{1,0:T(8,128)(2,1)S(1)}, bf16[256,512]{1,0:T(8,128)(2,1)S(1)}, u32[]{:S(2)}, u32[]{:S(2)}) %collective-permute-start.2) | collective-permute-done | bytes 262176 | tf_op jit(solution)/shard_map/coef_core/ppermute | solution.py:24
  11.0 0.2 fusion.31
  11.1 0.2 fusion.14
  11.3 3.7 %collective-permute-start.5 = (bf16[64,512]{1,0:T(8,128)(2,1)S(1)}, bf16[64,512]{1,0:T(8,128)(2,1)S(1)}, u32[]{:S(2)}, u32[]{:S(2)}) collective-permute-start(bf16[64,512]{1,0:T(8,128)(2,1)S(1)} %fusion.14), channel_id=1, source_target_pairs={{0,6},{1,7},{2,4},{3,5},{4,2},{5,3},{6,0},{7,1},{8,14},{9,15},{10,... | collective-permute-start | bytes 196616 | tf_op jit(solution)/shard_map/fit3/ppermute | solution.py:29
  15.0 0.2 fusion.29
  15.2 0.2 fusion.15
  15.4 0.2 fusion.30
  15.6 0.2 fusion.16
  15.8 0.8 %collective-permute-start.7 = (bf16[64,512]{1,0:T(8,128)(2,1)S(1)}, bf16[64,512]{1,0:T(8,128)(2,1)S(1)}, u32[]{:S(2)}, u32[]{:S(2)}) collective-permute-start(bf16[64,512]{1,0:T(8,128)(2,1)S(1)} %fusion.16), channel_id=1, source_target_pairs={{0,2},{1,3},{2,0},{3,1},{4,6},{5,7},{6,4},{7,5},{8,10},{9,11},{10,... | collective-permute-start | bytes 196616 | tf_op jit(solution)/shard_map/fit1/ppermute | solution.py:29
  16.7 0.7 %copy-done.5 = f32[256]{0:T(256)S(1)} copy-done((f32[256]{0:T(256)S(1)}, f32[256]{0:T(256)}, u32[]{:S(2)}) %copy-start.5) | copy-done | bytes 1048
  17.6 1.6 %collective-permute-start.11 = (bf16[256,512]{1,0:T(8,128)(2,1)S(1)}, bf16[256,512]{1,0:T(8,128)(2,1)S(1)}, u32[]{:S(2)}, u32[]{:S(2)}) collective-permute-start(bf16[256,512]{1,0:T(8,128)(2,1)S(1)} %convert_element_type.86), channel_id=1, source_target_pairs={{0,16},{1,9},{2,18},{3,11},{4,20},{5,13},{6,22},{7,15},{8,24},{9,1... | collective-permute-start | bytes 786440 | tf_op jit(solution)/shard_map/squares1/ppermute | solution.py:37
  19.2 2.0 %collective-permute-done.7 = bf16[64,512]{1,0:T(8,128)(2,1)S(1)} collective-permute-done((bf16[64,512]{1,0:T(8,128)(2,1)S(1)}, bf16[64,512]{1,0:T(8,128)(2,1)S(1)}, u32[]{:S(2)}, u32[]{:S(2)}) %collective-permute-start.7) | collective-permute-done | bytes 65568 | tf_op jit(solution)/shard_map/fit1/ppermute | solution.py:29
  21.3 0.2 fusion.17
  21.5 2.3 %collective-permute-start.10 = (bf16[64,512]{1,0:T(8,128)(2,1)S(1)}, bf16[64,512]{1,0:T(8,128)(2,1)S(1)}, u32[]{:S(2)}, u32[]{:S(2)}) collective-permute-start(bf16[64,512]{1,0:T(8,128)(2,1)S(1)} %fusion.17), channel_id=1, source_target_pairs={{0,6},{1,7},{2,4},{3,5},{4,2},{5,3},{6,0},{7,1},{8,14},{9,15},{10,... | collective-permute-start | bytes 196616 | tf_op jit(solution)/shard_map/residual3/ppermute | solution.py:29
  23.7 2.2 %collective-permute-start.8 = (bf16[64,512]{1,0:T(8,128)(2,1)S(1)}, bf16[64,512]{1,0:T(8,128)(2,1)S(1)}, u32[]{:S(2)}, u32[]{:S(2)}) collective-permute-start(bf16[64,512]{1,0:T(8,128)(2,1)S(1)} %fusion.17), channel_id=1, source_target_pairs={{0,2},{1,3},{2,0},{3,1},{4,6},{5,7},{6,4},{7,5},{8,10},{9,11},{10,... | collective-permute-start | bytes 196616 | tf_op jit(solution)/shard_map/residual1/ppermute | solution.py:29
  26.1 2.0 %collective-permute-done.10 = bf16[64,512]{1,0:T(8,128)(2,1)S(1)} collective-permute-done((bf16[64,512]{1,0:T(8,128)(2,1)S(1)}, bf16[64,512]{1,0:T(8,128)(2,1)S(1)}, u32[]{:S(2)}, u32[]{:S(2)}) %collective-permute-start.10) | collective-permute-done | bytes 65568 | tf_op jit(solution)/shard_map/residual3/ppermute | solution.py:29
  28.1 1.5 %collective-permute-done.9 = bf16[64,512]{1,0:T(8,128)(2,1)S(1)} collective-permute-done((bf16[64,512]{1,0:T(8,128)(2,1)S(1)}, bf16[64,512]{1,0:T(8,128)(2,1)S(1)}, u32[]{:S(2)}, u32[]{:S(2)}) %collective-permute-start.9) | collective-permute-done | bytes 65568 | tf_op jit(solution)/shard_map/residual2/ppermute | solution.py:29
  29.7 1.5 %collective-permute-done.13 = bf16[256,512]{1,0:T(8,128)(2,1)S(1)} collective-permute-done((bf16[256,512]{1,0:T(8,128)(2,1)S(1)}, bf16[256,512]{1,0:T(8,128)(2,1)S(1)}, u32[]{:S(2)}, u32[]{:S(2)}) %collective-permute-start.13) | collective-permute-done | bytes 262176 | tf_op jit(solution)/shard_map/residual_core/ppermute | solution.py:24
  31.2 0.2 fusion.39
  31.4 0.6 %multiply_convert_fusion = (bf16[256,512]{1,0:T(8,128)(2,1)S(1)}, f32[256,512]{1,0:T(8,128)S(1)}, bf16[256,512]{1,0:T(8,128)(2,1)S(1)}, f32[256,512]{1,0:T(8,128)S(1)}) fusion(f32[256,512]{1,0:T(8,128)S(1)} %get-tuple-element.44, f32[256,512]{1,0:T(8,128)S(1)} %broadcast_in_dim.2, f32[256,512]{1,0:T(8,128)S(1)} %convert_add_fusion.2, ...), kind=kOutput, calls=%fused_computation.35 | convolution fusion | flops 69992448 | bytes 4588544 | tf_op jit(solution)/shard_map/dot_general | solution.py:118
  32.0 0.2 collective-permute-start.14
  32.2 1.0 %collective-permute-start.21 = (bf16[256,512]{1,0:T(8,128)(2,1)S(1)}, bf16[256,512]{1,0:T(8,128)(2,1)S(1)}, u32[]{:S(2)}, u32[]{:S(2)}) collective-permute-start(bf16[256,512]{1,0:T(8,128)(2,1)S(1)} %get-tuple-element.41), channel_id=1, source_target_pairs={{0,8},{1,17},{2,10},{3,19},{4,12},{5,21},{6,14},{7,23},{8,0},{9,25... | collective-permute-start | bytes 786440 | tf_op jit(solution)/shard_map/squares0/ppermute | solution.py:37
  33.2 0.2 fusion.32
  33.4 0.2 collective-permute-done.14
  33.6 0.2 fusion.37
  33.9 2.6 %collective-permute-start.15 = (bf16[64,512]{1,0:T(8,128)(2,1)S(1)}, bf16[64,512]{1,0:T(8,128)(2,1)S(1)}, u32[]{:S(2)}, u32[]{:S(2)}) collective-permute-start(bf16[64,512]{1,0:T(8,128)(2,1)S(1)} %get-tuple-element.47), channel_id=1, source_target_pairs={{0,6},{1,7},{2,4},{3,5},{4,2},{5,3},{6,0},{7,1},{8,14},{9,15},{10,... | collective-permute-start | bytes 196616 | tf_op jit(solution)/shard_map/fit3/ppermute | solution.py:29
  36.4 1.9 %collective-permute-start.16 = (bf16[64,512]{1,0:T(8,128)(2,1)S(1)}, bf16[64,512]{1,0:T(8,128)(2,1)S(1)}, u32[]{:S(2)}, u32[]{:S(2)}) collective-permute-start(bf16[64,512]{1,0:T(8,128)(2,1)S(1)} %get-tuple-element.49), channel_id=1, source_target_pairs={{0,4},{1,5},{2,6},{3,7},{4,0},{5,1},{6,2},{7,3},{8,12},{9,13},{10,... | collective-permute-start | bytes 196616 | tf_op jit(solution)/shard_map/fit2/ppermute | solution.py:29
  38.3 0.3 collective-permute-done.21
  38.6 1.6 %collective-permute-start.22 = (bf16[256,512]{1,0:T(8,128)(2,1)S(1)}, bf16[256,512]{1,0:T(8,128)(2,1)S(1)}, u32[]{:S(2)}, u32[]{:S(2)}) collective-permute-start(bf16[256,512]{1,0:T(8,128)(2,1)S(1)} %fusion.22), channel_id=1, source_target_pairs={{0,16},{1,9},{2,18},{3,11},{4,20},{5,13},{6,22},{7,15},{8,24},{9,1... | collective-permute-start | bytes 786440 | tf_op jit(solution)/shard_map/squares1/ppermute | solution.py:37
  40.2 0.4 collective-permute-done.15
  40.7 2.3 %collective-permute-done.17 = bf16[64,512]{1,0:T(8,128)(2,1)S(1)} collective-permute-done((bf16[64,512]{1,0:T(8,128)(2,1)S(1)}, bf16[64,512]{1,0:T(8,128)(2,1)S(1)}, u32[]{:S(2)}, u32[]{:S(2)}) %collective-permute-start.17) | collective-permute-done | bytes 65568 | tf_op jit(solution)/shard_map/fit1/ppermute | solution.py:29
  42.9 0.2 collective-permute-done.16
  43.2 2.4 %collective-permute-start.20 = (bf16[64,512]{1,0:T(8,128)(2,1)S(1)}, bf16[64,512]{1,0:T(8,128)(2,1)S(1)}, u32[]{:S(2)}, u32[]{:S(2)}) collective-permute-start(bf16[64,512]{1,0:T(8,128)(2,1)S(1)} %fusion.26), channel_id=1, source_target_pairs={{0,6},{1,7},{2,4},{3,5},{4,2},{5,3},{6,0},{7,1},{8,14},{9,15},{10,... | collective-permute-start | bytes 196616 | tf_op jit(solution)/shard_map/residual3/ppermute | solution.py:29
  45.5 2.1 %collective-permute-start.18 = (bf16[64,512]{1,0:T(8,128)(2,1)S(1)}, bf16[64,512]{1,0:T(8,128)(2,1)S(1)}, u32[]{:S(2)}, u32[]{:S(2)}) collective-permute-start(bf16[64,512]{1,0:T(8,128)(2,1)S(1)} %fusion.26), channel_id=1, source_target_pairs={{0,2},{1,3},{2,0},{3,1},{4,6},{5,7},{6,4},{7,5},{8,10},{9,11},{10,... | collective-permute-start | bytes 196616 | tf_op jit(solution)/shard_map/residual1/ppermute | solution.py:29
  47.6 0.1 convert_add_fusion
  47.7 2.4 %collective-permute-done.20 = bf16[64,512]{1,0:T(8,128)(2,1)S(1)} collective-permute-done((bf16[64,512]{1,0:T(8,128)(2,1)S(1)}, bf16[64,512]{1,0:T(8,128)(2,1)S(1)}, u32[]{:S(2)}, u32[]{:S(2)}) %collective-permute-start.20) | collective-permute-done | bytes 65568 | tf_op jit(solution)/shard_map/residual3/ppermute | solution.py:29
  50.1 1.6 %collective-permute-done.19 = bf16[64,512]{1,0:T(8,128)(2,1)S(1)} collective-permute-done((bf16[64,512]{1,0:T(8,128)(2,1)S(1)}, bf16[64,512]{1,0:T(8,128)(2,1)S(1)}, u32[]{:S(2)}, u32[]{:S(2)}) %collective-permute-start.19) | collective-permute-done | bytes 65568 | tf_op jit(solution)/shard_map/residual2/ppermute | solution.py:29
  51.8 0.3 fusion.33
  52.1 1.2 %collective-permute-done.23 = bf16[256,512]{1,0:T(8,128)(2,1)S(1)} collective-permute-done((bf16[256,512]{1,0:T(8,128)(2,1)S(1)}, bf16[256,512]{1,0:T(8,128)(2,1)S(1)}, u32[]{:S(2)}, u32[]{:S(2)}) %collective-permute-start.23) | collective-permute-done | bytes 262176 | tf_op jit(solution)/shard_map/residual_core/ppermute | solution.py:24
  53.3 0.2 fusion.40
  53.6 1.1 %fusion.4 = f32[256,512]{1,0:T(8,128)} fusion(f32[256,512]{1,0:T(8,128)S(1)} %get-tuple-element.64, f32[256,512]{1,0:T(8,128)S(1)} %fusion.40, bf16[256,512]{1,0:T(8,128)(2,1)S(1)} %constant_dynamic-update-slice_fusion.4, f32[256,512]{1,0:T(8,128)S(1)} %get-tuple-element.40, f32[256,512]{1,0:T(8,128)S(1)} %get-tuple-element.39, f32[256]{0:T(256)S(1)} %add_divide_fusion, ...), kind=kOutput, calls=%fused_computation.5 | convolution fusion | flops 68812800 | bytes 3015680 | tf_op jit(solution)/shard_map/dot_general | solution.py:118
  (56 shorter events, 1.1 us)
Async XLA Ops:
  0.6 6.9 %copy-start.2 = (f32[256,512]{1,0:T(8,128)S(1)}, f32[256,512]{1,0:T(8,128)}, u32[]{:S(2)}) copy-start(f32[256,512]{1,0:T(8,128)} %param.8) | copy-start | bytes 1572868
  0.6 6.9 %copy-start.3 = (f32[256,512]{1,0:T(8,128)S(1)}, f32[256,512]{1,0:T(8,128)}, u32[]{:S(2)}) copy-start(f32[256,512]{1,0:T(8,128)} %param.7) | copy-start | bytes 1572868
  1.7 8.6 %collective-permute-start = (bf16[2,64,256]{2,1,0:T(8,128)(2,1)S(1)}, bf16[2,64,256]{2,1,0:T(8,128)(2,1)S(1)}, u32[]{:S(2)}, u32[]{:S(2)}) collective-permute-start(bf16[2,64,256]{2,1,0:T(8,128)(2,1)S(1)} %pad_maximum_fusion.2), channel_id=1, source_target_pairs={{0,6},{1,7},{2,4},{3,5},{4,2},{5,3},{6,0},{7,1},{8,14},{9,15},{10,... | collective-permute-start | bytes 196616 | tf_op jit(solution)/shard_map/cells3/ppermute | solution.py:29
  6.8 8.2 %collective-permute-start.1 = (bf16[2,64,256]{2,1,0:T(8,128)(2,1)S(1)}, bf16[2,64,256]{2,1,0:T(8,128)(2,1)S(1)}, u32[]{:S(2)}, u32[]{:S(2)}) collective-permute-start(bf16[2,64,256]{2,1,0:T(8,128)(2,1)S(1)} %pad_maximum_fusion.3), channel_id=1, source_target_pairs={{0,4},{1,5},{2,6},{3,7},{4,0},{5,1},{6,2},{7,3},{8,12},{9,13},{10,... | collective-permute-start | bytes 196616 | tf_op jit(solution)/shard_map/cells2/ppermute | solution.py:29
  6.9 8.5 %collective-permute-start.3 = (bf16[2,64,256]{2,1,0:T(8,128)(2,1)S(1)}, bf16[2,64,256]{2,1,0:T(8,128)(2,1)S(1)}, u32[]{:S(2)}, u32[]{:S(2)}) collective-permute-start(bf16[2,64,256]{2,1,0:T(8,128)(2,1)S(1)} %pad_maximum_fusion.4), channel_id=1, source_target_pairs={{0,2},{1,3},{2,0},{3,1},{4,6},{5,7},{6,4},{7,5},{8,10},{9,11},{10,... | collective-permute-start | bytes 196616 | tf_op jit(solution)/shard_map/cells1/ppermute | solution.py:29
  7.7 8.9 %collective-permute-start.4 = (bf16[256,512]{1,0:T(8,128)(2,1)S(1)}, bf16[256,512]{1,0:T(8,128)(2,1)S(1)}, u32[]{:S(2)}, u32[]{:S(2)}) collective-permute-start(bf16[256,512]{1,0:T(8,128)(2,1)S(1)} %get-tuple-element.43), channel_id=1, source_target_pairs={{0,8},{1,17},{2,10},{3,19},{4,12},{5,21},{6,14},{7,23},{8,0},{9,25... | collective-permute-start | bytes 786440 | tf_op jit(solution)/shard_map/squares0/ppermute | solution.py:37
  9.5 1.5 %collective-permute-start.2 = (bf16[256,512]{1,0:T(8,128)(2,1)S(1)}, bf16[256,512]{1,0:T(8,128)(2,1)S(1)}, u32[]{:S(2)}, u32[]{:S(2)}) collective-permute-start(bf16[256,512]{1,0:T(8,128)(2,1)S(1)} %get-tuple-element.46), channel_id=1, source_target_pairs={{0,1},{1,0},{2,3},{3,2},{4,5},{5,4},{6,7},{7,6},{8,9},{9,8},{10,11... | collective-permute-start | bytes 786440 | tf_op jit(solution)/shard_map/coef_core/ppermute | solution.py:24
  9.5 0.8 %copy-start.4 = (bf16[64,512]{1,0:T(8,128)(2,1)S(1)}, bf16[64,512]{1,0:T(8,128)(2,1)}, u32[]{:S(2)}) copy-start(bf16[64,512]{1,0:T(8,128)(2,1)} %param.6) | copy-start | bytes 196612
  11.3 7.9 %collective-permute-start.5 = (bf16[64,512]{1,0:T(8,128)(2,1)S(1)}, bf16[64,512]{1,0:T(8,128)(2,1)S(1)}, u32[]{:S(2)}, u32[]{:S(2)}) collective-permute-start(bf16[64,512]{1,0:T(8,128)(2,1)S(1)} %fusion.14), channel_id=1, source_target_pairs={{0,6},{1,7},{2,4},{3,5},{4,2},{5,3},{6,0},{7,1},{8,14},{9,15},{10,... | collective-permute-start | bytes 196616 | tf_op jit(solution)/shard_map/fit3/ppermute | solution.py:29
  15.3 5.9 %collective-permute-start.6 = (bf16[64,512]{1,0:T(8,128)(2,1)S(1)}, bf16[64,512]{1,0:T(8,128)(2,1)S(1)}, u32[]{:S(2)}, u32[]{:S(2)}) collective-permute-start(bf16[64,512]{1,0:T(8,128)(2,1)S(1)} %fusion.15), channel_id=1, source_target_pairs={{0,4},{1,5},{2,6},{3,7},{4,0},{5,1},{6,2},{7,3},{8,12},{9,13},{10,... | collective-permute-start | bytes 196616 | tf_op jit(solution)/shard_map/fit2/ppermute | solution.py:29
  15.8 5.5 %collective-permute-start.7 = (bf16[64,512]{1,0:T(8,128)(2,1)S(1)}, bf16[64,512]{1,0:T(8,128)(2,1)S(1)}, u32[]{:S(2)}, u32[]{:S(2)}) collective-permute-start(bf16[64,512]{1,0:T(8,128)(2,1)S(1)} %fusion.16), channel_id=1, source_target_pairs={{0,2},{1,3},{2,0},{3,1},{4,6},{5,7},{6,4},{7,5},{8,10},{9,11},{10,... | collective-permute-start | bytes 196616 | tf_op jit(solution)/shard_map/fit1/ppermute | solution.py:29
  16.7 0.7 %copy-start.5 = (f32[256]{0:T(256)S(1)}, f32[256]{0:T(256)}, u32[]{:S(2)}) copy-start(f32[256]{0:T(256)} %param.9) | copy-start | bytes 3076
  17.5 8.5 %collective-permute-start.12 = (bf16[256,256]{1,0:T(8,128)(2,1)S(1)}, bf16[256,256]{1,0:T(8,128)(2,1)S(1)}, u32[]{:S(2)}, u32[]{:S(2)}) collective-permute-start(bf16[256,256]{1,0:T(8,128)(2,1)S(1)} %pad_maximum_fusion), channel_id=1, source_target_pairs={{0,1},{1,0},{2,3},{3,2},{4,5},{5,4},{6,7},{7,6},{8,9},{9,8},{10,11... | collective-permute-start | bytes 393224 | tf_op jit(solution)/shard_map/cells_core/ppermute | solution.py:24
  17.6 8.4 %collective-permute-start.11 = (bf16[256,512]{1,0:T(8,128)(2,1)S(1)}, bf16[256,512]{1,0:T(8,128)(2,1)S(1)}, u32[]{:S(2)}, u32[]{:S(2)}) collective-permute-start(bf16[256,512]{1,0:T(8,128)(2,1)S(1)} %convert_element_type.86), channel_id=1, source_target_pairs={{0,16},{1,9},{2,18},{3,11},{4,20},{5,13},{6,22},{7,15},{8,24},{9,1... | collective-permute-start | bytes 786440 | tf_op jit(solution)/shard_map/squares1/ppermute | solution.py:37
  21.5 6.6 %collective-permute-start.10 = (bf16[64,512]{1,0:T(8,128)(2,1)S(1)}, bf16[64,512]{1,0:T(8,128)(2,1)S(1)}, u32[]{:S(2)}, u32[]{:S(2)}) collective-permute-start(bf16[64,512]{1,0:T(8,128)(2,1)S(1)} %fusion.17), channel_id=1, source_target_pairs={{0,6},{1,7},{2,4},{3,5},{4,2},{5,3},{6,0},{7,1},{8,14},{9,15},{10,... | collective-permute-start | bytes 196616 | tf_op jit(solution)/shard_map/residual3/ppermute | solution.py:29
  23.7 5.8 %collective-permute-start.9 = (bf16[64,512]{1,0:T(8,128)(2,1)S(1)}, bf16[64,512]{1,0:T(8,128)(2,1)S(1)}, u32[]{:S(2)}, u32[]{:S(2)}) collective-permute-start(bf16[64,512]{1,0:T(8,128)(2,1)S(1)} %fusion.17), channel_id=1, source_target_pairs={{0,4},{1,5},{2,6},{3,7},{4,0},{5,1},{6,2},{7,3},{8,12},{9,13},{10,... | collective-permute-start | bytes 196616 | tf_op jit(solution)/shard_map/residual2/ppermute | solution.py:29
  23.7 5.8 %collective-permute-start.8 = (bf16[64,512]{1,0:T(8,128)(2,1)S(1)}, bf16[64,512]{1,0:T(8,128)(2,1)S(1)}, u32[]{:S(2)}, u32[]{:S(2)}) collective-permute-start(bf16[64,512]{1,0:T(8,128)(2,1)S(1)} %fusion.17), channel_id=1, source_target_pairs={{0,2},{1,3},{2,0},{3,1},{4,6},{5,7},{6,4},{7,5},{8,10},{9,11},{10,... | collective-permute-start | bytes 196616 | tf_op jit(solution)/shard_map/residual1/ppermute | solution.py:29
  29.6 1.6 %collective-permute-start.13 = (bf16[256,512]{1,0:T(8,128)(2,1)S(1)}, bf16[256,512]{1,0:T(8,128)(2,1)S(1)}, u32[]{:S(2)}, u32[]{:S(2)}) collective-permute-start(bf16[256,512]{1,0:T(8,128)(2,1)S(1)} %constant_dynamic-update-slice_fusion), channel_id=1, source_target_pairs={{0,1},{1,0},{2,3},{3,2},{4,5},{5,4},{6,7},{7,6},{8,9},{9,8},{10,11... | collective-permute-start | bytes 786440 | tf_op jit(solution)/shard_map/residual_core/ppermute | solution.py:24
  32.0 1.6 %collective-permute-start.14 = (bf16[256,512]{1,0:T(8,128)(2,1)S(1)}, bf16[256,512]{1,0:T(8,128)(2,1)S(1)}, u32[]{:S(2)}, u32[]{:S(2)}) collective-permute-start(bf16[256,512]{1,0:T(8,128)(2,1)S(1)} %get-tuple-element.45), channel_id=1, source_target_pairs={{0,1},{1,0},{2,3},{3,2},{4,5},{5,4},{6,7},{7,6},{8,9},{9,8},{10,11... | collective-permute-start | bytes 786440 | tf_op jit(solution)/shard_map/coef_core/ppermute | solution.py:24
  32.2 6.4 %collective-permute-start.21 = (bf16[256,512]{1,0:T(8,128)(2,1)S(1)}, bf16[256,512]{1,0:T(8,128)(2,1)S(1)}, u32[]{:S(2)}, u32[]{:S(2)}) collective-permute-start(bf16[256,512]{1,0:T(8,128)(2,1)S(1)} %get-tuple-element.41), channel_id=1, source_target_pairs={{0,8},{1,17},{2,10},{3,19},{4,12},{5,21},{6,14},{7,23},{8,0},{9,25... | collective-permute-start | bytes 786440 | tf_op jit(solution)/shard_map/squares0/ppermute | solution.py:37
  33.9 6.8 %collective-permute-start.15 = (bf16[64,512]{1,0:T(8,128)(2,1)S(1)}, bf16[64,512]{1,0:T(8,128)(2,1)S(1)}, u32[]{:S(2)}, u32[]{:S(2)}) collective-permute-start(bf16[64,512]{1,0:T(8,128)(2,1)S(1)} %get-tuple-element.47), channel_id=1, source_target_pairs={{0,6},{1,7},{2,4},{3,5},{4,2},{5,3},{6,0},{7,1},{8,14},{9,15},{10,... | collective-permute-start | bytes 196616 | tf_op jit(solution)/shard_map/fit3/ppermute | solution.py:29
  36.4 6.5 %collective-permute-start.17 = (bf16[64,512]{1,0:T(8,128)(2,1)S(1)}, bf16[64,512]{1,0:T(8,128)(2,1)S(1)}, u32[]{:S(2)}, u32[]{:S(2)}) collective-permute-start(bf16[64,512]{1,0:T(8,128)(2,1)S(1)} %get-tuple-element.48), channel_id=1, source_target_pairs={{0,2},{1,3},{2,0},{3,1},{4,6},{5,7},{6,4},{7,5},{8,10},{9,11},{10,... | collective-permute-start | bytes 196616 | tf_op jit(solution)/shard_map/fit1/ppermute | solution.py:29
  36.4 6.7 %collective-permute-start.16 = (bf16[64,512]{1,0:T(8,128)(2,1)S(1)}, bf16[64,512]{1,0:T(8,128)(2,1)S(1)}, u32[]{:S(2)}, u32[]{:S(2)}) collective-permute-start(bf16[64,512]{1,0:T(8,128)(2,1)S(1)} %get-tuple-element.49), channel_id=1, source_target_pairs={{0,4},{1,5},{2,6},{3,7},{4,0},{5,1},{6,2},{7,3},{8,12},{9,13},{10,... | collective-permute-start | bytes 196616 | tf_op jit(solution)/shard_map/fit2/ppermute | solution.py:29
  38.6 9.0 %collective-permute-start.22 = (bf16[256,512]{1,0:T(8,128)(2,1)S(1)}, bf16[256,512]{1,0:T(8,128)(2,1)S(1)}, u32[]{:S(2)}, u32[]{:S(2)}) collective-permute-start(bf16[256,512]{1,0:T(8,128)(2,1)S(1)} %fusion.22), channel_id=1, source_target_pairs={{0,16},{1,9},{2,18},{3,11},{4,20},{5,13},{6,22},{7,15},{8,24},{9,1... | collective-permute-start | bytes 786440 | tf_op jit(solution)/shard_map/squares1/ppermute | solution.py:37
  43.2 6.9 %collective-permute-start.20 = (bf16[64,512]{1,0:T(8,128)(2,1)S(1)}, bf16[64,512]{1,0:T(8,128)(2,1)S(1)}, u32[]{:S(2)}, u32[]{:S(2)}) collective-permute-start(bf16[64,512]{1,0:T(8,128)(2,1)S(1)} %fusion.26), channel_id=1, source_target_pairs={{0,6},{1,7},{2,4},{3,5},{4,2},{5,3},{6,0},{7,1},{8,14},{9,15},{10,... | collective-permute-start | bytes 196616 | tf_op jit(solution)/shard_map/residual3/ppermute | solution.py:29
  45.5 6.1 %collective-permute-start.19 = (bf16[64,512]{1,0:T(8,128)(2,1)S(1)}, bf16[64,512]{1,0:T(8,128)(2,1)S(1)}, u32[]{:S(2)}, u32[]{:S(2)}) collective-permute-start(bf16[64,512]{1,0:T(8,128)(2,1)S(1)} %fusion.26), channel_id=1, source_target_pairs={{0,4},{1,5},{2,6},{3,7},{4,0},{5,1},{6,2},{7,3},{8,12},{9,13},{10,... | collective-permute-start | bytes 196616 | tf_op jit(solution)/shard_map/residual2/ppermute | solution.py:29
  45.5 6.1 %collective-permute-start.18 = (bf16[64,512]{1,0:T(8,128)(2,1)S(1)}, bf16[64,512]{1,0:T(8,128)(2,1)S(1)}, u32[]{:S(2)}, u32[]{:S(2)}) collective-permute-start(bf16[64,512]{1,0:T(8,128)(2,1)S(1)} %fusion.26), channel_id=1, source_target_pairs={{0,2},{1,3},{2,0},{3,1},{4,6},{5,7},{6,4},{7,5},{8,10},{9,11},{10,... | collective-permute-start | bytes 196616 | tf_op jit(solution)/shard_map/residual1/ppermute | solution.py:29
  51.7 1.6 %collective-permute-start.23 = (bf16[256,512]{1,0:T(8,128)(2,1)S(1)}, bf16[256,512]{1,0:T(8,128)(2,1)S(1)}, u32[]{:S(2)}, u32[]{:S(2)}) collective-permute-start(bf16[256,512]{1,0:T(8,128)(2,1)S(1)} %constant_dynamic-update-slice_fusion.4), channel_id=1, source_target_pairs={{0,1},{1,0},{2,3},{3,2},{4,5},{5,4},{6,7},{7,6},{8,9},{9,8},{10,11... | collective-permute-start | bytes 786440 | tf_op jit(solution)/shard_map/residual_core/ppermute | solution.py:24
  52.1 2.6 %copy-start = (f32[256,512]{1,0:T(8,128)}, f32[256,512]{1,0:T(8,128)S(1)}, u32[]{:S(2)}) copy-start(f32[256,512]{1,0:T(8,128)S(1)} %get-tuple-element.39) | copy-start | bytes 1572868
  52.1 2.6 %copy-start.1 = (f32[256,512]{1,0:T(8,128)}, f32[256,512]{1,0:T(8,128)S(1)}, u32[]{:S(2)}) copy-start(f32[256,512]{1,0:T(8,128)S(1)} %get-tuple-element.40) | copy-start | bytes 1572868

commit v5 on v4

--- a/solution.py
+++ b/solution.py
@@ -50,6 +50,8 @@
     me = lax.axis_index("shard")
     chip, core = me // 2, me % 2
     far_first = list(reversed(range(1, chips)))
+    order = [0] + far_first
+    evens_first = sorted(range(chips), key=lambda k: (k > 0, k % 2, k))
     contract = (((0,), (0,)), ((), ()))
 
     def dot(x, c):
@@ -59,7 +61,7 @@
         start = ((chip ^ k) * 2 + (core ^ side)) * mine
         return lax.dynamic_slice_in_dim(expression, start, mine, 1)
 
-    coef_copy = coef_init.astype(bf16)
+    (coef_copy,) = together(coef_init.astype(bf16))
     coef_other = core_swap(coef_copy, "coef_core")
     pairs = [jnp.stack([columns(k, 0), columns(k, 1)]) for k in range(chips)]
     for k in far_first:
@@ -78,7 +80,6 @@
             pairs[k], *_ = together(pairs[k], *before)
         leaving[k] = fit(k).astype(bf16)
         before = (leaving[k],)
-    order = [0] + far_first
     own = jnp.concatenate([pairs[k][0] for k in order])
     other = jnp.concatenate([pairs[k][1] for k in order])
 
@@ -89,14 +90,14 @@
         squares = merged * merged
         if cond_bits > 0:
             squares = squares + cond_swap(squares.astype(bf16), 1, "squares0").astype(f32)
-        if step > 0:
+        if step == 0:
+            held, squares, weights, response_rows, *_ = together(other, squares, weights, response_rows, *before)
+        else:
             coef_copy = coef.astype(bf16)
             coef_other = core_swap(coef_copy, "coef_core")
             fitted = (dot(own, coef_copy) + dot(other, coef_other)).reshape(chips, cells, targets)
             total = fitted[0]
             leaving = {k: fitted[order.index(k)].astype(bf16) for k in far_first}
-        else:
-            held, squares, weights, response_rows, *_ = together(other, squares, weights, response_rows, *before)
         arrived = [chip_swap(leaving[k], k, f"fit{k}") for k in far_first]
         for bit in range(1, cond_bits):
             squares = squares + cond_swap(squares.astype(bf16), 1 << bit, f"squares{bit}").astype(f32)
@@ -110,9 +111,8 @@
             across = core_swap(held, "cells_core")
             diagonal = jnp.sum(jnp.square(own.astype(f32)), 0) + jnp.sum(jnp.square(across.astype(f32)), 0)
             step_size = 1.0 / (diagonal / n_cells + rho_weight)[:, None]
-            residual, squares, step_size, across = together(residual, squares, step_size, across)
-        else:
-            residual, squares = together(residual, squares)
+        squares, step_size, across, *ready = together(squares, step_size, across, *[residual[k] for k in evens_first])
+        residual = dict(zip(evens_first, ready))
         residual = jnp.concatenate([residual[k] for k in order])
         residual_other = core_swap(residual, "residual_core")
         product = lax.dot_general(own, residual, contract, preferred_element_type=f32) + lax.dot_general(

time: 54.9 us -> 53.7 us (0.978)
  waiting for transfers between devices: 16.2 us -> 14.3 us
  starting transfers between devices: 30.1 us -> 30.8 us
    ppermute x5, waiting for transfers between devices: 3.6 us -> 2.77 us  [core_swap(): lax.ppermute(value, 'shard', [(i, i ^ 1) for i in range(lax.axis_size('sh...]
    ppermute x15, waiting for transfers between devices: 12.3 us -> 11.5 us  [chip_swap(): lax.ppermute(value, 'shard', [(i, i ^ 2 * mask) for i in range(lax.axis_s...]
  transfers between devices with their start and end apart: 24 -> 24, of which waited for: 13 -> 11; matrix products, arithmetic and copies ran while one was open for 5% -> 5% of each run, Pallas kernels for 0% -> 0%
where the time goes in v5:
time: 53.7 us; the launch traced here: 53.5 us
  starting transfers between devices  30.8 us (57%)
  waiting for transfers between devices  14.3 us (27%)
  matrix products  3.9 us (7%)
  local copies, waits for them, and re-layouts  2.51 us (5%)
  between operations  1.09 us (2%)
  other arithmetic  0.94 us (2%)
    ppermute x15, starting transfers between devices, chip_swap(): lax.ppermute(value, 'shard', [(i, i ^ 2 * mask) for i in range(lax.axis_s...  24.3 us
    ppermute x15, waiting for transfers between devices, chip_swap(): lax.ppermute(value, 'shard', [(i, i ^ 2 * mask) for i in range(lax.axis_s...  11.5 us
    ppermute x4, starting transfers between devices, cond_swap(): return lax.ppermute(value, ('cond', 'shard'), pairs)  6.01 us
    ppermute x5, waiting for transfers between devices, core_swap(): lax.ppermute(value, 'shard', [(i, i ^ 1) for i in range(lax.axis_size('sh...  2.77 us
    dot_general x10, matrix products, dot(): return jnp.dot(x, c, preferred_element_type=f32)  1.75 us
    dot_general x2, matrix products, shards(): lax.dot_general(own, residual, contract, preferred_element_type=f32)  1.66 us
    unnamed x18, local copies, waits for them, and re-layouts  1.39 us
  transfers between devices with their start and end apart: 24, of which 11 were waited for; matrix products, arithmetic and copies ran while one was open for 5% of the time, Pallas kernels for 0%

profile of v5, /device:TPU:0, one launch (start us, length us, event | category | flops | bytes accessed | tf_op | source)
XLA Modules:
  0.0 53.5 jit_solution(14937884462513310038)
XLA Ops:
  0.7 1.0 %constant_dynamic-slice_fusion = (bf16[64,256]{1,0:T(8,128)(2,1)S(1)}, bf16[1,64,256]{2,1,0:T(8,128)(2,1)S(1)}, bf16[1,64,256]{2,1,0:T(8,128)(2,1)S(1)}, bf16[1,...) fusion(bf16[64,2048]{1,0:T(8,128)(2,1)} %param.5, ...), kind=kLoop, calls=%fused_computation.72 | loop fusion | bytes 524320 | tf_op jit(solution)/shard_map/dynamic_slice | solution.py:62
  1.7 5.1 %collective-permute-start = (bf16[2,64,256]{2,1,0:T(8,128)(2,1)S(1)}, bf16[2,64,256]{2,1,0:T(8,128)(2,1)S(1)}, u32[]{:S(2)}, u32[]{:S(2)}) collective-permute-start(bf16[2,64,256]{2,1,0:T(8,128)(2,1)S(1)} %pad_maximum_fusion.2), channel_id=1, source_target_pairs={{0,6},{1,7},{2,4},{3,5},{4,2},{5,3},{6,0},{7,1},{8,14},{9,15},{10,... | collective-permute-start | bytes 196616 | tf_op jit(solution)/shard_map/cells3/ppermute | solution.py:29
  6.9 0.6 %collective-permute-start.3 = (bf16[2,64,256]{2,1,0:T(8,128)(2,1)S(1)}, bf16[2,64,256]{2,1,0:T(8,128)(2,1)S(1)}, u32[]{:S(2)}, u32[]{:S(2)}) collective-permute-start(bf16[2,64,256]{2,1,0:T(8,128)(2,1)S(1)} %pad_maximum_fusion.4), channel_id=1, source_target_pairs={{0,2},{1,3},{2,0},{3,1},{4,6},{5,7},{6,4},{7,5},{8,10},{9,11},{10,... | collective-permute-start | bytes 196616 | tf_op jit(solution)/shard_map/cells1/ppermute | solution.py:29
  7.6 0.1 multiply_convert_fusion.1
  7.8 1.8 %collective-permute-start.4 = (bf16[256,512]{1,0:T(8,128)(2,1)S(1)}, bf16[256,512]{1,0:T(8,128)(2,1)S(1)}, u32[]{:S(2)}, u32[]{:S(2)}) collective-permute-start(bf16[256,512]{1,0:T(8,128)(2,1)S(1)} %get-tuple-element.47), channel_id=1, source_target_pairs={{0,8},{1,17},{2,10},{3,19},{4,12},{5,21},{6,14},{7,23},{8,0},{9,25... | collective-permute-start | bytes 786440 | tf_op jit(solution)/shard_map/squares0/ppermute | solution.py:37
  9.5 0.2 fusion.38
  9.7 0.7 %copy-done.4 = bf16[64,512]{1,0:T(8,128)(2,1)S(1)} copy-done((bf16[64,512]{1,0:T(8,128)(2,1)S(1)}, bf16[64,512]{1,0:T(8,128)(2,1)}, u32[]{:S(2)}) %copy-start.4) | copy-done | bytes 65560
  10.4 0.2 fusion.31
  10.6 0.2 fusion.14
  10.8 3.7 %collective-permute-start.7 = (bf16[64,512]{1,0:T(8,128)(2,1)S(1)}, bf16[64,512]{1,0:T(8,128)(2,1)S(1)}, u32[]{:S(2)}, u32[]{:S(2)}) collective-permute-start(bf16[64,512]{1,0:T(8,128)(2,1)S(1)} %fusion.14), channel_id=1, source_target_pairs={{0,6},{1,7},{2,4},{3,5},{4,2},{5,3},{6,0},{7,1},{8,14},{9,15},{10,... | collective-permute-start | bytes 196616 | tf_op jit(solution)/shard_map/fit3/ppermute | solution.py:29
  14.4 0.2 fusion.29
  14.6 0.2 fusion.15
  14.9 0.2 fusion.30
  15.0 0.2 fusion.16
  15.2 1.3 %collective-permute-start.9 = (bf16[64,512]{1,0:T(8,128)(2,1)S(1)}, bf16[64,512]{1,0:T(8,128)(2,1)S(1)}, u32[]{:S(2)}, u32[]{:S(2)}) collective-permute-start(bf16[64,512]{1,0:T(8,128)(2,1)S(1)} %fusion.16), channel_id=1, source_target_pairs={{0,2},{1,3},{2,0},{3,1},{4,6},{5,7},{6,4},{7,5},{8,10},{9,11},{10,... | collective-permute-start | bytes 196616 | tf_op jit(solution)/shard_map/fit1/ppermute | solution.py:29
  16.7 0.7 %copy-done.5 = f32[256]{0:T(256)S(1)} copy-done((f32[256]{0:T(256)S(1)}, f32[256]{0:T(256)}, u32[]{:S(2)}) %copy-start.5) | copy-done | bytes 1048
  17.3 0.1 broadcast_in_dim.2
  17.5 1.6 %collective-permute-start.5 = (bf16[256,512]{1,0:T(8,128)(2,1)S(1)}, bf16[256,512]{1,0:T(8,128)(2,1)S(1)}, u32[]{:S(2)}, u32[]{:S(2)}) collective-permute-start(bf16[256,512]{1,0:T(8,128)(2,1)S(1)} %convert_element_type.82), channel_id=1, source_target_pairs={{0,16},{1,9},{2,18},{3,11},{4,20},{5,13},{6,22},{7,15},{8,24},{9,1... | collective-permute-start | bytes 786440 | tf_op jit(solution)/shard_map/squares1/ppermute | solution.py:37
  19.2 1.6 %collective-permute-done.9 = bf16[64,512]{1,0:T(8,128)(2,1)S(1)} collective-permute-done((bf16[64,512]{1,0:T(8,128)(2,1)S(1)}, bf16[64,512]{1,0:T(8,128)(2,1)S(1)}, u32[]{:S(2)}, u32[]{:S(2)}) %collective-permute-start.9) | collective-permute-done | bytes 65568 | tf_op jit(solution)/shard_map/fit1/ppermute | solution.py:29
  20.8 0.2 fusion.17
  21.0 2.3 %collective-permute-start.12 = (bf16[64,512]{1,0:T(8,128)(2,1)S(1)}, bf16[64,512]{1,0:T(8,128)(2,1)S(1)}, u32[]{:S(2)}, u32[]{:S(2)}) collective-permute-start(bf16[64,512]{1,0:T(8,128)(2,1)S(1)} %fusion.17), channel_id=1, source_target_pairs={{0,6},{1,7},{2,4},{3,5},{4,2},{5,3},{6,0},{7,1},{8,14},{9,15},{10,... | collective-permute-start | bytes 196616 | tf_op jit(solution)/shard_map/residual3/ppermute | solution.py:29
  23.2 2.2 %collective-permute-start.10 = (bf16[64,512]{1,0:T(8,128)(2,1)S(1)}, bf16[64,512]{1,0:T(8,128)(2,1)S(1)}, u32[]{:S(2)}, u32[]{:S(2)}) collective-permute-start(bf16[64,512]{1,0:T(8,128)(2,1)S(1)} %fusion.17), channel_id=1, source_target_pairs={{0,4},{1,5},{2,6},{3,7},{4,0},{5,1},{6,2},{7,3},{8,12},{9,13},{10,... | collective-permute-start | bytes 196616 | tf_op jit(solution)/shard_map/residual2/ppermute | solution.py:29
  25.5 0.1 convert_add_fusion.2
  25.6 2.1 %collective-permute-done.12 = bf16[64,512]{1,0:T(8,128)(2,1)S(1)} collective-permute-done((bf16[64,512]{1,0:T(8,128)(2,1)S(1)}, bf16[64,512]{1,0:T(8,128)(2,1)S(1)}, u32[]{:S(2)}, u32[]{:S(2)}) %collective-permute-start.12) | collective-permute-done | bytes 65568 | tf_op jit(solution)/shard_map/residual3/ppermute | solution.py:29
  27.6 0.4 collective-permute-done.11
  28.0 0.9 %collective-permute-done.10 = bf16[64,512]{1,0:T(8,128)(2,1)S(1)} collective-permute-done((bf16[64,512]{1,0:T(8,128)(2,1)S(1)}, bf16[64,512]{1,0:T(8,128)(2,1)S(1)}, u32[]{:S(2)}, u32[]{:S(2)}) %collective-permute-start.10) | collective-permute-done | bytes 65568 | tf_op jit(solution)/shard_map/residual2/ppermute | solution.py:29
  29.1 1.5 %collective-permute-done.13 = bf16[256,512]{1,0:T(8,128)(2,1)S(1)} collective-permute-done((bf16[256,512]{1,0:T(8,128)(2,1)S(1)}, bf16[256,512]{1,0:T(8,128)(2,1)S(1)}, u32[]{:S(2)}, u32[]{:S(2)}) %collective-permute-start.13) | collective-permute-done | bytes 262176 | tf_op jit(solution)/shard_map/residual_core/ppermute | solution.py:24
  30.6 0.2 fusion.39
  30.8 0.6 %multiply_convert_fusion = (bf16[256,512]{1,0:T(8,128)(2,1)S(1)}, f32[256,512]{1,0:T(8,128)S(1)}, bf16[256,512]{1,0:T(8,128)(2,1)S(1)}, f32[256,512]{1,0:T(8,128)S(1)}) fusion(f32[256,512]{1,0:T(8,128)S(1)} %get-tuple-element.48, f32[256,512]{1,0:T(8,128)S(1)} %broadcast_in_dim.2, f32[256,512]{1,0:T(8,128)S(1)} %convert_add_fusion.2, ...), kind=kOutput, calls=%fused_computation.35 | convolution fusion | flops 69992448 | bytes 4588544 | tf_op jit(solution)/shard_map/dot_general | solution.py:118
  31.4 0.2 collective-permute-start.16
  31.6 1.7 %collective-permute-start.14 = (bf16[256,512]{1,0:T(8,128)(2,1)S(1)}, bf16[256,512]{1,0:T(8,128)(2,1)S(1)}, u32[]{:S(2)}, u32[]{:S(2)}) collective-permute-start(bf16[256,512]{1,0:T(8,128)(2,1)S(1)} %get-tuple-element.45), channel_id=1, source_target_pairs={{0,8},{1,17},{2,10},{3,19},{4,12},{5,21},{6,14},{7,23},{8,0},{9,25... | collective-permute-start | bytes 786440 | tf_op jit(solution)/shard_map/squares0/ppermute | solution.py:37
  33.3 0.2 fusion.32
  33.5 0.2 fusion.37
  33.8 2.6 %collective-permute-start.17 = (bf16[64,512]{1,0:T(8,128)(2,1)S(1)}, bf16[64,512]{1,0:T(8,128)(2,1)S(1)}, u32[]{:S(2)}, u32[]{:S(2)}) collective-permute-start(bf16[64,512]{1,0:T(8,128)(2,1)S(1)} %get-tuple-element.51), channel_id=1, source_target_pairs={{0,6},{1,7},{2,4},{3,5},{4,2},{5,3},{6,0},{7,1},{8,14},{9,15},{10,... | collective-permute-start | bytes 196616 | tf_op jit(solution)/shard_map/fit3/ppermute | solution.py:29
  36.4 1.9 %collective-permute-start.18 = (bf16[64,512]{1,0:T(8,128)(2,1)S(1)}, bf16[64,512]{1,0:T(8,128)(2,1)S(1)}, u32[]{:S(2)}, u32[]{:S(2)}) collective-permute-start(bf16[64,512]{1,0:T(8,128)(2,1)S(1)} %get-tuple-element.53), channel_id=1, source_target_pairs={{0,4},{1,5},{2,6},{3,7},{4,0},{5,1},{6,2},{7,3},{8,12},{9,13},{10,... | collective-permute-start | bytes 196616 | tf_op jit(solution)/shard_map/fit2/ppermute | solution.py:29
  38.3 1.0 %collective-permute-start.15 = (bf16[256,512]{1,0:T(8,128)(2,1)S(1)}, bf16[256,512]{1,0:T(8,128)(2,1)S(1)}, u32[]{:S(2)}, u32[]{:S(2)}) collective-permute-start(bf16[256,512]{1,0:T(8,128)(2,1)S(1)} %fusion.22), channel_id=1, source_target_pairs={{0,16},{1,9},{2,18},{3,11},{4,20},{5,13},{6,22},{7,15},{8,24},{9,1... | collective-permute-start | bytes 786440 | tf_op jit(solution)/shard_map/squares1/ppermute | solution.py:37
  39.3 0.8 %collective-permute-done.17 = bf16[64,512]{1,0:T(8,128)(2,1)S(1)} collective-permute-done((bf16[64,512]{1,0:T(8,128)(2,1)S(1)}, bf16[64,512]{1,0:T(8,128)(2,1)S(1)}, u32[]{:S(2)}, u32[]{:S(2)}) %collective-permute-start.17) | collective-permute-done | bytes 65568 | tf_op jit(solution)/shard_map/fit3/ppermute | solution.py:29
  40.1 1.7 %collective-permute-done.19 = bf16[64,512]{1,0:T(8,128)(2,1)S(1)} collective-permute-done((bf16[64,512]{1,0:T(8,128)(2,1)S(1)}, bf16[64,512]{1,0:T(8,128)(2,1)S(1)}, u32[]{:S(2)}, u32[]{:S(2)}) %collective-permute-start.19) | collective-permute-done | bytes 65568 | tf_op jit(solution)/shard_map/fit1/ppermute | solution.py:29
  41.7 0.6 %collective-permute-done.18 = bf16[64,512]{1,0:T(8,128)(2,1)S(1)} collective-permute-done((bf16[64,512]{1,0:T(8,128)(2,1)S(1)}, bf16[64,512]{1,0:T(8,128)(2,1)S(1)}, u32[]{:S(2)}, u32[]{:S(2)}) %collective-permute-start.18) | collective-permute-done | bytes 65568 | tf_op jit(solution)/shard_map/fit2/ppermute | solution.py:29
  42.3 2.9 %collective-permute-start.22 = (bf16[64,512]{1,0:T(8,128)(2,1)S(1)}, bf16[64,512]{1,0:T(8,128)(2,1)S(1)}, u32[]{:S(2)}, u32[]{:S(2)}) collective-permute-start(bf16[64,512]{1,0:T(8,128)(2,1)S(1)} %fusion.26), channel_id=1, source_target_pairs={{0,6},{1,7},{2,4},{3,5},{4,2},{5,3},{6,0},{7,1},{8,14},{9,15},{10,... | collective-permute-start | bytes 196616 | tf_op jit(solution)/shard_map/residual3/ppermute | solution.py:29
  45.2 1.6 %collective-permute-start.20 = (bf16[64,512]{1,0:T(8,128)(2,1)S(1)}, bf16[64,512]{1,0:T(8,128)(2,1)S(1)}, u32[]{:S(2)}, u32[]{:S(2)}) collective-permute-start(bf16[64,512]{1,0:T(8,128)(2,1)S(1)} %fusion.26), channel_id=1, source_target_pairs={{0,4},{1,5},{2,6},{3,7},{4,0},{5,1},{6,2},{7,3},{8,12},{9,13},{10,... | collective-permute-start | bytes 196616 | tf_op jit(solution)/shard_map/residual2/ppermute | solution.py:29
  46.8 0.1 convert_add_fusion
  46.9 2.1 %collective-permute-done.22 = bf16[64,512]{1,0:T(8,128)(2,1)S(1)} collective-permute-done((bf16[64,512]{1,0:T(8,128)(2,1)S(1)}, bf16[64,512]{1,0:T(8,128)(2,1)S(1)}, u32[]{:S(2)}, u32[]{:S(2)}) %collective-permute-start.22) | collective-permute-done | bytes 65568 | tf_op jit(solution)/shard_map/residual3/ppermute | solution.py:29
  49.0 1.5 %collective-permute-done.21 = bf16[64,512]{1,0:T(8,128)(2,1)S(1)} collective-permute-done((bf16[64,512]{1,0:T(8,128)(2,1)S(1)}, bf16[64,512]{1,0:T(8,128)(2,1)S(1)}, u32[]{:S(2)}, u32[]{:S(2)}) %collective-permute-start.21) | collective-permute-done | bytes 65568 | tf_op jit(solution)/shard_map/residual1/ppermute | solution.py:29
  50.6 0.3 fusion.33
  50.9 1.2 %collective-permute-done.23 = bf16[256,512]{1,0:T(8,128)(2,1)S(1)} collective-permute-done((bf16[256,512]{1,0:T(8,128)(2,1)S(1)}, bf16[256,512]{1,0:T(8,128)(2,1)S(1)}, u32[]{:S(2)}, u32[]{:S(2)}) %collective-permute-start.23) | collective-permute-done | bytes 262176 | tf_op jit(solution)/shard_map/residual_core/ppermute | solution.py:24
  52.1 0.2 fusion.40
  52.4 1.1 %fusion.4 = f32[256,512]{1,0:T(8,128)} fusion(f32[256,512]{1,0:T(8,128)S(1)} %get-tuple-element.68, f32[256,512]{1,0:T(8,128)S(1)} %fusion.40, bf16[256,512]{1,0:T(8,128)(2,1)S(1)} %constant_dynamic-update-slice_fusion.4, f32[256,512]{1,0:T(8,128)S(1)} %get-tuple-element.44, f32[256,512]{1,0:T(8,128)S(1)} %get-tuple-element.43, f32[256]{0:T(256)S(1)} %add_divide_fusion, ...), kind=kOutput, calls=%fused_computation.5 | convolution fusion | flops 68812800 | bytes 3015680 | tf_op jit(solution)/shard_map/dot_general | solution.py:118
  (56 shorter events, 1.0 us)
Async XLA Ops:
  0.6 6.9 %copy-start.2 = (f32[256,512]{1,0:T(8,128)S(1)}, f32[256,512]{1,0:T(8,128)}, u32[]{:S(2)}) copy-start(f32[256,512]{1,0:T(8,128)} %param.8) | copy-start | bytes 1572868
  0.6 6.9 %copy-start.3 = (f32[256,512]{1,0:T(8,128)S(1)}, f32[256,512]{1,0:T(8,128)}, u32[]{:S(2)}) copy-start(f32[256,512]{1,0:T(8,128)} %param.7) | copy-start | bytes 1572868
  1.7 8.7 %collective-permute-start = (bf16[2,64,256]{2,1,0:T(8,128)(2,1)S(1)}, bf16[2,64,256]{2,1,0:T(8,128)(2,1)S(1)}, u32[]{:S(2)}, u32[]{:S(2)}) collective-permute-start(bf16[2,64,256]{2,1,0:T(8,128)(2,1)S(1)} %pad_maximum_fusion.2), channel_id=1, source_target_pairs={{0,6},{1,7},{2,4},{3,5},{4,2},{5,3},{6,0},{7,1},{8,14},{9,15},{10,... | collective-permute-start | bytes 196616 | tf_op jit(solution)/shard_map/cells3/ppermute | solution.py:29
  6.8 7.6 %collective-permute-start.1 = (bf16[2,64,256]{2,1,0:T(8,128)(2,1)S(1)}, bf16[2,64,256]{2,1,0:T(8,128)(2,1)S(1)}, u32[]{:S(2)}, u32[]{:S(2)}) collective-permute-start(bf16[2,64,256]{2,1,0:T(8,128)(2,1)S(1)} %pad_maximum_fusion.3), channel_id=1, source_target_pairs={{0,4},{1,5},{2,6},{3,7},{4,0},{5,1},{6,2},{7,3},{8,12},{9,13},{10,... | collective-permute-start | bytes 196616 | tf_op jit(solution)/shard_map/cells2/ppermute | solution.py:29
  6.9 7.9 %collective-permute-start.3 = (bf16[2,64,256]{2,1,0:T(8,128)(2,1)S(1)}, bf16[2,64,256]{2,1,0:T(8,128)(2,1)S(1)}, u32[]{:S(2)}, u32[]{:S(2)}) collective-permute-start(bf16[2,64,256]{2,1,0:T(8,128)(2,1)S(1)} %pad_maximum_fusion.4), channel_id=1, source_target_pairs={{0,2},{1,3},{2,0},{3,1},{4,6},{5,7},{6,4},{7,5},{8,10},{9,11},{10,... | collective-permute-start | bytes 196616 | tf_op jit(solution)/shard_map/cells1/ppermute | solution.py:29
  7.7 2.7 %collective-permute-start.2 = (bf16[256,512]{1,0:T(8,128)(2,1)S(1)}, bf16[256,512]{1,0:T(8,128)(2,1)S(1)}, u32[]{:S(2)}, u32[]{:S(2)}) collective-permute-start(bf16[256,512]{1,0:T(8,128)(2,1)S(1)} %get-tuple-element.50), channel_id=1, source_target_pairs={{0,1},{1,0},{2,3},{3,2},{4,5},{5,4},{6,7},{7,6},{8,9},{9,8},{10,11... | collective-permute-start | bytes 786440 | tf_op jit(solution)/shard_map/coef_core/ppermute | solution.py:24
  7.8 8.8 %collective-permute-start.4 = (bf16[256,512]{1,0:T(8,128)(2,1)S(1)}, bf16[256,512]{1,0:T(8,128)(2,1)S(1)}, u32[]{:S(2)}, u32[]{:S(2)}) collective-permute-start(bf16[256,512]{1,0:T(8,128)(2,1)S(1)} %get-tuple-element.47), channel_id=1, source_target_pairs={{0,8},{1,17},{2,10},{3,19},{4,12},{5,21},{6,14},{7,23},{8,0},{9,25... | collective-permute-start | bytes 786440 | tf_op jit(solution)/shard_map/squares0/ppermute | solution.py:37
  9.5 0.8 %copy-start.4 = (bf16[64,512]{1,0:T(8,128)(2,1)S(1)}, bf16[64,512]{1,0:T(8,128)(2,1)}, u32[]{:S(2)}) copy-start(bf16[64,512]{1,0:T(8,128)(2,1)} %param.6) | copy-start | bytes 196612
  10.8 8.4 %collective-permute-start.7 = (bf16[64,512]{1,0:T(8,128)(2,1)S(1)}, bf16[64,512]{1,0:T(8,128)(2,1)S(1)}, u32[]{:S(2)}, u32[]{:S(2)}) collective-permute-start(bf16[64,512]{1,0:T(8,128)(2,1)S(1)} %fusion.14), channel_id=1, source_target_pairs={{0,6},{1,7},{2,4},{3,5},{4,2},{5,3},{6,0},{7,1},{8,14},{9,15},{10,... | collective-permute-start | bytes 196616 | tf_op jit(solution)/shard_map/fit3/ppermute | solution.py:29
  14.8 6.0 %collective-permute-start.8 = (bf16[64,512]{1,0:T(8,128)(2,1)S(1)}, bf16[64,512]{1,0:T(8,128)(2,1)S(1)}, u32[]{:S(2)}, u32[]{:S(2)}) collective-permute-start(bf16[64,512]{1,0:T(8,128)(2,1)S(1)} %fusion.15), channel_id=1, source_target_pairs={{0,4},{1,5},{2,6},{3,7},{4,0},{5,1},{6,2},{7,3},{8,12},{9,13},{10,... | collective-permute-start | bytes 196616 | tf_op jit(solution)/shard_map/fit2/ppermute | solution.py:29
  15.2 5.6 %collective-permute-start.9 = (bf16[64,512]{1,0:T(8,128)(2,1)S(1)}, bf16[64,512]{1,0:T(8,128)(2,1)S(1)}, u32[]{:S(2)}, u32[]{:S(2)}) collective-permute-start(bf16[64,512]{1,0:T(8,128)(2,1)S(1)} %fusion.16), channel_id=1, source_target_pairs={{0,2},{1,3},{2,0},{3,1},{4,6},{5,7},{6,4},{7,5},{8,10},{9,11},{10,... | collective-permute-start | bytes 196616 | tf_op jit(solution)/shard_map/fit1/ppermute | solution.py:29
  16.6 0.7 %copy-start.5 = (f32[256]{0:T(256)S(1)}, f32[256]{0:T(256)}, u32[]{:S(2)}) copy-start(f32[256]{0:T(256)} %param.9) | copy-start | bytes 3076
  17.4 8.0 %collective-permute-start.6 = (bf16[256,256]{1,0:T(8,128)(2,1)S(1)}, bf16[256,256]{1,0:T(8,128)(2,1)S(1)}, u32[]{:S(2)}, u32[]{:S(2)}) collective-permute-start(bf16[256,256]{1,0:T(8,128)(2,1)S(1)} %pad_maximum_fusion), channel_id=1, source_target_pairs={{0,1},{1,0},{2,3},{3,2},{4,5},{5,4},{6,7},{7,6},{8,9},{9,8},{10,11... | collective-permute-start | bytes 393224 | tf_op jit(solution)/shard_map/cells_core/ppermute | solution.py:24
  17.5 7.9 %collective-permute-start.5 = (bf16[256,512]{1,0:T(8,128)(2,1)S(1)}, bf16[256,512]{1,0:T(8,128)(2,1)S(1)}, u32[]{:S(2)}, u32[]{:S(2)}) collective-permute-start(bf16[256,512]{1,0:T(8,128)(2,1)S(1)} %convert_element_type.82), channel_id=1, source_target_pairs={{0,16},{1,9},{2,18},{3,11},{4,20},{5,13},{6,22},{7,15},{8,24},{9,1... | collective-permute-start | bytes 786440 | tf_op jit(solution)/shard_map/squares1/ppermute | solution.py:37
  21.0 6.7 %collective-permute-start.12 = (bf16[64,512]{1,0:T(8,128)(2,1)S(1)}, bf16[64,512]{1,0:T(8,128)(2,1)S(1)}, u32[]{:S(2)}, u32[]{:S(2)}) collective-permute-start(bf16[64,512]{1,0:T(8,128)(2,1)S(1)} %fusion.17), channel_id=1, source_target_pairs={{0,6},{1,7},{2,4},{3,5},{4,2},{5,3},{6,0},{7,1},{8,14},{9,15},{10,... | collective-permute-start | bytes 196616 | tf_op jit(solution)/shard_map/residual3/ppermute | solution.py:29
  23.2 4.8 %collective-permute-start.11 = (bf16[64,512]{1,0:T(8,128)(2,1)S(1)}, bf16[64,512]{1,0:T(8,128)(2,1)S(1)}, u32[]{:S(2)}, u32[]{:S(2)}) collective-permute-start(bf16[64,512]{1,0:T(8,128)(2,1)S(1)} %fusion.17), channel_id=1, source_target_pairs={{0,2},{1,3},{2,0},{3,1},{4,6},{5,7},{6,4},{7,5},{8,10},{9,11},{10,... | collective-permute-start | bytes 196616 | tf_op jit(solution)/shard_map/residual1/ppermute | solution.py:29
  23.2 5.7 %collective-permute-start.10 = (bf16[64,512]{1,0:T(8,128)(2,1)S(1)}, bf16[64,512]{1,0:T(8,128)(2,1)S(1)}, u32[]{:S(2)}, u32[]{:S(2)}) collective-permute-start(bf16[64,512]{1,0:T(8,128)(2,1)S(1)} %fusion.17), channel_id=1, source_target_pairs={{0,4},{1,5},{2,6},{3,7},{4,0},{5,1},{6,2},{7,3},{8,12},{9,13},{10,... | collective-permute-start | bytes 196616 | tf_op jit(solution)/shard_map/residual2/ppermute | solution.py:29
  29.0 1.6 %collective-permute-start.13 = (bf16[256,512]{1,0:T(8,128)(2,1)S(1)}, bf16[256,512]{1,0:T(8,128)(2,1)S(1)}, u32[]{:S(2)}, u32[]{:S(2)}) collective-permute-start(bf16[256,512]{1,0:T(8,128)(2,1)S(1)} %constant_dynamic-update-slice_fusion), channel_id=1, source_target_pairs={{0,1},{1,0},{2,3},{3,2},{4,5},{5,4},{6,7},{7,6},{8,9},{9,8},{10,11... | collective-permute-start | bytes 786440 | tf_op jit(solution)/shard_map/residual_core/ppermute | solution.py:24
  31.4 2.1 %collective-permute-start.16 = (bf16[256,512]{1,0:T(8,128)(2,1)S(1)}, bf16[256,512]{1,0:T(8,128)(2,1)S(1)}, u32[]{:S(2)}, u32[]{:S(2)}) collective-permute-start(bf16[256,512]{1,0:T(8,128)(2,1)S(1)} %get-tuple-element.49), channel_id=1, source_target_pairs={{0,1},{1,0},{2,3},{3,2},{4,5},{5,4},{6,7},{7,6},{8,9},{9,8},{10,11... | collective-permute-start | bytes 786440 | tf_op jit(solution)/shard_map/coef_core/ppermute | solution.py:24
  31.6 6.7 %collective-permute-start.14 = (bf16[256,512]{1,0:T(8,128)(2,1)S(1)}, bf16[256,512]{1,0:T(8,128)(2,1)S(1)}, u32[]{:S(2)}, u32[]{:S(2)}) collective-permute-start(bf16[256,512]{1,0:T(8,128)(2,1)S(1)} %get-tuple-element.45), channel_id=1, source_target_pairs={{0,8},{1,17},{2,10},{3,19},{4,12},{5,21},{6,14},{7,23},{8,0},{9,25... | collective-permute-start | bytes 786440 | tf_op jit(solution)/shard_map/squares0/ppermute | solution.py:37
  33.8 6.3 %collective-permute-start.17 = (bf16[64,512]{1,0:T(8,128)(2,1)S(1)}, bf16[64,512]{1,0:T(8,128)(2,1)S(1)}, u32[]{:S(2)}, u32[]{:S(2)}) collective-permute-start(bf16[64,512]{1,0:T(8,128)(2,1)S(1)} %get-tuple-element.51), channel_id=1, source_target_pairs={{0,6},{1,7},{2,4},{3,5},{4,2},{5,3},{6,0},{7,1},{8,14},{9,15},{10,... | collective-permute-start | bytes 196616 | tf_op jit(solution)/shard_map/fit3/ppermute | solution.py:29
  36.4 5.4 %collective-permute-start.19 = (bf16[64,512]{1,0:T(8,128)(2,1)S(1)}, bf16[64,512]{1,0:T(8,128)(2,1)S(1)}, u32[]{:S(2)}, u32[]{:S(2)}) collective-permute-start(bf16[64,512]{1,0:T(8,128)(2,1)S(1)} %get-tuple-element.52), channel_id=1, source_target_pairs={{0,2},{1,3},{2,0},{3,1},{4,6},{5,7},{6,4},{7,5},{8,10},{9,11},{10,... | collective-permute-start | bytes 196616 | tf_op jit(solution)/shard_map/fit1/ppermute | solution.py:29
  36.4 5.9 %collective-permute-start.18 = (bf16[64,512]{1,0:T(8,128)(2,1)S(1)}, bf16[64,512]{1,0:T(8,128)(2,1)S(1)}, u32[]{:S(2)}, u32[]{:S(2)}) collective-permute-start(bf16[64,512]{1,0:T(8,128)(2,1)S(1)} %get-tuple-element.53), channel_id=1, source_target_pairs={{0,4},{1,5},{2,6},{3,7},{4,0},{5,1},{6,2},{7,3},{8,12},{9,13},{10,... | collective-permute-start | bytes 196616 | tf_op jit(solution)/shard_map/fit2/ppermute | solution.py:29
  38.3 8.5 %collective-permute-start.15 = (bf16[256,512]{1,0:T(8,128)(2,1)S(1)}, bf16[256,512]{1,0:T(8,128)(2,1)S(1)}, u32[]{:S(2)}, u32[]{:S(2)}) collective-permute-start(bf16[256,512]{1,0:T(8,128)(2,1)S(1)} %fusion.22), channel_id=1, source_target_pairs={{0,16},{1,9},{2,18},{3,11},{4,20},{5,13},{6,22},{7,15},{8,24},{9,1... | collective-permute-start | bytes 786440 | tf_op jit(solution)/shard_map/squares1/ppermute | solution.py:37
  42.3 6.6 %collective-permute-start.22 = (bf16[64,512]{1,0:T(8,128)(2,1)S(1)}, bf16[64,512]{1,0:T(8,128)(2,1)S(1)}, u32[]{:S(2)}, u32[]{:S(2)}) collective-permute-start(bf16[64,512]{1,0:T(8,128)(2,1)S(1)} %fusion.26), channel_id=1, source_target_pairs={{0,6},{1,7},{2,4},{3,5},{4,2},{5,3},{6,0},{7,1},{8,14},{9,15},{10,... | collective-permute-start | bytes 196616 | tf_op jit(solution)/shard_map/residual3/ppermute | solution.py:29
  45.2 5.3 %collective-permute-start.21 = (bf16[64,512]{1,0:T(8,128)(2,1)S(1)}, bf16[64,512]{1,0:T(8,128)(2,1)S(1)}, u32[]{:S(2)}, u32[]{:S(2)}) collective-permute-start(bf16[64,512]{1,0:T(8,128)(2,1)S(1)} %fusion.26), channel_id=1, source_target_pairs={{0,2},{1,3},{2,0},{3,1},{4,6},{5,7},{6,4},{7,5},{8,10},{9,11},{10,... | collective-permute-start | bytes 196616 | tf_op jit(solution)/shard_map/residual1/ppermute | solution.py:29
  45.2 5.3 %collective-permute-start.20 = (bf16[64,512]{1,0:T(8,128)(2,1)S(1)}, bf16[64,512]{1,0:T(8,128)(2,1)S(1)}, u32[]{:S(2)}, u32[]{:S(2)}) collective-permute-start(bf16[64,512]{1,0:T(8,128)(2,1)S(1)} %fusion.26), channel_id=1, source_target_pairs={{0,4},{1,5},{2,6},{3,7},{4,0},{5,1},{6,2},{7,3},{8,12},{9,13},{10,... | collective-permute-start | bytes 196616 | tf_op jit(solution)/shard_map/residual2/ppermute | solution.py:29
  50.5 1.6 %collective-permute-start.23 = (bf16[256,512]{1,0:T(8,128)(2,1)S(1)}, bf16[256,512]{1,0:T(8,128)(2,1)S(1)}, u32[]{:S(2)}, u32[]{:S(2)}) collective-permute-start(bf16[256,512]{1,0:T(8,128)(2,1)S(1)} %constant_dynamic-update-slice_fusion.4), channel_id=1, source_target_pairs={{0,1},{1,0},{2,3},{3,2},{4,5},{5,4},{6,7},{7,6},{8,9},{9,8},{10,11... | collective-permute-start | bytes 786440 | tf_op jit(solution)/shard_map/residual_core/ppermute | solution.py:24
  50.9 2.6 %copy-start = (f32[256,512]{1,0:T(8,128)}, f32[256,512]{1,0:T(8,128)S(1)}, u32[]{:S(2)}) copy-start(f32[256,512]{1,0:T(8,128)S(1)} %get-tuple-element.43) | copy-start | bytes 1572868
  50.9 2.6 %copy-start.1 = (f32[256,512]{1,0:T(8,128)}, f32[256,512]{1,0:T(8,128)S(1)}, u32[]{:S(2)}) copy-start(f32[256,512]{1,0:T(8,128)S(1)} %get-tuple-element.44) | copy-start | bytes 1572868

commit v6 on v5

--- a/solution.py
+++ b/solution.py
@@ -115,14 +115,15 @@
         residual = dict(zip(evens_first, ready))
         residual = jnp.concatenate([residual[k] for k in order])
         residual_other = core_swap(residual, "residual_core")
-        product = lax.dot_general(own, residual, contract, preferred_element_type=f32) + lax.dot_general(
-            across, residual_other, contract, preferred_element_type=f32
-        )
-
         norms = jnp.sqrt(squares)
         consensus = merged * (1.0 - weights / jnp.maximum(norms, weights))
         dual = merged - consensus
-        coef = coef + (rho_weight * (consensus - dual) - product / n_cells - rho_weight * coef) * step_size
+        scale = step_size / n_cells
+        coef = coef + (rho_weight * (consensus - dual) - rho_weight * coef) * step_size
+        coef = coef - lax.dot_general(own, residual, contract, preferred_element_type=f32) * scale
+        if step < ITERS - 1:
+            residual_other, coef, dual = together(residual_other, coef, dual)
+        coef = coef - lax.dot_general(across, residual_other, contract, preferred_element_type=f32) * scale
     return (coef, consensus, dual)
 
 

time: 53.7 us -> 53.4 us (level)
  waiting for transfers between devices: 14.3 us -> 13.6 us
    dot_general x2, matrix products: 1.66 us -> 0.73 us  [shards(): lax.dot_general(own, residual, contract, preferred_element_type=f32) * scale]
    dot_general x2, matrix products: 0.48 us -> 1.33 us  [shards(): lax.dot_general(across, residual_other, contract, preferred_element_type=...]
    ppermute x5, waiting for transfers between devices: 2.77 us -> 2.06 us  [core_swap(): lax.ppermute(value, 'shard', [(i, i ^ 1) for i in range(lax.axis_size('sh...]
  transfers between devices with their start and end apart: 24 -> 24, of which waited for: 11 -> 11; matrix products, arithmetic and copies ran while one was open for 5% -> 7% of each run, Pallas kernels for 0% -> 0%
where the time goes in v6:
time: 53.4 us; the launch traced here: 53.2 us
  starting transfers between devices  30.8 us (58%)
  waiting for transfers between devices  13.6 us (25%)
  matrix products  3.83 us (7%)
  local copies, waits for them, and re-layouts  2.52 us (5%)
  other arithmetic  1.37 us (3%)
  between operations  1.13 us (2%)
    ppermute x15, starting transfers between devices, chip_swap(): lax.ppermute(value, 'shard', [(i, i ^ 2 * mask) for i in range(lax.axis_s...  24.2 us
    ppermute x15, waiting for transfers between devices, chip_swap(): lax.ppermute(value, 'shard', [(i, i ^ 2 * mask) for i in range(lax.axis_s...  11.5 us
    ppermute x4, starting transfers between devices, cond_swap(): return lax.ppermute(value, ('cond', 'shard'), pairs)  6.08 us
    ppermute x5, waiting for transfers between devices, core_swap(): lax.ppermute(value, 'shard', [(i, i ^ 1) for i in range(lax.axis_size('sh...  2.06 us
    dot_general x10, matrix products, dot(): return jnp.dot(x, c, preferred_element_type=f32)  1.76 us
    unnamed x18, local copies, waits for them, and re-layouts  1.39 us
    dot_general x2, matrix products, shards(): lax.dot_general(across, residual_other, contract, preferred_element_type=...  1.33 us
  transfers between devices with their start and end apart: 24, of which 11 were waited for; matrix products, arithmetic and copies ran while one was open for 7% of the time, Pallas kernels for 0%

profile of v6, /device:TPU:0, one launch (start us, length us, event | category | flops | bytes accessed | tf_op | source)
XLA Modules:
  0.0 53.2 jit_solution(16539802522481893774)
XLA Ops:
  0.7 1.0 %constant_dynamic-slice_fusion = (bf16[64,256]{1,0:T(8,128)(2,1)S(1)}, bf16[1,64,256]{2,1,0:T(8,128)(2,1)S(1)}, bf16[1,64,256]{2,1,0:T(8,128)(2,1)S(1)}, bf16[1,...) fusion(bf16[64,2048]{1,0:T(8,128)(2,1)} %param.5, ...), kind=kLoop, calls=%fused_computation.65 | loop fusion | bytes 524320 | tf_op jit(solution)/shard_map/dynamic_slice | solution.py:62
  1.7 5.1 %collective-permute-start = (bf16[2,64,256]{2,1,0:T(8,128)(2,1)S(1)}, bf16[2,64,256]{2,1,0:T(8,128)(2,1)S(1)}, u32[]{:S(2)}, u32[]{:S(2)}) collective-permute-start(bf16[2,64,256]{2,1,0:T(8,128)(2,1)S(1)} %pad_maximum_fusion.2), channel_id=1, source_target_pairs={{0,6},{1,7},{2,4},{3,5},{4,2},{5,3},{6,0},{7,1},{8,14},{9,15},{10,... | collective-permute-start | bytes 196616 | tf_op jit(solution)/shard_map/cells3/ppermute | solution.py:29
  6.9 0.6 %collective-permute-start.3 = (bf16[2,64,256]{2,1,0:T(8,128)(2,1)S(1)}, bf16[2,64,256]{2,1,0:T(8,128)(2,1)S(1)}, u32[]{:S(2)}, u32[]{:S(2)}) collective-permute-start(bf16[2,64,256]{2,1,0:T(8,128)(2,1)S(1)} %pad_maximum_fusion.4), channel_id=1, source_target_pairs={{0,2},{1,3},{2,0},{3,1},{4,6},{5,7},{6,4},{7,5},{8,10},{9,11},{10,... | collective-permute-start | bytes 196616 | tf_op jit(solution)/shard_map/cells1/ppermute | solution.py:29
  7.6 0.1 multiply_convert_fusion.1
  7.8 1.8 %collective-permute-start.4 = (bf16[256,512]{1,0:T(8,128)(2,1)S(1)}, bf16[256,512]{1,0:T(8,128)(2,1)S(1)}, u32[]{:S(2)}, u32[]{:S(2)}) collective-permute-start(bf16[256,512]{1,0:T(8,128)(2,1)S(1)} %get-tuple-element.55), channel_id=1, source_target_pairs={{0,8},{1,17},{2,10},{3,19},{4,12},{5,21},{6,14},{7,23},{8,0},{9,25... | collective-permute-start | bytes 786440 | tf_op jit(solution)/shard_map/squares0/ppermute | solution.py:37
  9.5 0.2 fusion.29
  9.7 0.7 %copy-done.4 = bf16[64,512]{1,0:T(8,128)(2,1)S(1)} copy-done((bf16[64,512]{1,0:T(8,128)(2,1)S(1)}, bf16[64,512]{1,0:T(8,128)(2,1)}, u32[]{:S(2)}) %copy-start.4) | copy-done | bytes 65560
  10.4 0.2 fusion.22
  10.6 0.2 fusion.6
  10.8 3.7 %collective-permute-start.7 = (bf16[64,512]{1,0:T(8,128)(2,1)S(1)}, bf16[64,512]{1,0:T(8,128)(2,1)S(1)}, u32[]{:S(2)}, u32[]{:S(2)}) collective-permute-start(bf16[64,512]{1,0:T(8,128)(2,1)S(1)} %fusion.6), channel_id=1, source_target_pairs={{0,6},{1,7},{2,4},{3,5},{4,2},{5,3},{6,0},{7,1},{8,14},{9,15},{10,... | collective-permute-start | bytes 196616 | tf_op jit(solution)/shard_map/fit3/ppermute | solution.py:29
  14.4 0.2 fusion.20
  14.6 0.2 fusion.7
  14.9 0.2 fusion.21
  15.0 0.2 fusion.8
  15.2 1.3 %collective-permute-start.9 = (bf16[64,512]{1,0:T(8,128)(2,1)S(1)}, bf16[64,512]{1,0:T(8,128)(2,1)S(1)}, u32[]{:S(2)}, u32[]{:S(2)}) collective-permute-start(bf16[64,512]{1,0:T(8,128)(2,1)S(1)} %fusion.8), channel_id=1, source_target_pairs={{0,2},{1,3},{2,0},{3,1},{4,6},{5,7},{6,4},{7,5},{8,10},{9,11},{10,... | collective-permute-start | bytes 196616 | tf_op jit(solution)/shard_map/fit1/ppermute | solution.py:29
  16.7 0.7 %copy-done.5 = f32[256]{0:T(256)S(1)} copy-done((f32[256]{0:T(256)S(1)}, f32[256]{0:T(256)}, u32[]{:S(2)}) %copy-start.5) | copy-done | bytes 1048
  17.5 1.6 %collective-permute-start.5 = (bf16[256,512]{1,0:T(8,128)(2,1)S(1)}, bf16[256,512]{1,0:T(8,128)(2,1)S(1)}, u32[]{:S(2)}, u32[]{:S(2)}) collective-permute-start(bf16[256,512]{1,0:T(8,128)(2,1)S(1)} %convert_element_type.82), channel_id=1, source_target_pairs={{0,16},{1,9},{2,18},{3,11},{4,20},{5,13},{6,22},{7,15},{8,24},{9,1... | collective-permute-start | bytes 786440 | tf_op jit(solution)/shard_map/squares1/ppermute | solution.py:37
  19.2 1.6 %collective-permute-done.9 = bf16[64,512]{1,0:T(8,128)(2,1)S(1)} collective-permute-done((bf16[64,512]{1,0:T(8,128)(2,1)S(1)}, bf16[64,512]{1,0:T(8,128)(2,1)S(1)}, u32[]{:S(2)}, u32[]{:S(2)}) %collective-permute-start.9) | collective-permute-done | bytes 65568 | tf_op jit(solution)/shard_map/fit1/ppermute | solution.py:29
  20.8 0.2 fusion.9
  21.0 2.3 %collective-permute-start.12 = (bf16[64,512]{1,0:T(8,128)(2,1)S(1)}, bf16[64,512]{1,0:T(8,128)(2,1)S(1)}, u32[]{:S(2)}, u32[]{:S(2)}) collective-permute-start(bf16[64,512]{1,0:T(8,128)(2,1)S(1)} %fusion.9), channel_id=1, source_target_pairs={{0,6},{1,7},{2,4},{3,5},{4,2},{5,3},{6,0},{7,1},{8,14},{9,15},{10,... | collective-permute-start | bytes 196616 | tf_op jit(solution)/shard_map/residual3/ppermute | solution.py:29
  23.2 2.2 %collective-permute-start.10 = (bf16[64,512]{1,0:T(8,128)(2,1)S(1)}, bf16[64,512]{1,0:T(8,128)(2,1)S(1)}, u32[]{:S(2)}, u32[]{:S(2)}) collective-permute-start(bf16[64,512]{1,0:T(8,128)(2,1)S(1)} %fusion.9), channel_id=1, source_target_pairs={{0,4},{1,5},{2,6},{3,7},{4,0},{5,1},{6,2},{7,3},{8,12},{9,13},{10,... | collective-permute-start | bytes 196616 | tf_op jit(solution)/shard_map/residual2/ppermute | solution.py:29
  25.6 2.0 %collective-permute-done.12 = bf16[64,512]{1,0:T(8,128)(2,1)S(1)} collective-permute-done((bf16[64,512]{1,0:T(8,128)(2,1)S(1)}, bf16[64,512]{1,0:T(8,128)(2,1)S(1)}, u32[]{:S(2)}, u32[]{:S(2)}) %collective-permute-start.12) | collective-permute-done | bytes 65568 | tf_op jit(solution)/shard_map/residual3/ppermute | solution.py:29
  27.5 0.5 collective-permute-done.11
  28.0 0.9 %collective-permute-done.10 = bf16[64,512]{1,0:T(8,128)(2,1)S(1)} collective-permute-done((bf16[64,512]{1,0:T(8,128)(2,1)S(1)}, bf16[64,512]{1,0:T(8,128)(2,1)S(1)}, u32[]{:S(2)}, u32[]{:S(2)}) %collective-permute-start.10) | collective-permute-done | bytes 65568 | tf_op jit(solution)/shard_map/residual2/ppermute | solution.py:29
  29.1 0.5 fusion.1
  29.6 0.2 fusion.19
  29.8 0.8 %collective-permute-done.13 = bf16[256,512]{1,0:T(8,128)(2,1)S(1)} collective-permute-done((bf16[256,512]{1,0:T(8,128)(2,1)S(1)}, bf16[256,512]{1,0:T(8,128)(2,1)S(1)}, u32[]{:S(2)}, u32[]{:S(2)}) %collective-permute-start.13) | collective-permute-done | bytes 262176 | tf_op jit(solution)/shard_map/residual_core/ppermute | solution.py:24
  30.6 0.3 convolution_multiply_fusion.2
  30.9 0.2 collective-permute-start.16
  31.1 0.1 multiply_convert_fusion
  31.2 1.8 %collective-permute-start.14 = (bf16[256,512]{1,0:T(8,128)(2,1)S(1)}, bf16[256,512]{1,0:T(8,128)(2,1)S(1)}, u32[]{:S(2)}, u32[]{:S(2)}) collective-permute-start(bf16[256,512]{1,0:T(8,128)(2,1)S(1)} %get-tuple-element.53), channel_id=1, source_target_pairs={{0,8},{1,17},{2,10},{3,19},{4,12},{5,21},{6,14},{7,23},{8,0},{9,25... | collective-permute-start | bytes 786440 | tf_op jit(solution)/shard_map/squares0/ppermute | solution.py:37
  33.0 0.2 fusion.23
  33.3 0.2 fusion.28
  33.5 2.6 %collective-permute-start.17 = (bf16[64,512]{1,0:T(8,128)(2,1)S(1)}, bf16[64,512]{1,0:T(8,128)(2,1)S(1)}, u32[]{:S(2)}, u32[]{:S(2)}) collective-permute-start(bf16[64,512]{1,0:T(8,128)(2,1)S(1)} %get-tuple-element.58), channel_id=1, source_target_pairs={{0,6},{1,7},{2,4},{3,5},{4,2},{5,3},{6,0},{7,1},{8,14},{9,15},{10,... | collective-permute-start | bytes 196616 | tf_op jit(solution)/shard_map/fit3/ppermute | solution.py:29
  36.1 1.9 %collective-permute-start.18 = (bf16[64,512]{1,0:T(8,128)(2,1)S(1)}, bf16[64,512]{1,0:T(8,128)(2,1)S(1)}, u32[]{:S(2)}, u32[]{:S(2)}) collective-permute-start(bf16[64,512]{1,0:T(8,128)(2,1)S(1)} %get-tuple-element.60), channel_id=1, source_target_pairs={{0,4},{1,5},{2,6},{3,7},{4,0},{5,1},{6,2},{7,3},{8,12},{9,13},{10,... | collective-permute-start | bytes 196616 | tf_op jit(solution)/shard_map/fit2/ppermute | solution.py:29
  38.0 1.0 %collective-permute-start.15 = (bf16[256,512]{1,0:T(8,128)(2,1)S(1)}, bf16[256,512]{1,0:T(8,128)(2,1)S(1)}, u32[]{:S(2)}, u32[]{:S(2)}) collective-permute-start(bf16[256,512]{1,0:T(8,128)(2,1)S(1)} %fusion.14), channel_id=1, source_target_pairs={{0,16},{1,9},{2,18},{3,11},{4,20},{5,13},{6,22},{7,15},{8,24},{9,1... | collective-permute-start | bytes 786440 | tf_op jit(solution)/shard_map/squares1/ppermute | solution.py:37
  39.0 0.8 %collective-permute-done.17 = bf16[64,512]{1,0:T(8,128)(2,1)S(1)} collective-permute-done((bf16[64,512]{1,0:T(8,128)(2,1)S(1)}, bf16[64,512]{1,0:T(8,128)(2,1)S(1)}, u32[]{:S(2)}, u32[]{:S(2)}) %collective-permute-start.17) | collective-permute-done | bytes 65568 | tf_op jit(solution)/shard_map/fit3/ppermute | solution.py:29
  39.8 1.7 %collective-permute-done.19 = bf16[64,512]{1,0:T(8,128)(2,1)S(1)} collective-permute-done((bf16[64,512]{1,0:T(8,128)(2,1)S(1)}, bf16[64,512]{1,0:T(8,128)(2,1)S(1)}, u32[]{:S(2)}, u32[]{:S(2)}) %collective-permute-start.19) | collective-permute-done | bytes 65568 | tf_op jit(solution)/shard_map/fit1/ppermute | solution.py:29
  41.4 0.6 %collective-permute-done.18 = bf16[64,512]{1,0:T(8,128)(2,1)S(1)} collective-permute-done((bf16[64,512]{1,0:T(8,128)(2,1)S(1)}, bf16[64,512]{1,0:T(8,128)(2,1)S(1)}, u32[]{:S(2)}, u32[]{:S(2)}) %collective-permute-start.18) | collective-permute-done | bytes 65568 | tf_op jit(solution)/shard_map/fit2/ppermute | solution.py:29
  42.1 2.9 %collective-permute-start.22 = (bf16[64,512]{1,0:T(8,128)(2,1)S(1)}, bf16[64,512]{1,0:T(8,128)(2,1)S(1)}, u32[]{:S(2)}, u32[]{:S(2)}) collective-permute-start(bf16[64,512]{1,0:T(8,128)(2,1)S(1)} %fusion.18), channel_id=1, source_target_pairs={{0,6},{1,7},{2,4},{3,5},{4,2},{5,3},{6,0},{7,1},{8,14},{9,15},{10,... | collective-permute-start | bytes 196616 | tf_op jit(solution)/shard_map/residual3/ppermute | solution.py:29
  44.9 1.6 %collective-permute-start.20 = (bf16[64,512]{1,0:T(8,128)(2,1)S(1)}, bf16[64,512]{1,0:T(8,128)(2,1)S(1)}, u32[]{:S(2)}, u32[]{:S(2)}) collective-permute-start(bf16[64,512]{1,0:T(8,128)(2,1)S(1)} %fusion.18), channel_id=1, source_target_pairs={{0,4},{1,5},{2,6},{3,7},{4,0},{5,1},{6,2},{7,3},{8,12},{9,13},{10,... | collective-permute-start | bytes 196616 | tf_op jit(solution)/shard_map/residual2/ppermute | solution.py:29
  46.5 0.1 convert_add_fusion
  46.6 2.1 %collective-permute-done.22 = bf16[64,512]{1,0:T(8,128)(2,1)S(1)} collective-permute-done((bf16[64,512]{1,0:T(8,128)(2,1)S(1)}, bf16[64,512]{1,0:T(8,128)(2,1)S(1)}, u32[]{:S(2)}, u32[]{:S(2)}) %collective-permute-start.22) | collective-permute-done | bytes 65568 | tf_op jit(solution)/shard_map/residual3/ppermute | solution.py:29
  48.7 1.5 %collective-permute-done.21 = bf16[64,512]{1,0:T(8,128)(2,1)S(1)} collective-permute-done((bf16[64,512]{1,0:T(8,128)(2,1)S(1)}, bf16[64,512]{1,0:T(8,128)(2,1)S(1)}, u32[]{:S(2)}, u32[]{:S(2)}) %collective-permute-start.21) | collective-permute-done | bytes 65568 | tf_op jit(solution)/shard_map/residual1/ppermute | solution.py:29
  50.2 0.3 fusion.24
  50.6 0.2 convolution_multiply_fusion.1
  50.9 1.3 %collective-permute-done.23 = bf16[256,512]{1,0:T(8,128)(2,1)S(1)} collective-permute-done((bf16[256,512]{1,0:T(8,128)(2,1)S(1)}, bf16[256,512]{1,0:T(8,128)(2,1)S(1)}, u32[]{:S(2)}, u32[]{:S(2)}) %collective-permute-start.23) | collective-permute-done | bytes 262176 | tf_op jit(solution)/shard_map/residual_core/ppermute | solution.py:24
  52.2 1.1 %fusion = f32[256,512]{1,0:T(8,128)} fusion(bf16[256,256]{1,0:T(8,128)(2,1)S(1)} %collective-permute-done.6, bf16[256,512]{1,0:T(8,128)(2,1)S(1)} %collective-permute-done.23, f32[256,512]{1,0:T(8,128)S(1)} %convolution_multiply_fusion.1, f32[256,512]{1,0:T(8,128)S(1)} %get-tuple-element.52, f32[256,512]{1,0:T(8,128)S(1)} %get-tuple-element.50, ...), kind=kOutput, calls=%fused_computation.1 | convolution fusion | flops 68288512 | bytes 3016704 | tf_op jit(solution)/shard_map/dot_general | solution.py:126
  (61 shorter events, 1.2 us)
Async XLA Ops:
  0.6 6.9 %copy-start.2 = (f32[256,512]{1,0:T(8,128)S(1)}, f32[256,512]{1,0:T(8,128)}, u32[]{:S(2)}) copy-start(f32[256,512]{1,0:T(8,128)} %param.8) | copy-start | bytes 1572868
  0.6 6.9 %copy-start.3 = (f32[256,512]{1,0:T(8,128)S(1)}, f32[256,512]{1,0:T(8,128)}, u32[]{:S(2)}) copy-start(f32[256,512]{1,0:T(8,128)} %param.7) | copy-start | bytes 1572868
  1.7 8.7 %collective-permute-start = (bf16[2,64,256]{2,1,0:T(8,128)(2,1)S(1)}, bf16[2,64,256]{2,1,0:T(8,128)(2,1)S(1)}, u32[]{:S(2)}, u32[]{:S(2)}) collective-permute-start(bf16[2,64,256]{2,1,0:T(8,128)(2,1)S(1)} %pad_maximum_fusion.2), channel_id=1, source_target_pairs={{0,6},{1,7},{2,4},{3,5},{4,2},{5,3},{6,0},{7,1},{8,14},{9,15},{10,... | collective-permute-start | bytes 196616 | tf_op jit(solution)/shard_map/cells3/ppermute | solution.py:29
  6.8 7.6 %collective-permute-start.1 = (bf16[2,64,256]{2,1,0:T(8,128)(2,1)S(1)}, bf16[2,64,256]{2,1,0:T(8,128)(2,1)S(1)}, u32[]{:S(2)}, u32[]{:S(2)}) collective-permute-start(bf16[2,64,256]{2,1,0:T(8,128)(2,1)S(1)} %pad_maximum_fusion.3), channel_id=1, source_target_pairs={{0,4},{1,5},{2,6},{3,7},{4,0},{5,1},{6,2},{7,3},{8,12},{9,13},{10,... | collective-permute-start | bytes 196616 | tf_op jit(solution)/shard_map/cells2/ppermute | solution.py:29
  6.9 7.9 %collective-permute-start.3 = (bf16[2,64,256]{2,1,0:T(8,128)(2,1)S(1)}, bf16[2,64,256]{2,1,0:T(8,128)(2,1)S(1)}, u32[]{:S(2)}, u32[]{:S(2)}) collective-permute-start(bf16[2,64,256]{2,1,0:T(8,128)(2,1)S(1)} %pad_maximum_fusion.4), channel_id=1, source_target_pairs={{0,2},{1,3},{2,0},{3,1},{4,6},{5,7},{6,4},{7,5},{8,10},{9,11},{10,... | collective-permute-start | bytes 196616 | tf_op jit(solution)/shard_map/cells1/ppermute | solution.py:29
  7.7 2.7 %collective-permute-start.2 = (bf16[256,512]{1,0:T(8,128)(2,1)S(1)}, bf16[256,512]{1,0:T(8,128)(2,1)S(1)}, u32[]{:S(2)}, u32[]{:S(2)}) collective-permute-start(bf16[256,512]{1,0:T(8,128)(2,1)S(1)} %get-tuple-element.57), channel_id=1, source_target_pairs={{0,1},{1,0},{2,3},{3,2},{4,5},{5,4},{6,7},{7,6},{8,9},{9,8},{10,11... | collective-permute-start | bytes 786440 | tf_op jit(solution)/shard_map/coef_core/ppermute | solution.py:24
  7.8 8.8 %collective-permute-start.4 = (bf16[256,512]{1,0:T(8,128)(2,1)S(1)}, bf16[256,512]{1,0:T(8,128)(2,1)S(1)}, u32[]{:S(2)}, u32[]{:S(2)}) collective-permute-start(bf16[256,512]{1,0:T(8,128)(2,1)S(1)} %get-tuple-element.55), channel_id=1, source_target_pairs={{0,8},{1,17},{2,10},{3,19},{4,12},{5,21},{6,14},{7,23},{8,0},{9,25... | collective-permute-start | bytes 786440 | tf_op jit(solution)/shard_map/squares0/ppermute | solution.py:37
  9.5 0.8 %copy-start.4 = (bf16[64,512]{1,0:T(8,128)(2,1)S(1)}, bf16[64,512]{1,0:T(8,128)(2,1)}, u32[]{:S(2)}) copy-start(bf16[64,512]{1,0:T(8,128)(2,1)} %param.6) | copy-start | bytes 196612
  10.8 8.4 %collective-permute-start.7 = (bf16[64,512]{1,0:T(8,128)(2,1)S(1)}, bf16[64,512]{1,0:T(8,128)(2,1)S(1)}, u32[]{:S(2)}, u32[]{:S(2)}) collective-permute-start(bf16[64,512]{1,0:T(8,128)(2,1)S(1)} %fusion.6), channel_id=1, source_target_pairs={{0,6},{1,7},{2,4},{3,5},{4,2},{5,3},{6,0},{7,1},{8,14},{9,15},{10,... | collective-permute-start | bytes 196616 | tf_op jit(solution)/shard_map/fit3/ppermute | solution.py:29
  14.8 6.0 %collective-permute-start.8 = (bf16[64,512]{1,0:T(8,128)(2,1)S(1)}, bf16[64,512]{1,0:T(8,128)(2,1)S(1)}, u32[]{:S(2)}, u32[]{:S(2)}) collective-permute-start(bf16[64,512]{1,0:T(8,128)(2,1)S(1)} %fusion.7), channel_id=1, source_target_pairs={{0,4},{1,5},{2,6},{3,7},{4,0},{5,1},{6,2},{7,3},{8,12},{9,13},{10,... | collective-permute-start | bytes 196616 | tf_op jit(solution)/shard_map/fit2/ppermute | solution.py:29
  15.2 5.6 %collective-permute-start.9 = (bf16[64,512]{1,0:T(8,128)(2,1)S(1)}, bf16[64,512]{1,0:T(8,128)(2,1)S(1)}, u32[]{:S(2)}, u32[]{:S(2)}) collective-permute-start(bf16[64,512]{1,0:T(8,128)(2,1)S(1)} %fusion.8), channel_id=1, source_target_pairs={{0,2},{1,3},{2,0},{3,1},{4,6},{5,7},{6,4},{7,5},{8,10},{9,11},{10,... | collective-permute-start | bytes 196616 | tf_op jit(solution)/shard_map/fit1/ppermute | solution.py:29
  16.6 0.7 %copy-start.5 = (f32[256]{0:T(256)S(1)}, f32[256]{0:T(256)}, u32[]{:S(2)}) copy-start(f32[256]{0:T(256)} %param.9) | copy-start | bytes 3076
  17.4 8.0 %collective-permute-start.6 = (bf16[256,256]{1,0:T(8,128)(2,1)S(1)}, bf16[256,256]{1,0:T(8,128)(2,1)S(1)}, u32[]{:S(2)}, u32[]{:S(2)}) collective-permute-start(bf16[256,256]{1,0:T(8,128)(2,1)S(1)} %pad_maximum_fusion), channel_id=1, source_target_pairs={{0,1},{1,0},{2,3},{3,2},{4,5},{5,4},{6,7},{7,6},{8,9},{9,8},{10,11... | collective-permute-start | bytes 393224 | tf_op jit(solution)/shard_map/cells_core/ppermute | solution.py:24
  17.5 7.9 %collective-permute-start.5 = (bf16[256,512]{1,0:T(8,128)(2,1)S(1)}, bf16[256,512]{1,0:T(8,128)(2,1)S(1)}, u32[]{:S(2)}, u32[]{:S(2)}) collective-permute-start(bf16[256,512]{1,0:T(8,128)(2,1)S(1)} %convert_element_type.82), channel_id=1, source_target_pairs={{0,16},{1,9},{2,18},{3,11},{4,20},{5,13},{6,22},{7,15},{8,24},{9,1... | collective-permute-start | bytes 786440 | tf_op jit(solution)/shard_map/squares1/ppermute | solution.py:37
  21.0 6.6 %collective-permute-start.12 = (bf16[64,512]{1,0:T(8,128)(2,1)S(1)}, bf16[64,512]{1,0:T(8,128)(2,1)S(1)}, u32[]{:S(2)}, u32[]{:S(2)}) collective-permute-start(bf16[64,512]{1,0:T(8,128)(2,1)S(1)} %fusion.9), channel_id=1, source_target_pairs={{0,6},{1,7},{2,4},{3,5},{4,2},{5,3},{6,0},{7,1},{8,14},{9,15},{10,... | collective-permute-start | bytes 196616 | tf_op jit(solution)/shard_map/residual3/ppermute | solution.py:29
  23.2 4.8 %collective-permute-start.11 = (bf16[64,512]{1,0:T(8,128)(2,1)S(1)}, bf16[64,512]{1,0:T(8,128)(2,1)S(1)}, u32[]{:S(2)}, u32[]{:S(2)}) collective-permute-start(bf16[64,512]{1,0:T(8,128)(2,1)S(1)} %fusion.9), channel_id=1, source_target_pairs={{0,2},{1,3},{2,0},{3,1},{4,6},{5,7},{6,4},{7,5},{8,10},{9,11},{10,... | collective-permute-start | bytes 196616 | tf_op jit(solution)/shard_map/residual1/ppermute | solution.py:29
  23.2 5.7 %collective-permute-start.10 = (bf16[64,512]{1,0:T(8,128)(2,1)S(1)}, bf16[64,512]{1,0:T(8,128)(2,1)S(1)}, u32[]{:S(2)}, u32[]{:S(2)}) collective-permute-start(bf16[64,512]{1,0:T(8,128)(2,1)S(1)} %fusion.9), channel_id=1, source_target_pairs={{0,4},{1,5},{2,6},{3,7},{4,0},{5,1},{6,2},{7,3},{8,12},{9,13},{10,... | collective-permute-start | bytes 196616 | tf_op jit(solution)/shard_map/residual2/ppermute | solution.py:29
  29.0 1.6 %collective-permute-start.13 = (bf16[256,512]{1,0:T(8,128)(2,1)S(1)}, bf16[256,512]{1,0:T(8,128)(2,1)S(1)}, u32[]{:S(2)}, u32[]{:S(2)}) collective-permute-start(bf16[256,512]{1,0:T(8,128)(2,1)S(1)} %constant_dynamic-update-slice_fusion), channel_id=1, source_target_pairs={{0,1},{1,0},{2,3},{3,2},{4,5},{5,4},{6,7},{7,6},{8,9},{9,8},{10,11... | collective-permute-start | bytes 786440 | tf_op jit(solution)/shard_map/residual_core/ppermute | solution.py:24
  30.9 2.3 %collective-permute-start.16 = (bf16[256,512]{1,0:T(8,128)(2,1)S(1)}, bf16[256,512]{1,0:T(8,128)(2,1)S(1)}, u32[]{:S(2)}, u32[]{:S(2)}) collective-permute-start(bf16[256,512]{1,0:T(8,128)(2,1)S(1)} %get-tuple-element.51), channel_id=1, source_target_pairs={{0,1},{1,0},{2,3},{3,2},{4,5},{5,4},{6,7},{7,6},{8,9},{9,8},{10,11... | collective-permute-start | bytes 786440 | tf_op jit(solution)/shard_map/coef_core/ppermute | solution.py:24
  31.2 6.7 %collective-permute-start.14 = (bf16[256,512]{1,0:T(8,128)(2,1)S(1)}, bf16[256,512]{1,0:T(8,128)(2,1)S(1)}, u32[]{:S(2)}, u32[]{:S(2)}) collective-permute-start(bf16[256,512]{1,0:T(8,128)(2,1)S(1)} %get-tuple-element.53), channel_id=1, source_target_pairs={{0,8},{1,17},{2,10},{3,19},{4,12},{5,21},{6,14},{7,23},{8,0},{9,25... | collective-permute-start | bytes 786440 | tf_op jit(solution)/shard_map/squares0/ppermute | solution.py:37
  33.5 6.3 %collective-permute-start.17 = (bf16[64,512]{1,0:T(8,128)(2,1)S(1)}, bf16[64,512]{1,0:T(8,128)(2,1)S(1)}, u32[]{:S(2)}, u32[]{:S(2)}) collective-permute-start(bf16[64,512]{1,0:T(8,128)(2,1)S(1)} %get-tuple-element.58), channel_id=1, source_target_pairs={{0,6},{1,7},{2,4},{3,5},{4,2},{5,3},{6,0},{7,1},{8,14},{9,15},{10,... | collective-permute-start | bytes 196616 | tf_op jit(solution)/shard_map/fit3/ppermute | solution.py:29
  36.1 5.3 %collective-permute-start.19 = (bf16[64,512]{1,0:T(8,128)(2,1)S(1)}, bf16[64,512]{1,0:T(8,128)(2,1)S(1)}, u32[]{:S(2)}, u32[]{:S(2)}) collective-permute-start(bf16[64,512]{1,0:T(8,128)(2,1)S(1)} %get-tuple-element.59), channel_id=1, source_target_pairs={{0,2},{1,3},{2,0},{3,1},{4,6},{5,7},{6,4},{7,5},{8,10},{9,11},{10,... | collective-permute-start | bytes 196616 | tf_op jit(solution)/shard_map/fit1/ppermute | solution.py:29
  36.1 5.9 %collective-permute-start.18 = (bf16[64,512]{1,0:T(8,128)(2,1)S(1)}, bf16[64,512]{1,0:T(8,128)(2,1)S(1)}, u32[]{:S(2)}, u32[]{:S(2)}) collective-permute-start(bf16[64,512]{1,0:T(8,128)(2,1)S(1)} %get-tuple-element.60), channel_id=1, source_target_pairs={{0,4},{1,5},{2,6},{3,7},{4,0},{5,1},{6,2},{7,3},{8,12},{9,13},{10,... | collective-permute-start | bytes 196616 | tf_op jit(solution)/shard_map/fit2/ppermute | solution.py:29
  38.0 8.5 %collective-permute-start.15 = (bf16[256,512]{1,0:T(8,128)(2,1)S(1)}, bf16[256,512]{1,0:T(8,128)(2,1)S(1)}, u32[]{:S(2)}, u32[]{:S(2)}) collective-permute-start(bf16[256,512]{1,0:T(8,128)(2,1)S(1)} %fusion.14), channel_id=1, source_target_pairs={{0,16},{1,9},{2,18},{3,11},{4,20},{5,13},{6,22},{7,15},{8,24},{9,1... | collective-permute-start | bytes 786440 | tf_op jit(solution)/shard_map/squares1/ppermute | solution.py:37
  42.1 6.6 %collective-permute-start.22 = (bf16[64,512]{1,0:T(8,128)(2,1)S(1)}, bf16[64,512]{1,0:T(8,128)(2,1)S(1)}, u32[]{:S(2)}, u32[]{:S(2)}) collective-permute-start(bf16[64,512]{1,0:T(8,128)(2,1)S(1)} %fusion.18), channel_id=1, source_target_pairs={{0,6},{1,7},{2,4},{3,5},{4,2},{5,3},{6,0},{7,1},{8,14},{9,15},{10,... | collective-permute-start | bytes 196616 | tf_op jit(solution)/shard_map/residual3/ppermute | solution.py:29
  44.9 5.3 %collective-permute-start.21 = (bf16[64,512]{1,0:T(8,128)(2,1)S(1)}, bf16[64,512]{1,0:T(8,128)(2,1)S(1)}, u32[]{:S(2)}, u32[]{:S(2)}) collective-permute-start(bf16[64,512]{1,0:T(8,128)(2,1)S(1)} %fusion.18), channel_id=1, source_target_pairs={{0,2},{1,3},{2,0},{3,1},{4,6},{5,7},{6,4},{7,5},{8,10},{9,11},{10,... | collective-permute-start | bytes 196616 | tf_op jit(solution)/shard_map/residual1/ppermute | solution.py:29
  44.9 5.3 %collective-permute-start.20 = (bf16[64,512]{1,0:T(8,128)(2,1)S(1)}, bf16[64,512]{1,0:T(8,128)(2,1)S(1)}, u32[]{:S(2)}, u32[]{:S(2)}) collective-permute-start(bf16[64,512]{1,0:T(8,128)(2,1)S(1)} %fusion.18), channel_id=1, source_target_pairs={{0,4},{1,5},{2,6},{3,7},{4,0},{5,1},{6,2},{7,3},{8,12},{9,13},{10,... | collective-permute-start | bytes 196616 | tf_op jit(solution)/shard_map/residual2/ppermute | solution.py:29
  50.5 1.7 %copy-start = (f32[256,512]{1,0:T(8,128)}, f32[256,512]{1,0:T(8,128)S(1)}, u32[]{:S(2)}) copy-start(f32[256,512]{1,0:T(8,128)S(1)} %get-tuple-element.49) | copy-start | bytes 1572868
  50.5 1.7 %copy-start.1 = (f32[256,512]{1,0:T(8,128)}, f32[256,512]{1,0:T(8,128)S(1)}, u32[]{:S(2)}) copy-start(f32[256,512]{1,0:T(8,128)S(1)} %get-tuple-element.50) | copy-start | bytes 1572868
  50.5 1.6 %collective-permute-start.23 = (bf16[256,512]{1,0:T(8,128)(2,1)S(1)}, bf16[256,512]{1,0:T(8,128)(2,1)S(1)}, u32[]{:S(2)}, u32[]{:S(2)}) collective-permute-start(bf16[256,512]{1,0:T(8,128)(2,1)S(1)} %constant_dynamic-update-slice_fusion.4), channel_id=1, source_target_pairs={{0,1},{1,0},{2,3},{3,2},{4,5},{5,4},{6,7},{7,6},{8,9},{9,8},{10,11... | collective-permute-start | bytes 786440 | tf_op jit(solution)/shard_map/residual_core/ppermute | solution.py:24

commit v7 on v6

--- a/solution.py
+++ b/solution.py
@@ -31,7 +31,7 @@
 
 def cond_swap(value, mask, what):
     conds, size = lax.axis_size("cond"), lax.axis_size("shard")
-    masks = (mask, mirrored(mask, bits_of(conds)))
+    masks = (mirrored(mask, bits_of(conds)), mask)
     pairs = [(c * size + i, (c ^ masks[i % 2]) * size + i) for c in range(conds) for i in range(size)]
     with jax.named_scope(what):
         return lax.ppermute(value, ("cond", "shard"), pairs)

time: 53.4 us -> 53.2 us (level)
  transfers between devices with their start and end apart: 24 -> 24, of which waited for: 11 -> 12; matrix products, arithmetic and copies ran while one was open for 7% -> 7% of each run, Pallas kernels for 0% -> 0%
where the time goes in v7:
time: 53.2 us; the launch traced here: 53 us
  starting transfers between devices  30.9 us (58%)
  waiting for transfers between devices  13.3 us (25%)
  matrix products  3.81 us (7%)
  local copies, waits for them, and re-layouts  2.52 us (5%)
  other arithmetic  1.37 us (3%)
  between operations  1.13 us (2%)
    ppermute x15, starting transfers between devices, chip_swap(): lax.ppermute(value, 'shard', [(i, i ^ 2 * mask) for i in range(lax.axis_s...  24.2 us
    ppermute x15, waiting for transfers between devices, chip_swap(): lax.ppermute(value, 'shard', [(i, i ^ 2 * mask) for i in range(lax.axis_s...  11.2 us
    ppermute x4, starting transfers between devices, cond_swap(): return lax.ppermute(value, ('cond', 'shard'), pairs)  6.17 us
    ppermute x5, waiting for transfers between devices, core_swap(): lax.ppermute(value, 'shard', [(i, i ^ 1) for i in range(lax.axis_size('sh...  2.05 us
    dot_general x10, matrix products, dot(): return jnp.dot(x, c, preferred_element_type=f32)  1.75 us
    unnamed x18, local copies, waits for them, and re-layouts  1.39 us
    dot_general x2, matrix products, shards(): lax.dot_general(across, residual_other, contract, preferred_element_type=...  1.32 us
  transfers between devices with their start and end apart: 24, of which 12 were waited for; matrix products, arithmetic and copies ran while one was open for 7% of the time, Pallas kernels for 0%

profile of v7, /device:TPU:0, one launch (start us, length us, event | category | flops | bytes accessed | tf_op | source)
XLA Modules:
  0.0 53.0 jit_solution(15791430886329536095)
XLA Ops:
  0.7 1.0 %constant_dynamic-slice_fusion = (bf16[64,256]{1,0:T(8,128)(2,1)S(1)}, bf16[1,64,256]{2,1,0:T(8,128)(2,1)S(1)}, bf16[1,64,256]{2,1,0:T(8,128)(2,1)S(1)}, bf16[1,...) fusion(bf16[64,2048]{1,0:T(8,128)(2,1)} %param.5, ...), kind=kLoop, calls=%fused_computation.65 | loop fusion | bytes 524320 | tf_op jit(solution)/shard_map/dynamic_slice | solution.py:62
  1.7 5.1 %collective-permute-start = (bf16[2,64,256]{2,1,0:T(8,128)(2,1)S(1)}, bf16[2,64,256]{2,1,0:T(8,128)(2,1)S(1)}, u32[]{:S(2)}, u32[]{:S(2)}) collective-permute-start(bf16[2,64,256]{2,1,0:T(8,128)(2,1)S(1)} %pad_maximum_fusion.2), channel_id=1, source_target_pairs={{0,6},{1,7},{2,4},{3,5},{4,2},{5,3},{6,0},{7,1},{8,14},{9,15},{10,... | collective-permute-start | bytes 196616 | tf_op jit(solution)/shard_map/cells3/ppermute | solution.py:29
  6.9 0.6 %collective-permute-start.3 = (bf16[2,64,256]{2,1,0:T(8,128)(2,1)S(1)}, bf16[2,64,256]{2,1,0:T(8,128)(2,1)S(1)}, u32[]{:S(2)}, u32[]{:S(2)}) collective-permute-start(bf16[2,64,256]{2,1,0:T(8,128)(2,1)S(1)} %pad_maximum_fusion.4), channel_id=1, source_target_pairs={{0,2},{1,3},{2,0},{3,1},{4,6},{5,7},{6,4},{7,5},{8,10},{9,11},{10,... | collective-permute-start | bytes 196616 | tf_op jit(solution)/shard_map/cells1/ppermute | solution.py:29
  7.6 0.1 multiply_convert_fusion.1
  7.8 1.8 %collective-permute-start.4 = (bf16[256,512]{1,0:T(8,128)(2,1)S(1)}, bf16[256,512]{1,0:T(8,128)(2,1)S(1)}, u32[]{:S(2)}, u32[]{:S(2)}) collective-permute-start(bf16[256,512]{1,0:T(8,128)(2,1)S(1)} %get-tuple-element.55), channel_id=1, source_target_pairs={{0,16},{1,9},{2,18},{3,11},{4,20},{5,13},{6,22},{7,15},{8,24},{9,1... | collective-permute-start | bytes 786440 | tf_op jit(solution)/shard_map/squares0/ppermute | solution.py:37
  9.6 0.2 fusion.29
  9.7 0.7 %copy-done.4 = bf16[64,512]{1,0:T(8,128)(2,1)S(1)} copy-done((bf16[64,512]{1,0:T(8,128)(2,1)S(1)}, bf16[64,512]{1,0:T(8,128)(2,1)}, u32[]{:S(2)}) %copy-start.4) | copy-done | bytes 65560
  10.4 0.2 fusion.22
  10.6 0.2 fusion.6
  10.8 3.7 %collective-permute-start.7 = (bf16[64,512]{1,0:T(8,128)(2,1)S(1)}, bf16[64,512]{1,0:T(8,128)(2,1)S(1)}, u32[]{:S(2)}, u32[]{:S(2)}) collective-permute-start(bf16[64,512]{1,0:T(8,128)(2,1)S(1)} %fusion.6), channel_id=1, source_target_pairs={{0,6},{1,7},{2,4},{3,5},{4,2},{5,3},{6,0},{7,1},{8,14},{9,15},{10,... | collective-permute-start | bytes 196616 | tf_op jit(solution)/shard_map/fit3/ppermute | solution.py:29
  14.5 0.2 fusion.20
  14.6 0.2 fusion.7
  14.9 0.2 fusion.21
  15.1 0.2 fusion.8
  15.2 1.3 %collective-permute-start.9 = (bf16[64,512]{1,0:T(8,128)(2,1)S(1)}, bf16[64,512]{1,0:T(8,128)(2,1)S(1)}, u32[]{:S(2)}, u32[]{:S(2)}) collective-permute-start(bf16[64,512]{1,0:T(8,128)(2,1)S(1)} %fusion.8), channel_id=1, source_target_pairs={{0,2},{1,3},{2,0},{3,1},{4,6},{5,7},{6,4},{7,5},{8,10},{9,11},{10,... | collective-permute-start | bytes 196616 | tf_op jit(solution)/shard_map/fit1/ppermute | solution.py:29
  16.7 0.7 %copy-done.5 = f32[256]{0:T(256)S(1)} copy-done((f32[256]{0:T(256)S(1)}, f32[256]{0:T(256)}, u32[]{:S(2)}) %copy-start.5) | copy-done | bytes 1048
  17.5 1.6 %collective-permute-start.5 = (bf16[256,512]{1,0:T(8,128)(2,1)S(1)}, bf16[256,512]{1,0:T(8,128)(2,1)S(1)}, u32[]{:S(2)}, u32[]{:S(2)}) collective-permute-start(bf16[256,512]{1,0:T(8,128)(2,1)S(1)} %convert_element_type.82), channel_id=1, source_target_pairs={{0,8},{1,17},{2,10},{3,19},{4,12},{5,21},{6,14},{7,23},{8,0},{9,25... | collective-permute-start | bytes 786440 | tf_op jit(solution)/shard_map/squares1/ppermute | solution.py:37
  19.1 1.6 %collective-permute-done.9 = bf16[64,512]{1,0:T(8,128)(2,1)S(1)} collective-permute-done((bf16[64,512]{1,0:T(8,128)(2,1)S(1)}, bf16[64,512]{1,0:T(8,128)(2,1)S(1)}, u32[]{:S(2)}, u32[]{:S(2)}) %collective-permute-start.9) | collective-permute-done | bytes 65568 | tf_op jit(solution)/shard_map/fit1/ppermute | solution.py:29
  20.8 0.2 fusion.9
  21.0 2.3 %collective-permute-start.12 = (bf16[64,512]{1,0:T(8,128)(2,1)S(1)}, bf16[64,512]{1,0:T(8,128)(2,1)S(1)}, u32[]{:S(2)}, u32[]{:S(2)}) collective-permute-start(bf16[64,512]{1,0:T(8,128)(2,1)S(1)} %fusion.9), channel_id=1, source_target_pairs={{0,6},{1,7},{2,4},{3,5},{4,2},{5,3},{6,0},{7,1},{8,14},{9,15},{10,... | collective-permute-start | bytes 196616 | tf_op jit(solution)/shard_map/residual3/ppermute | solution.py:29
  23.3 2.1 %collective-permute-start.10 = (bf16[64,512]{1,0:T(8,128)(2,1)S(1)}, bf16[64,512]{1,0:T(8,128)(2,1)S(1)}, u32[]{:S(2)}, u32[]{:S(2)}) collective-permute-start(bf16[64,512]{1,0:T(8,128)(2,1)S(1)} %fusion.9), channel_id=1, source_target_pairs={{0,4},{1,5},{2,6},{3,7},{4,0},{5,1},{6,2},{7,3},{8,12},{9,13},{10,... | collective-permute-start | bytes 196616 | tf_op jit(solution)/shard_map/residual2/ppermute | solution.py:29
  25.6 2.0 %collective-permute-done.12 = bf16[64,512]{1,0:T(8,128)(2,1)S(1)} collective-permute-done((bf16[64,512]{1,0:T(8,128)(2,1)S(1)}, bf16[64,512]{1,0:T(8,128)(2,1)S(1)}, u32[]{:S(2)}, u32[]{:S(2)}) %collective-permute-start.12) | collective-permute-done | bytes 65568 | tf_op jit(solution)/shard_map/residual3/ppermute | solution.py:29
  27.6 0.5 collective-permute-done.11
  28.1 0.7 %collective-permute-done.10 = bf16[64,512]{1,0:T(8,128)(2,1)S(1)} collective-permute-done((bf16[64,512]{1,0:T(8,128)(2,1)S(1)}, bf16[64,512]{1,0:T(8,128)(2,1)S(1)}, u32[]{:S(2)}, u32[]{:S(2)}) %collective-permute-start.10) | collective-permute-done | bytes 65568 | tf_op jit(solution)/shard_map/residual2/ppermute | solution.py:29
  29.0 0.5 fusion.1
  29.5 0.2 fusion.19
  29.7 0.8 %collective-permute-done.13 = bf16[256,512]{1,0:T(8,128)(2,1)S(1)} collective-permute-done((bf16[256,512]{1,0:T(8,128)(2,1)S(1)}, bf16[256,512]{1,0:T(8,128)(2,1)S(1)}, u32[]{:S(2)}, u32[]{:S(2)}) %collective-permute-start.13) | collective-permute-done | bytes 262176 | tf_op jit(solution)/shard_map/residual_core/ppermute | solution.py:24
  30.5 0.2 convolution_multiply_fusion.2
  30.9 0.2 collective-permute-start.16
  31.2 1.9 %collective-permute-start.14 = (bf16[256,512]{1,0:T(8,128)(2,1)S(1)}, bf16[256,512]{1,0:T(8,128)(2,1)S(1)}, u32[]{:S(2)}, u32[]{:S(2)}) collective-permute-start(bf16[256,512]{1,0:T(8,128)(2,1)S(1)} %get-tuple-element.53), channel_id=1, source_target_pairs={{0,16},{1,9},{2,18},{3,11},{4,20},{5,13},{6,22},{7,15},{8,24},{9,1... | collective-permute-start | bytes 786440 | tf_op jit(solution)/shard_map/squares0/ppermute | solution.py:37
  33.1 0.2 fusion.23
  33.3 0.2 fusion.28
  33.5 2.6 %collective-permute-start.17 = (bf16[64,512]{1,0:T(8,128)(2,1)S(1)}, bf16[64,512]{1,0:T(8,128)(2,1)S(1)}, u32[]{:S(2)}, u32[]{:S(2)}) collective-permute-start(bf16[64,512]{1,0:T(8,128)(2,1)S(1)} %get-tuple-element.58), channel_id=1, source_target_pairs={{0,6},{1,7},{2,4},{3,5},{4,2},{5,3},{6,0},{7,1},{8,14},{9,15},{10,... | collective-permute-start | bytes 196616 | tf_op jit(solution)/shard_map/fit3/ppermute | solution.py:29
  36.1 1.9 %collective-permute-start.18 = (bf16[64,512]{1,0:T(8,128)(2,1)S(1)}, bf16[64,512]{1,0:T(8,128)(2,1)S(1)}, u32[]{:S(2)}, u32[]{:S(2)}) collective-permute-start(bf16[64,512]{1,0:T(8,128)(2,1)S(1)} %get-tuple-element.60), channel_id=1, source_target_pairs={{0,4},{1,5},{2,6},{3,7},{4,0},{5,1},{6,2},{7,3},{8,12},{9,13},{10,... | collective-permute-start | bytes 196616 | tf_op jit(solution)/shard_map/fit2/ppermute | solution.py:29
  38.1 0.9 %collective-permute-start.15 = (bf16[256,512]{1,0:T(8,128)(2,1)S(1)}, bf16[256,512]{1,0:T(8,128)(2,1)S(1)}, u32[]{:S(2)}, u32[]{:S(2)}) collective-permute-start(bf16[256,512]{1,0:T(8,128)(2,1)S(1)} %fusion.14), channel_id=1, source_target_pairs={{0,8},{1,17},{2,10},{3,19},{4,12},{5,21},{6,14},{7,23},{8,0},{9,25... | collective-permute-start | bytes 786440 | tf_op jit(solution)/shard_map/squares1/ppermute | solution.py:37
  39.0 0.8 %collective-permute-done.17 = bf16[64,512]{1,0:T(8,128)(2,1)S(1)} collective-permute-done((bf16[64,512]{1,0:T(8,128)(2,1)S(1)}, bf16[64,512]{1,0:T(8,128)(2,1)S(1)}, u32[]{:S(2)}, u32[]{:S(2)}) %collective-permute-start.17) | collective-permute-done | bytes 65568 | tf_op jit(solution)/shard_map/fit3/ppermute | solution.py:29
  39.8 1.8 %collective-permute-done.19 = bf16[64,512]{1,0:T(8,128)(2,1)S(1)} collective-permute-done((bf16[64,512]{1,0:T(8,128)(2,1)S(1)}, bf16[64,512]{1,0:T(8,128)(2,1)S(1)}, u32[]{:S(2)}, u32[]{:S(2)}) %collective-permute-start.19) | collective-permute-done | bytes 65568 | tf_op jit(solution)/shard_map/fit1/ppermute | solution.py:29
  41.6 0.4 collective-permute-done.18
  42.1 2.1 %collective-permute-start.22 = (bf16[64,512]{1,0:T(8,128)(2,1)S(1)}, bf16[64,512]{1,0:T(8,128)(2,1)S(1)}, u32[]{:S(2)}, u32[]{:S(2)}) collective-permute-start(bf16[64,512]{1,0:T(8,128)(2,1)S(1)} %fusion.18), channel_id=1, source_target_pairs={{0,6},{1,7},{2,4},{3,5},{4,2},{5,3},{6,0},{7,1},{8,14},{9,15},{10,... | collective-permute-start | bytes 196616 | tf_op jit(solution)/shard_map/residual3/ppermute | solution.py:29
  44.2 0.4 collective-permute-start.21
  44.6 1.9 %collective-permute-start.20 = (bf16[64,512]{1,0:T(8,128)(2,1)S(1)}, bf16[64,512]{1,0:T(8,128)(2,1)S(1)}, u32[]{:S(2)}, u32[]{:S(2)}) collective-permute-start(bf16[64,512]{1,0:T(8,128)(2,1)S(1)} %fusion.18), channel_id=1, source_target_pairs={{0,4},{1,5},{2,6},{3,7},{4,0},{5,1},{6,2},{7,3},{8,12},{9,13},{10,... | collective-permute-start | bytes 196616 | tf_op jit(solution)/shard_map/residual2/ppermute | solution.py:29
  46.6 2.1 %collective-permute-done.22 = bf16[64,512]{1,0:T(8,128)(2,1)S(1)} collective-permute-done((bf16[64,512]{1,0:T(8,128)(2,1)S(1)}, bf16[64,512]{1,0:T(8,128)(2,1)S(1)}, u32[]{:S(2)}, u32[]{:S(2)}) %collective-permute-start.22) | collective-permute-done | bytes 65568 | tf_op jit(solution)/shard_map/residual3/ppermute | solution.py:29
  48.7 0.5 collective-permute-done.21
  49.2 0.7 %collective-permute-done.20 = bf16[64,512]{1,0:T(8,128)(2,1)S(1)} collective-permute-done((bf16[64,512]{1,0:T(8,128)(2,1)S(1)}, bf16[64,512]{1,0:T(8,128)(2,1)S(1)}, u32[]{:S(2)}, u32[]{:S(2)}) %collective-permute-start.20) | collective-permute-done | bytes 65568 | tf_op jit(solution)/shard_map/residual2/ppermute | solution.py:29
  49.9 0.2 fusion.24
  50.4 0.3 convolution_multiply_fusion.1
  50.6 1.2 %collective-permute-done.23 = bf16[256,512]{1,0:T(8,128)(2,1)S(1)} collective-permute-done((bf16[256,512]{1,0:T(8,128)(2,1)S(1)}, bf16[256,512]{1,0:T(8,128)(2,1)S(1)}, u32[]{:S(2)}, u32[]{:S(2)}) %collective-permute-start.23) | collective-permute-done | bytes 262176 | tf_op jit(solution)/shard_map/residual_core/ppermute | solution.py:24
  51.9 1.1 %fusion = f32[256,512]{1,0:T(8,128)} fusion(bf16[256,256]{1,0:T(8,128)(2,1)S(1)} %collective-permute-done.6, bf16[256,512]{1,0:T(8,128)(2,1)S(1)} %collective-permute-done.23, f32[256,512]{1,0:T(8,128)S(1)} %convolution_multiply_fusion.1, f32[256,512]{1,0:T(8,128)S(1)} %get-tuple-element.52, f32[256,512]{1,0:T(8,128)S(1)} %get-tuple-element.50, ...), kind=kOutput, calls=%fused_computation.1 | convolution fusion | flops 68288512 | bytes 3016704 | tf_op jit(solution)/shard_map/dot_general | solution.py:126
  (61 shorter events, 1.4 us)
Async XLA Ops:
  0.6 6.9 %copy-start.2 = (f32[256,512]{1,0:T(8,128)S(1)}, f32[256,512]{1,0:T(8,128)}, u32[]{:S(2)}) copy-start(f32[256,512]{1,0:T(8,128)} %param.8) | copy-start | bytes 1572868
  0.6 6.9 %copy-start.3 = (f32[256,512]{1,0:T(8,128)S(1)}, f32[256,512]{1,0:T(8,128)}, u32[]{:S(2)}) copy-start(f32[256,512]{1,0:T(8,128)} %param.7) | copy-start | bytes 1572868
  1.7 8.7 %collective-permute-start = (bf16[2,64,256]{2,1,0:T(8,128)(2,1)S(1)}, bf16[2,64,256]{2,1,0:T(8,128)(2,1)S(1)}, u32[]{:S(2)}, u32[]{:S(2)}) collective-permute-start(bf16[2,64,256]{2,1,0:T(8,128)(2,1)S(1)} %pad_maximum_fusion.2), channel_id=1, source_target_pairs={{0,6},{1,7},{2,4},{3,5},{4,2},{5,3},{6,0},{7,1},{8,14},{9,15},{10,... | collective-permute-start | bytes 196616 | tf_op jit(solution)/shard_map/cells3/ppermute | solution.py:29
  6.8 7.6 %collective-permute-start.1 = (bf16[2,64,256]{2,1,0:T(8,128)(2,1)S(1)}, bf16[2,64,256]{2,1,0:T(8,128)(2,1)S(1)}, u32[]{:S(2)}, u32[]{:S(2)}) collective-permute-start(bf16[2,64,256]{2,1,0:T(8,128)(2,1)S(1)} %pad_maximum_fusion.3), channel_id=1, source_target_pairs={{0,4},{1,5},{2,6},{3,7},{4,0},{5,1},{6,2},{7,3},{8,12},{9,13},{10,... | collective-permute-start | bytes 196616 | tf_op jit(solution)/shard_map/cells2/ppermute | solution.py:29
  6.9 8.0 %collective-permute-start.3 = (bf16[2,64,256]{2,1,0:T(8,128)(2,1)S(1)}, bf16[2,64,256]{2,1,0:T(8,128)(2,1)S(1)}, u32[]{:S(2)}, u32[]{:S(2)}) collective-permute-start(bf16[2,64,256]{2,1,0:T(8,128)(2,1)S(1)} %pad_maximum_fusion.4), channel_id=1, source_target_pairs={{0,2},{1,3},{2,0},{3,1},{4,6},{5,7},{6,4},{7,5},{8,10},{9,11},{10,... | collective-permute-start | bytes 196616 | tf_op jit(solution)/shard_map/cells1/ppermute | solution.py:29
  7.7 2.7 %collective-permute-start.2 = (bf16[256,512]{1,0:T(8,128)(2,1)S(1)}, bf16[256,512]{1,0:T(8,128)(2,1)S(1)}, u32[]{:S(2)}, u32[]{:S(2)}) collective-permute-start(bf16[256,512]{1,0:T(8,128)(2,1)S(1)} %get-tuple-element.57), channel_id=1, source_target_pairs={{0,1},{1,0},{2,3},{3,2},{4,5},{5,4},{6,7},{7,6},{8,9},{9,8},{10,11... | collective-permute-start | bytes 786440 | tf_op jit(solution)/shard_map/coef_core/ppermute | solution.py:24
  7.8 8.8 %collective-permute-start.4 = (bf16[256,512]{1,0:T(8,128)(2,1)S(1)}, bf16[256,512]{1,0:T(8,128)(2,1)S(1)}, u32[]{:S(2)}, u32[]{:S(2)}) collective-permute-start(bf16[256,512]{1,0:T(8,128)(2,1)S(1)} %get-tuple-element.55), channel_id=1, source_target_pairs={{0,16},{1,9},{2,18},{3,11},{4,20},{5,13},{6,22},{7,15},{8,24},{9,1... | collective-permute-start | bytes 786440 | tf_op jit(solution)/shard_map/squares0/ppermute | solution.py:37
  9.6 0.8 %copy-start.4 = (bf16[64,512]{1,0:T(8,128)(2,1)S(1)}, bf16[64,512]{1,0:T(8,128)(2,1)}, u32[]{:S(2)}) copy-start(bf16[64,512]{1,0:T(8,128)(2,1)} %param.6) | copy-start | bytes 196612
  10.8 8.4 %collective-permute-start.7 = (bf16[64,512]{1,0:T(8,128)(2,1)S(1)}, bf16[64,512]{1,0:T(8,128)(2,1)S(1)}, u32[]{:S(2)}, u32[]{:S(2)}) collective-permute-start(bf16[64,512]{1,0:T(8,128)(2,1)S(1)} %fusion.6), channel_id=1, source_target_pairs={{0,6},{1,7},{2,4},{3,5},{4,2},{5,3},{6,0},{7,1},{8,14},{9,15},{10,... | collective-permute-start | bytes 196616 | tf_op jit(solution)/shard_map/fit3/ppermute | solution.py:29
  14.8 6.0 %collective-permute-start.8 = (bf16[64,512]{1,0:T(8,128)(2,1)S(1)}, bf16[64,512]{1,0:T(8,128)(2,1)S(1)}, u32[]{:S(2)}, u32[]{:S(2)}) collective-permute-start(bf16[64,512]{1,0:T(8,128)(2,1)S(1)} %fusion.7), channel_id=1, source_target_pairs={{0,4},{1,5},{2,6},{3,7},{4,0},{5,1},{6,2},{7,3},{8,12},{9,13},{10,... | collective-permute-start | bytes 196616 | tf_op jit(solution)/shard_map/fit2/ppermute | solution.py:29
  15.2 5.5 %collective-permute-start.9 = (bf16[64,512]{1,0:T(8,128)(2,1)S(1)}, bf16[64,512]{1,0:T(8,128)(2,1)S(1)}, u32[]{:S(2)}, u32[]{:S(2)}) collective-permute-start(bf16[64,512]{1,0:T(8,128)(2,1)S(1)} %fusion.8), channel_id=1, source_target_pairs={{0,2},{1,3},{2,0},{3,1},{4,6},{5,7},{6,4},{7,5},{8,10},{9,11},{10,... | collective-permute-start | bytes 196616 | tf_op jit(solution)/shard_map/fit1/ppermute | solution.py:29
  16.6 0.7 %copy-start.5 = (f32[256]{0:T(256)S(1)}, f32[256]{0:T(256)}, u32[]{:S(2)}) copy-start(f32[256]{0:T(256)} %param.9) | copy-start | bytes 3076
  17.4 8.0 %collective-permute-start.6 = (bf16[256,256]{1,0:T(8,128)(2,1)S(1)}, bf16[256,256]{1,0:T(8,128)(2,1)S(1)}, u32[]{:S(2)}, u32[]{:S(2)}) collective-permute-start(bf16[256,256]{1,0:T(8,128)(2,1)S(1)} %pad_maximum_fusion), channel_id=1, source_target_pairs={{0,1},{1,0},{2,3},{3,2},{4,5},{5,4},{6,7},{7,6},{8,9},{9,8},{10,11... | collective-permute-start | bytes 393224 | tf_op jit(solution)/shard_map/cells_core/ppermute | solution.py:24
  17.5 8.0 %collective-permute-start.5 = (bf16[256,512]{1,0:T(8,128)(2,1)S(1)}, bf16[256,512]{1,0:T(8,128)(2,1)S(1)}, u32[]{:S(2)}, u32[]{:S(2)}) collective-permute-start(bf16[256,512]{1,0:T(8,128)(2,1)S(1)} %convert_element_type.82), channel_id=1, source_target_pairs={{0,8},{1,17},{2,10},{3,19},{4,12},{5,21},{6,14},{7,23},{8,0},{9,25... | collective-permute-start | bytes 786440 | tf_op jit(solution)/shard_map/squares1/ppermute | solution.py:37
  21.0 6.7 %collective-permute-start.12 = (bf16[64,512]{1,0:T(8,128)(2,1)S(1)}, bf16[64,512]{1,0:T(8,128)(2,1)S(1)}, u32[]{:S(2)}, u32[]{:S(2)}) collective-permute-start(bf16[64,512]{1,0:T(8,128)(2,1)S(1)} %fusion.9), channel_id=1, source_target_pairs={{0,6},{1,7},{2,4},{3,5},{4,2},{5,3},{6,0},{7,1},{8,14},{9,15},{10,... | collective-permute-start | bytes 196616 | tf_op jit(solution)/shard_map/residual3/ppermute | solution.py:29
  23.3 4.8 %collective-permute-start.11 = (bf16[64,512]{1,0:T(8,128)(2,1)S(1)}, bf16[64,512]{1,0:T(8,128)(2,1)S(1)}, u32[]{:S(2)}, u32[]{:S(2)}) collective-permute-start(bf16[64,512]{1,0:T(8,128)(2,1)S(1)} %fusion.9), channel_id=1, source_target_pairs={{0,2},{1,3},{2,0},{3,1},{4,6},{5,7},{6,4},{7,5},{8,10},{9,11},{10,... | collective-permute-start | bytes 196616 | tf_op jit(solution)/shard_map/residual1/ppermute | solution.py:29
  23.3 5.6 %collective-permute-start.10 = (bf16[64,512]{1,0:T(8,128)(2,1)S(1)}, bf16[64,512]{1,0:T(8,128)(2,1)S(1)}, u32[]{:S(2)}, u32[]{:S(2)}) collective-permute-start(bf16[64,512]{1,0:T(8,128)(2,1)S(1)} %fusion.9), channel_id=1, source_target_pairs={{0,4},{1,5},{2,6},{3,7},{4,0},{5,1},{6,2},{7,3},{8,12},{9,13},{10,... | collective-permute-start | bytes 196616 | tf_op jit(solution)/shard_map/residual2/ppermute | solution.py:29
  28.9 1.6 %collective-permute-start.13 = (bf16[256,512]{1,0:T(8,128)(2,1)S(1)}, bf16[256,512]{1,0:T(8,128)(2,1)S(1)}, u32[]{:S(2)}, u32[]{:S(2)}) collective-permute-start(bf16[256,512]{1,0:T(8,128)(2,1)S(1)} %constant_dynamic-update-slice_fusion), channel_id=1, source_target_pairs={{0,1},{1,0},{2,3},{3,2},{4,5},{5,4},{6,7},{7,6},{8,9},{9,8},{10,11... | collective-permute-start | bytes 786440 | tf_op jit(solution)/shard_map/residual_core/ppermute | solution.py:24
  30.9 2.4 %collective-permute-start.16 = (bf16[256,512]{1,0:T(8,128)(2,1)S(1)}, bf16[256,512]{1,0:T(8,128)(2,1)S(1)}, u32[]{:S(2)}, u32[]{:S(2)}) collective-permute-start(bf16[256,512]{1,0:T(8,128)(2,1)S(1)} %get-tuple-element.51), channel_id=1, source_target_pairs={{0,1},{1,0},{2,3},{3,2},{4,5},{5,4},{6,7},{7,6},{8,9},{9,8},{10,11... | collective-permute-start | bytes 786440 | tf_op jit(solution)/shard_map/coef_core/ppermute | solution.py:24
  31.2 6.8 %collective-permute-start.14 = (bf16[256,512]{1,0:T(8,128)(2,1)S(1)}, bf16[256,512]{1,0:T(8,128)(2,1)S(1)}, u32[]{:S(2)}, u32[]{:S(2)}) collective-permute-start(bf16[256,512]{1,0:T(8,128)(2,1)S(1)} %get-tuple-element.53), channel_id=1, source_target_pairs={{0,16},{1,9},{2,18},{3,11},{4,20},{5,13},{6,22},{7,15},{8,24},{9,1... | collective-permute-start | bytes 786440 | tf_op jit(solution)/shard_map/squares0/ppermute | solution.py:37
  33.5 6.3 %collective-permute-start.17 = (bf16[64,512]{1,0:T(8,128)(2,1)S(1)}, bf16[64,512]{1,0:T(8,128)(2,1)S(1)}, u32[]{:S(2)}, u32[]{:S(2)}) collective-permute-start(bf16[64,512]{1,0:T(8,128)(2,1)S(1)} %get-tuple-element.58), channel_id=1, source_target_pairs={{0,6},{1,7},{2,4},{3,5},{4,2},{5,3},{6,0},{7,1},{8,14},{9,15},{10,... | collective-permute-start | bytes 196616 | tf_op jit(solution)/shard_map/fit3/ppermute | solution.py:29
  36.1 5.5 %collective-permute-start.19 = (bf16[64,512]{1,0:T(8,128)(2,1)S(1)}, bf16[64,512]{1,0:T(8,128)(2,1)S(1)}, u32[]{:S(2)}, u32[]{:S(2)}) collective-permute-start(bf16[64,512]{1,0:T(8,128)(2,1)S(1)} %get-tuple-element.59), channel_id=1, source_target_pairs={{0,2},{1,3},{2,0},{3,1},{4,6},{5,7},{6,4},{7,5},{8,10},{9,11},{10,... | collective-permute-start | bytes 196616 | tf_op jit(solution)/shard_map/fit1/ppermute | solution.py:29
  36.1 5.9 %collective-permute-start.18 = (bf16[64,512]{1,0:T(8,128)(2,1)S(1)}, bf16[64,512]{1,0:T(8,128)(2,1)S(1)}, u32[]{:S(2)}, u32[]{:S(2)}) collective-permute-start(bf16[64,512]{1,0:T(8,128)(2,1)S(1)} %get-tuple-element.60), channel_id=1, source_target_pairs={{0,4},{1,5},{2,6},{3,7},{4,0},{5,1},{6,2},{7,3},{8,12},{9,13},{10,... | collective-permute-start | bytes 196616 | tf_op jit(solution)/shard_map/fit2/ppermute | solution.py:29
  38.1 8.4 %collective-permute-start.15 = (bf16[256,512]{1,0:T(8,128)(2,1)S(1)}, bf16[256,512]{1,0:T(8,128)(2,1)S(1)}, u32[]{:S(2)}, u32[]{:S(2)}) collective-permute-start(bf16[256,512]{1,0:T(8,128)(2,1)S(1)} %fusion.14), channel_id=1, source_target_pairs={{0,8},{1,17},{2,10},{3,19},{4,12},{5,21},{6,14},{7,23},{8,0},{9,25... | collective-permute-start | bytes 786440 | tf_op jit(solution)/shard_map/squares1/ppermute | solution.py:37
  42.1 6.7 %collective-permute-start.22 = (bf16[64,512]{1,0:T(8,128)(2,1)S(1)}, bf16[64,512]{1,0:T(8,128)(2,1)S(1)}, u32[]{:S(2)}, u32[]{:S(2)}) collective-permute-start(bf16[64,512]{1,0:T(8,128)(2,1)S(1)} %fusion.18), channel_id=1, source_target_pairs={{0,6},{1,7},{2,4},{3,5},{4,2},{5,3},{6,0},{7,1},{8,14},{9,15},{10,... | collective-permute-start | bytes 196616 | tf_op jit(solution)/shard_map/residual3/ppermute | solution.py:29
  44.2 5.0 %collective-permute-start.21 = (bf16[64,512]{1,0:T(8,128)(2,1)S(1)}, bf16[64,512]{1,0:T(8,128)(2,1)S(1)}, u32[]{:S(2)}, u32[]{:S(2)}) collective-permute-start(bf16[64,512]{1,0:T(8,128)(2,1)S(1)} %fusion.18), channel_id=1, source_target_pairs={{0,2},{1,3},{2,0},{3,1},{4,6},{5,7},{6,4},{7,5},{8,10},{9,11},{10,... | collective-permute-start | bytes 196616 | tf_op jit(solution)/shard_map/residual1/ppermute | solution.py:29
  44.6 5.4 %collective-permute-start.20 = (bf16[64,512]{1,0:T(8,128)(2,1)S(1)}, bf16[64,512]{1,0:T(8,128)(2,1)S(1)}, u32[]{:S(2)}, u32[]{:S(2)}) collective-permute-start(bf16[64,512]{1,0:T(8,128)(2,1)S(1)} %fusion.18), channel_id=1, source_target_pairs={{0,4},{1,5},{2,6},{3,7},{4,0},{5,1},{6,2},{7,3},{8,12},{9,13},{10,... | collective-permute-start | bytes 196616 | tf_op jit(solution)/shard_map/residual2/ppermute | solution.py:29
  50.2 1.7 %copy-start = (f32[256,512]{1,0:T(8,128)}, f32[256,512]{1,0:T(8,128)S(1)}, u32[]{:S(2)}) copy-start(f32[256,512]{1,0:T(8,128)S(1)} %get-tuple-element.49) | copy-start | bytes 1572868
  50.2 1.7 %copy-start.1 = (f32[256,512]{1,0:T(8,128)}, f32[256,512]{1,0:T(8,128)S(1)}, u32[]{:S(2)}) copy-start(f32[256,512]{1,0:T(8,128)S(1)} %get-tuple-element.50) | copy-start | bytes 1572868
  50.3 1.6 %collective-permute-start.23 = (bf16[256,512]{1,0:T(8,128)(2,1)S(1)}, bf16[256,512]{1,0:T(8,128)(2,1)S(1)}, u32[]{:S(2)}, u32[]{:S(2)}) collective-permute-start(bf16[256,512]{1,0:T(8,128)(2,1)S(1)} %constant_dynamic-update-slice_fusion.4), channel_id=1, source_target_pairs={{0,1},{1,0},{2,3},{3,2},{4,5},{5,4},{6,7},{7,6},{8,9},{9,8},{10,11... | collective-permute-start | bytes 786440 | tf_op jit(solution)/shard_map/residual_core/ppermute | solution.py:24

commit v8 on v6

--- a/solution.py
+++ b/solution.py
@@ -91,7 +91,7 @@
         if cond_bits > 0:
             squares = squares + cond_swap(squares.astype(bf16), 1, "squares0").astype(f32)
         if step == 0:
-            held, squares, weights, response_rows, *_ = together(other, squares, weights, response_rows, *before)
+            held, squares, response_rows, *_ = together(other, squares, response_rows, *before)
         else:
             coef_copy = coef.astype(bf16)
             coef_other = core_swap(coef_copy, "coef_core")
@@ -111,7 +111,7 @@
             across = core_swap(held, "cells_core")
             diagonal = jnp.sum(jnp.square(own.astype(f32)), 0) + jnp.sum(jnp.square(across.astype(f32)), 0)
             step_size = 1.0 / (diagonal / n_cells + rho_weight)[:, None]
-        squares, step_size, across, *ready = together(squares, step_size, across, *[residual[k] for k in evens_first])
+        squares, step_size, across, weights, *ready = together(squares, step_size, across, weights, *[residual[k] for k in evens_first])
         residual = dict(zip(evens_first, ready))
         residual = jnp.concatenate([residual[k] for k in order])
         residual_other = core_swap(residual, "residual_core")

time: 53.4 us -> 52.9 us (level)
  local copies, waits for them, and re-layouts: 2.52 us -> 1.87 us
    unnamed x18, local copies, waits for them, and re-layouts: 1.39 us -> 0.74 us
    ppermute x15, waiting for transfers between devices: 11.5 us -> 12.1 us  [chip_swap(): lax.ppermute(value, 'shard', [(i, i ^ 2 * mask) for i in range(lax.axis_s...]
  transfers between devices with their start and end apart: 24 -> 24, of which waited for: 11 -> 12; matrix products, arithmetic and copies ran while one was open for 7% -> 7% of each run, Pallas kernels for 0% -> 0%
where the time goes in v8:
time: 52.9 us; the launch traced here: 52.7 us
  starting transfers between devices  30.6 us (58%)
  waiting for transfers between devices  13.9 us (26%)
  matrix products  3.82 us (7%)
  local copies, waits for them, and re-layouts  1.87 us (4%)
  other arithmetic  1.37 us (3%)
  between operations  1.13 us (2%)
    ppermute x15, starting transfers between devices, chip_swap(): lax.ppermute(value, 'shard', [(i, i ^ 2 * mask) for i in range(lax.axis_s...  24.2 us
    ppermute x15, waiting for transfers between devices, chip_swap(): lax.ppermute(value, 'shard', [(i, i ^ 2 * mask) for i in range(lax.axis_s...  12.1 us
    ppermute x4, starting transfers between devices, cond_swap(): return lax.ppermute(value, ('cond', 'shard'), pairs)  5.88 us
    ppermute x5, waiting for transfers between devices, core_swap(): lax.ppermute(value, 'shard', [(i, i ^ 1) for i in range(lax.axis_size('sh...  1.77 us
    dot_general x10, matrix products, dot(): return jnp.dot(x, c, preferred_element_type=f32)  1.76 us
    dot_general x2, matrix products, shards(): lax.dot_general(across, residual_other, contract, preferred_element_type=...  1.32 us
  transfers between devices with their start and end apart: 24, of which 12 were waited for; matrix products, arithmetic and copies ran while one was open for 7% of the time, Pallas kernels for 0%

profile of v8, /device:TPU:0, one launch (start us, length us, event | category | flops | bytes accessed | tf_op | source)
XLA Modules:
  0.0 52.7 jit_solution(10779621246433034005)
XLA Ops:
  0.7 1.0 %constant_dynamic-slice_fusion = (bf16[64,256]{1,0:T(8,128)(2,1)S(1)}, bf16[1,64,256]{2,1,0:T(8,128)(2,1)S(1)}, bf16[1,64,256]{2,1,0:T(8,128)(2,1)S(1)}, bf16[1,...) fusion(bf16[64,2048]{1,0:T(8,128)(2,1)} %param.5, ...), kind=kLoop, calls=%fused_computation.65 | loop fusion | bytes 524320 | tf_op jit(solution)/shard_map/dynamic_slice | solution.py:62
  1.7 5.1 %collective-permute-start = (bf16[2,64,256]{2,1,0:T(8,128)(2,1)S(1)}, bf16[2,64,256]{2,1,0:T(8,128)(2,1)S(1)}, u32[]{:S(2)}, u32[]{:S(2)}) collective-permute-start(bf16[2,64,256]{2,1,0:T(8,128)(2,1)S(1)} %pad_maximum_fusion.2), channel_id=1, source_target_pairs={{0,6},{1,7},{2,4},{3,5},{4,2},{5,3},{6,0},{7,1},{8,14},{9,15},{10,... | collective-permute-start | bytes 196616 | tf_op jit(solution)/shard_map/cells3/ppermute | solution.py:29
  6.9 0.6 %collective-permute-start.3 = (bf16[2,64,256]{2,1,0:T(8,128)(2,1)S(1)}, bf16[2,64,256]{2,1,0:T(8,128)(2,1)S(1)}, u32[]{:S(2)}, u32[]{:S(2)}) collective-permute-start(bf16[2,64,256]{2,1,0:T(8,128)(2,1)S(1)} %pad_maximum_fusion.4), channel_id=1, source_target_pairs={{0,2},{1,3},{2,0},{3,1},{4,6},{5,7},{6,4},{7,5},{8,10},{9,11},{10,... | collective-permute-start | bytes 196616 | tf_op jit(solution)/shard_map/cells1/ppermute | solution.py:29
  7.6 0.1 multiply_convert_fusion.1
  7.8 1.8 %collective-permute-start.4 = (bf16[256,512]{1,0:T(8,128)(2,1)S(1)}, bf16[256,512]{1,0:T(8,128)(2,1)S(1)}, u32[]{:S(2)}, u32[]{:S(2)}) collective-permute-start(bf16[256,512]{1,0:T(8,128)(2,1)S(1)} %get-tuple-element.57), channel_id=1, source_target_pairs={{0,8},{1,17},{2,10},{3,19},{4,12},{5,21},{6,14},{7,23},{8,0},{9,25... | collective-permute-start | bytes 786440 | tf_op jit(solution)/shard_map/squares0/ppermute | solution.py:37
  9.5 0.2 fusion.29
  9.7 0.7 %copy-done.4 = bf16[64,512]{1,0:T(8,128)(2,1)S(1)} copy-done((bf16[64,512]{1,0:T(8,128)(2,1)S(1)}, bf16[64,512]{1,0:T(8,128)(2,1)}, u32[]{:S(2)}) %copy-start.4) | copy-done | bytes 65560
  10.4 0.2 fusion.22
  10.6 0.2 fusion.6
  10.8 3.7 %collective-permute-start.7 = (bf16[64,512]{1,0:T(8,128)(2,1)S(1)}, bf16[64,512]{1,0:T(8,128)(2,1)S(1)}, u32[]{:S(2)}, u32[]{:S(2)}) collective-permute-start(bf16[64,512]{1,0:T(8,128)(2,1)S(1)} %fusion.6), channel_id=1, source_target_pairs={{0,6},{1,7},{2,4},{3,5},{4,2},{5,3},{6,0},{7,1},{8,14},{9,15},{10,... | collective-permute-start | bytes 196616 | tf_op jit(solution)/shard_map/fit3/ppermute | solution.py:29
  14.4 0.2 fusion.20
  14.6 0.2 fusion.7
  14.9 0.2 fusion.21
  15.0 0.2 fusion.8
  15.2 1.3 %collective-permute-start.9 = (bf16[64,512]{1,0:T(8,128)(2,1)S(1)}, bf16[64,512]{1,0:T(8,128)(2,1)S(1)}, u32[]{:S(2)}, u32[]{:S(2)}) collective-permute-start(bf16[64,512]{1,0:T(8,128)(2,1)S(1)} %fusion.8), channel_id=1, source_target_pairs={{0,2},{1,3},{2,0},{3,1},{4,6},{5,7},{6,4},{7,5},{8,10},{9,11},{10,... | collective-permute-start | bytes 196616 | tf_op jit(solution)/shard_map/fit1/ppermute | solution.py:29
  16.8 1.6 %collective-permute-start.5 = (bf16[256,512]{1,0:T(8,128)(2,1)S(1)}, bf16[256,512]{1,0:T(8,128)(2,1)S(1)}, u32[]{:S(2)}, u32[]{:S(2)}) collective-permute-start(bf16[256,512]{1,0:T(8,128)(2,1)S(1)} %convert_element_type.82), channel_id=1, source_target_pairs={{0,16},{1,9},{2,18},{3,11},{4,20},{5,13},{6,22},{7,15},{8,24},{9,1... | collective-permute-start | bytes 786440 | tf_op jit(solution)/shard_map/squares1/ppermute | solution.py:37
  18.4 2.3 %collective-permute-done.9 = bf16[64,512]{1,0:T(8,128)(2,1)S(1)} collective-permute-done((bf16[64,512]{1,0:T(8,128)(2,1)S(1)}, bf16[64,512]{1,0:T(8,128)(2,1)S(1)}, u32[]{:S(2)}, u32[]{:S(2)}) %collective-permute-start.9) | collective-permute-done | bytes 65568 | tf_op jit(solution)/shard_map/fit1/ppermute | solution.py:29
  20.8 0.2 fusion.9
  21.0 2.3 %collective-permute-start.12 = (bf16[64,512]{1,0:T(8,128)(2,1)S(1)}, bf16[64,512]{1,0:T(8,128)(2,1)S(1)}, u32[]{:S(2)}, u32[]{:S(2)}) collective-permute-start(bf16[64,512]{1,0:T(8,128)(2,1)S(1)} %fusion.9), channel_id=1, source_target_pairs={{0,6},{1,7},{2,4},{3,5},{4,2},{5,3},{6,0},{7,1},{8,14},{9,15},{10,... | collective-permute-start | bytes 196616 | tf_op jit(solution)/shard_map/residual3/ppermute | solution.py:29
  23.2 2.2 %collective-permute-start.10 = (bf16[64,512]{1,0:T(8,128)(2,1)S(1)}, bf16[64,512]{1,0:T(8,128)(2,1)S(1)}, u32[]{:S(2)}, u32[]{:S(2)}) collective-permute-start(bf16[64,512]{1,0:T(8,128)(2,1)S(1)} %fusion.9), channel_id=1, source_target_pairs={{0,4},{1,5},{2,6},{3,7},{4,0},{5,1},{6,2},{7,3},{8,12},{9,13},{10,... | collective-permute-start | bytes 196616 | tf_op jit(solution)/shard_map/residual2/ppermute | solution.py:29
  25.6 2.0 %collective-permute-done.12 = bf16[64,512]{1,0:T(8,128)(2,1)S(1)} collective-permute-done((bf16[64,512]{1,0:T(8,128)(2,1)S(1)}, bf16[64,512]{1,0:T(8,128)(2,1)S(1)}, u32[]{:S(2)}, u32[]{:S(2)}) %collective-permute-start.12) | collective-permute-done | bytes 65568 | tf_op jit(solution)/shard_map/residual3/ppermute | solution.py:29
  27.6 0.4 collective-permute-done.11
  28.0 0.9 %collective-permute-done.10 = bf16[64,512]{1,0:T(8,128)(2,1)S(1)} collective-permute-done((bf16[64,512]{1,0:T(8,128)(2,1)S(1)}, bf16[64,512]{1,0:T(8,128)(2,1)S(1)}, u32[]{:S(2)}, u32[]{:S(2)}) %collective-permute-start.10) | collective-permute-done | bytes 65568 | tf_op jit(solution)/shard_map/residual2/ppermute | solution.py:29
  29.2 0.5 fusion.1
  29.7 0.2 fusion.19
  29.9 0.8 %collective-permute-done.13 = bf16[256,512]{1,0:T(8,128)(2,1)S(1)} collective-permute-done((bf16[256,512]{1,0:T(8,128)(2,1)S(1)}, bf16[256,512]{1,0:T(8,128)(2,1)S(1)}, u32[]{:S(2)}, u32[]{:S(2)}) %collective-permute-start.13) | collective-permute-done | bytes 262176 | tf_op jit(solution)/shard_map/residual_core/ppermute | solution.py:24
  30.7 0.2 convolution_multiply_fusion.2
  31.1 0.2 collective-permute-start.16
  31.3 0.1 multiply_convert_fusion
  31.4 1.8 %collective-permute-start.14 = (bf16[256,512]{1,0:T(8,128)(2,1)S(1)}, bf16[256,512]{1,0:T(8,128)(2,1)S(1)}, u32[]{:S(2)}, u32[]{:S(2)}) collective-permute-start(bf16[256,512]{1,0:T(8,128)(2,1)S(1)} %get-tuple-element.55), channel_id=1, source_target_pairs={{0,8},{1,17},{2,10},{3,19},{4,12},{5,21},{6,14},{7,23},{8,0},{9,25... | collective-permute-start | bytes 786440 | tf_op jit(solution)/shard_map/squares0/ppermute | solution.py:37
  33.1 0.2 fusion.23
  33.4 0.2 fusion.28
  33.6 2.6 %collective-permute-start.17 = (bf16[64,512]{1,0:T(8,128)(2,1)S(1)}, bf16[64,512]{1,0:T(8,128)(2,1)S(1)}, u32[]{:S(2)}, u32[]{:S(2)}) collective-permute-start(bf16[64,512]{1,0:T(8,128)(2,1)S(1)} %get-tuple-element.60), channel_id=1, source_target_pairs={{0,6},{1,7},{2,4},{3,5},{4,2},{5,3},{6,0},{7,1},{8,14},{9,15},{10,... | collective-permute-start | bytes 196616 | tf_op jit(solution)/shard_map/fit3/ppermute | solution.py:29
  36.2 1.9 %collective-permute-start.18 = (bf16[64,512]{1,0:T(8,128)(2,1)S(1)}, bf16[64,512]{1,0:T(8,128)(2,1)S(1)}, u32[]{:S(2)}, u32[]{:S(2)}) collective-permute-start(bf16[64,512]{1,0:T(8,128)(2,1)S(1)} %get-tuple-element.62), channel_id=1, source_target_pairs={{0,4},{1,5},{2,6},{3,7},{4,0},{5,1},{6,2},{7,3},{8,12},{9,13},{10,... | collective-permute-start | bytes 196616 | tf_op jit(solution)/shard_map/fit2/ppermute | solution.py:29
  38.2 0.8 %collective-permute-start.15 = (bf16[256,512]{1,0:T(8,128)(2,1)S(1)}, bf16[256,512]{1,0:T(8,128)(2,1)S(1)}, u32[]{:S(2)}, u32[]{:S(2)}) collective-permute-start(bf16[256,512]{1,0:T(8,128)(2,1)S(1)} %fusion.14), channel_id=1, source_target_pairs={{0,16},{1,9},{2,18},{3,11},{4,20},{5,13},{6,22},{7,15},{8,24},{9,1... | collective-permute-start | bytes 786440 | tf_op jit(solution)/shard_map/squares1/ppermute | solution.py:37
  39.0 1.3 %collective-permute-done.17 = bf16[64,512]{1,0:T(8,128)(2,1)S(1)} collective-permute-done((bf16[64,512]{1,0:T(8,128)(2,1)S(1)}, bf16[64,512]{1,0:T(8,128)(2,1)S(1)}, u32[]{:S(2)}, u32[]{:S(2)}) %collective-permute-start.17) | collective-permute-done | bytes 65568 | tf_op jit(solution)/shard_map/fit3/ppermute | solution.py:29
  40.3 0.6 %collective-permute-done.19 = bf16[64,512]{1,0:T(8,128)(2,1)S(1)} collective-permute-done((bf16[64,512]{1,0:T(8,128)(2,1)S(1)}, bf16[64,512]{1,0:T(8,128)(2,1)S(1)}, u32[]{:S(2)}, u32[]{:S(2)}) %collective-permute-start.19) | collective-permute-done | bytes 65568 | tf_op jit(solution)/shard_map/fit1/ppermute | solution.py:29
  40.9 0.8 %collective-permute-done.18 = bf16[64,512]{1,0:T(8,128)(2,1)S(1)} collective-permute-done((bf16[64,512]{1,0:T(8,128)(2,1)S(1)}, bf16[64,512]{1,0:T(8,128)(2,1)S(1)}, u32[]{:S(2)}, u32[]{:S(2)}) %collective-permute-start.18) | collective-permute-done | bytes 65568 | tf_op jit(solution)/shard_map/fit2/ppermute | solution.py:29
  41.8 2.7 %collective-permute-start.22 = (bf16[64,512]{1,0:T(8,128)(2,1)S(1)}, bf16[64,512]{1,0:T(8,128)(2,1)S(1)}, u32[]{:S(2)}, u32[]{:S(2)}) collective-permute-start(bf16[64,512]{1,0:T(8,128)(2,1)S(1)} %fusion.18), channel_id=1, source_target_pairs={{0,6},{1,7},{2,4},{3,5},{4,2},{5,3},{6,0},{7,1},{8,14},{9,15},{10,... | collective-permute-start | bytes 196616 | tf_op jit(solution)/shard_map/residual3/ppermute | solution.py:29
  44.4 1.8 %collective-permute-start.20 = (bf16[64,512]{1,0:T(8,128)(2,1)S(1)}, bf16[64,512]{1,0:T(8,128)(2,1)S(1)}, u32[]{:S(2)}, u32[]{:S(2)}) collective-permute-start(bf16[64,512]{1,0:T(8,128)(2,1)S(1)} %fusion.18), channel_id=1, source_target_pairs={{0,4},{1,5},{2,6},{3,7},{4,0},{5,1},{6,2},{7,3},{8,12},{9,13},{10,... | collective-permute-start | bytes 196616 | tf_op jit(solution)/shard_map/residual2/ppermute | solution.py:29
  46.2 0.1 convert_add_fusion
  46.3 2.1 %collective-permute-done.22 = bf16[64,512]{1,0:T(8,128)(2,1)S(1)} collective-permute-done((bf16[64,512]{1,0:T(8,128)(2,1)S(1)}, bf16[64,512]{1,0:T(8,128)(2,1)S(1)}, u32[]{:S(2)}, u32[]{:S(2)}) %collective-permute-start.22) | collective-permute-done | bytes 65568 | tf_op jit(solution)/shard_map/residual3/ppermute | solution.py:29
  48.5 0.7 %collective-permute-done.21 = bf16[64,512]{1,0:T(8,128)(2,1)S(1)} collective-permute-done((bf16[64,512]{1,0:T(8,128)(2,1)S(1)}, bf16[64,512]{1,0:T(8,128)(2,1)S(1)}, u32[]{:S(2)}, u32[]{:S(2)}) %collective-permute-start.21) | collective-permute-done | bytes 65568 | tf_op jit(solution)/shard_map/residual1/ppermute | solution.py:29
  49.2 0.8 %collective-permute-done.20 = bf16[64,512]{1,0:T(8,128)(2,1)S(1)} collective-permute-done((bf16[64,512]{1,0:T(8,128)(2,1)S(1)}, bf16[64,512]{1,0:T(8,128)(2,1)S(1)}, u32[]{:S(2)}, u32[]{:S(2)}) %collective-permute-start.20) | collective-permute-done | bytes 65568 | tf_op jit(solution)/shard_map/residual2/ppermute | solution.py:29
  50.1 0.3 fusion.24
  50.4 0.3 convolution_multiply_fusion.1
  50.7 1.0 %collective-permute-done.23 = bf16[256,512]{1,0:T(8,128)(2,1)S(1)} collective-permute-done((bf16[256,512]{1,0:T(8,128)(2,1)S(1)}, bf16[256,512]{1,0:T(8,128)(2,1)S(1)}, u32[]{:S(2)}, u32[]{:S(2)}) %collective-permute-start.23) | collective-permute-done | bytes 262176 | tf_op jit(solution)/shard_map/residual_core/ppermute | solution.py:24
  51.6 1.1 %fusion = f32[256,512]{1,0:T(8,128)} fusion(bf16[256,256]{1,0:T(8,128)(2,1)S(1)} %collective-permute-done.6, bf16[256,512]{1,0:T(8,128)(2,1)S(1)} %collective-permute-done.23, f32[256,512]{1,0:T(8,128)S(1)} %convolution_multiply_fusion.1, f32[256,512]{1,0:T(8,128)S(1)} %get-tuple-element.54, f32[256,512]{1,0:T(8,128)S(1)} %get-tuple-element.52, ...), kind=kOutput, calls=%fused_computation.1 | convolution fusion | flops 68288512 | bytes 3016704 | tf_op jit(solution)/shard_map/dot_general | solution.py:126
  (61 shorter events, 1.2 us)
Async XLA Ops:
  0.6 6.9 %copy-start.2 = (f32[256,512]{1,0:T(8,128)S(1)}, f32[256,512]{1,0:T(8,128)}, u32[]{:S(2)}) copy-start(f32[256,512]{1,0:T(8,128)} %param.8) | copy-start | bytes 1572868
  0.6 6.9 %copy-start.3 = (f32[256,512]{1,0:T(8,128)S(1)}, f32[256,512]{1,0:T(8,128)}, u32[]{:S(2)}) copy-start(f32[256,512]{1,0:T(8,128)} %param.7) | copy-start | bytes 1572868
  1.7 8.7 %collective-permute-start = (bf16[2,64,256]{2,1,0:T(8,128)(2,1)S(1)}, bf16[2,64,256]{2,1,0:T(8,128)(2,1)S(1)}, u32[]{:S(2)}, u32[]{:S(2)}) collective-permute-start(bf16[2,64,256]{2,1,0:T(8,128)(2,1)S(1)} %pad_maximum_fusion.2), channel_id=1, source_target_pairs={{0,6},{1,7},{2,4},{3,5},{4,2},{5,3},{6,0},{7,1},{8,14},{9,15},{10,... | collective-permute-start | bytes 196616 | tf_op jit(solution)/shard_map/cells3/ppermute | solution.py:29
  6.8 7.6 %collective-permute-start.1 = (bf16[2,64,256]{2,1,0:T(8,128)(2,1)S(1)}, bf16[2,64,256]{2,1,0:T(8,128)(2,1)S(1)}, u32[]{:S(2)}, u32[]{:S(2)}) collective-permute-start(bf16[2,64,256]{2,1,0:T(8,128)(2,1)S(1)} %pad_maximum_fusion.3), channel_id=1, source_target_pairs={{0,4},{1,5},{2,6},{3,7},{4,0},{5,1},{6,2},{7,3},{8,12},{9,13},{10,... | collective-permute-start | bytes 196616 | tf_op jit(solution)/shard_map/cells2/ppermute | solution.py:29
  6.9 7.9 %collective-permute-start.3 = (bf16[2,64,256]{2,1,0:T(8,128)(2,1)S(1)}, bf16[2,64,256]{2,1,0:T(8,128)(2,1)S(1)}, u32[]{:S(2)}, u32[]{:S(2)}) collective-permute-start(bf16[2,64,256]{2,1,0:T(8,128)(2,1)S(1)} %pad_maximum_fusion.4), channel_id=1, source_target_pairs={{0,2},{1,3},{2,0},{3,1},{4,6},{5,7},{6,4},{7,5},{8,10},{9,11},{10,... | collective-permute-start | bytes 196616 | tf_op jit(solution)/shard_map/cells1/ppermute | solution.py:29
  7.7 2.7 %collective-permute-start.2 = (bf16[256,512]{1,0:T(8,128)(2,1)S(1)}, bf16[256,512]{1,0:T(8,128)(2,1)S(1)}, u32[]{:S(2)}, u32[]{:S(2)}) collective-permute-start(bf16[256,512]{1,0:T(8,128)(2,1)S(1)} %get-tuple-element.59), channel_id=1, source_target_pairs={{0,1},{1,0},{2,3},{3,2},{4,5},{5,4},{6,7},{7,6},{8,9},{9,8},{10,11... | collective-permute-start | bytes 786440 | tf_op jit(solution)/shard_map/coef_core/ppermute | solution.py:24
  7.8 8.8 %collective-permute-start.4 = (bf16[256,512]{1,0:T(8,128)(2,1)S(1)}, bf16[256,512]{1,0:T(8,128)(2,1)S(1)}, u32[]{:S(2)}, u32[]{:S(2)}) collective-permute-start(bf16[256,512]{1,0:T(8,128)(2,1)S(1)} %get-tuple-element.57), channel_id=1, source_target_pairs={{0,8},{1,17},{2,10},{3,19},{4,12},{5,21},{6,14},{7,23},{8,0},{9,25... | collective-permute-start | bytes 786440 | tf_op jit(solution)/shard_map/squares0/ppermute | solution.py:37
  9.5 0.8 %copy-start.4 = (bf16[64,512]{1,0:T(8,128)(2,1)S(1)}, bf16[64,512]{1,0:T(8,128)(2,1)}, u32[]{:S(2)}) copy-start(bf16[64,512]{1,0:T(8,128)(2,1)} %param.6) | copy-start | bytes 196612
  10.8 7.6 %collective-permute-start.7 = (bf16[64,512]{1,0:T(8,128)(2,1)S(1)}, bf16[64,512]{1,0:T(8,128)(2,1)S(1)}, u32[]{:S(2)}, u32[]{:S(2)}) collective-permute-start(bf16[64,512]{1,0:T(8,128)(2,1)S(1)} %fusion.6), channel_id=1, source_target_pairs={{0,6},{1,7},{2,4},{3,5},{4,2},{5,3},{6,0},{7,1},{8,14},{9,15},{10,... | collective-permute-start | bytes 196616 | tf_op jit(solution)/shard_map/fit3/ppermute | solution.py:29
  14.8 6.0 %collective-permute-start.8 = (bf16[64,512]{1,0:T(8,128)(2,1)S(1)}, bf16[64,512]{1,0:T(8,128)(2,1)S(1)}, u32[]{:S(2)}, u32[]{:S(2)}) collective-permute-start(bf16[64,512]{1,0:T(8,128)(2,1)S(1)} %fusion.7), channel_id=1, source_target_pairs={{0,4},{1,5},{2,6},{3,7},{4,0},{5,1},{6,2},{7,3},{8,12},{9,13},{10,... | collective-permute-start | bytes 196616 | tf_op jit(solution)/shard_map/fit2/ppermute | solution.py:29
  15.2 5.6 %collective-permute-start.9 = (bf16[64,512]{1,0:T(8,128)(2,1)S(1)}, bf16[64,512]{1,0:T(8,128)(2,1)S(1)}, u32[]{:S(2)}, u32[]{:S(2)}) collective-permute-start(bf16[64,512]{1,0:T(8,128)(2,1)S(1)} %fusion.8), channel_id=1, source_target_pairs={{0,2},{1,3},{2,0},{3,1},{4,6},{5,7},{6,4},{7,5},{8,10},{9,11},{10,... | collective-permute-start | bytes 196616 | tf_op jit(solution)/shard_map/fit1/ppermute | solution.py:29
  16.6 8.8 %collective-permute-start.6 = (bf16[256,256]{1,0:T(8,128)(2,1)S(1)}, bf16[256,256]{1,0:T(8,128)(2,1)S(1)}, u32[]{:S(2)}, u32[]{:S(2)}) collective-permute-start(bf16[256,256]{1,0:T(8,128)(2,1)S(1)} %pad_maximum_fusion), channel_id=1, source_target_pairs={{0,1},{1,0},{2,3},{3,2},{4,5},{5,4},{6,7},{7,6},{8,9},{9,8},{10,11... | collective-permute-start | bytes 393224 | tf_op jit(solution)/shard_map/cells_core/ppermute | solution.py:24
  16.8 8.7 %collective-permute-start.5 = (bf16[256,512]{1,0:T(8,128)(2,1)S(1)}, bf16[256,512]{1,0:T(8,128)(2,1)S(1)}, u32[]{:S(2)}, u32[]{:S(2)}) collective-permute-start(bf16[256,512]{1,0:T(8,128)(2,1)S(1)} %convert_element_type.82), channel_id=1, source_target_pairs={{0,16},{1,9},{2,18},{3,11},{4,20},{5,13},{6,22},{7,15},{8,24},{9,1... | collective-permute-start | bytes 786440 | tf_op jit(solution)/shard_map/squares1/ppermute | solution.py:37
  21.0 6.7 %collective-permute-start.12 = (bf16[64,512]{1,0:T(8,128)(2,1)S(1)}, bf16[64,512]{1,0:T(8,128)(2,1)S(1)}, u32[]{:S(2)}, u32[]{:S(2)}) collective-permute-start(bf16[64,512]{1,0:T(8,128)(2,1)S(1)} %fusion.9), channel_id=1, source_target_pairs={{0,6},{1,7},{2,4},{3,5},{4,2},{5,3},{6,0},{7,1},{8,14},{9,15},{10,... | collective-permute-start | bytes 196616 | tf_op jit(solution)/shard_map/residual3/ppermute | solution.py:29
  23.2 4.8 %collective-permute-start.11 = (bf16[64,512]{1,0:T(8,128)(2,1)S(1)}, bf16[64,512]{1,0:T(8,128)(2,1)S(1)}, u32[]{:S(2)}, u32[]{:S(2)}) collective-permute-start(bf16[64,512]{1,0:T(8,128)(2,1)S(1)} %fusion.9), channel_id=1, source_target_pairs={{0,2},{1,3},{2,0},{3,1},{4,6},{5,7},{6,4},{7,5},{8,10},{9,11},{10,... | collective-permute-start | bytes 196616 | tf_op jit(solution)/shard_map/residual1/ppermute | solution.py:29
  23.2 5.7 %collective-permute-start.10 = (bf16[64,512]{1,0:T(8,128)(2,1)S(1)}, bf16[64,512]{1,0:T(8,128)(2,1)S(1)}, u32[]{:S(2)}, u32[]{:S(2)}) collective-permute-start(bf16[64,512]{1,0:T(8,128)(2,1)S(1)} %fusion.9), channel_id=1, source_target_pairs={{0,4},{1,5},{2,6},{3,7},{4,0},{5,1},{6,2},{7,3},{8,12},{9,13},{10,... | collective-permute-start | bytes 196616 | tf_op jit(solution)/shard_map/residual2/ppermute | solution.py:29
  25.5 3.5 %copy-start.5 = (f32[256]{0:T(256)S(1)}, f32[256]{0:T(256)}, u32[]{:S(2)}) copy-start(f32[256]{0:T(256)} %param.9) | copy-start | bytes 3076
  29.1 1.6 %collective-permute-start.13 = (bf16[256,512]{1,0:T(8,128)(2,1)S(1)}, bf16[256,512]{1,0:T(8,128)(2,1)S(1)}, u32[]{:S(2)}, u32[]{:S(2)}) collective-permute-start(bf16[256,512]{1,0:T(8,128)(2,1)S(1)} %constant_dynamic-update-slice_fusion), channel_id=1, source_target_pairs={{0,1},{1,0},{2,3},{3,2},{4,5},{5,4},{6,7},{7,6},{8,9},{9,8},{10,11... | collective-permute-start | bytes 786440 | tf_op jit(solution)/shard_map/residual_core/ppermute | solution.py:24
  31.1 2.3 %collective-permute-start.16 = (bf16[256,512]{1,0:T(8,128)(2,1)S(1)}, bf16[256,512]{1,0:T(8,128)(2,1)S(1)}, u32[]{:S(2)}, u32[]{:S(2)}) collective-permute-start(bf16[256,512]{1,0:T(8,128)(2,1)S(1)} %get-tuple-element.53), channel_id=1, source_target_pairs={{0,1},{1,0},{2,3},{3,2},{4,5},{5,4},{6,7},{7,6},{8,9},{9,8},{10,11... | collective-permute-start | bytes 786440 | tf_op jit(solution)/shard_map/coef_core/ppermute | solution.py:24
  31.4 6.7 %collective-permute-start.14 = (bf16[256,512]{1,0:T(8,128)(2,1)S(1)}, bf16[256,512]{1,0:T(8,128)(2,1)S(1)}, u32[]{:S(2)}, u32[]{:S(2)}) collective-permute-start(bf16[256,512]{1,0:T(8,128)(2,1)S(1)} %get-tuple-element.55), channel_id=1, source_target_pairs={{0,8},{1,17},{2,10},{3,19},{4,12},{5,21},{6,14},{7,23},{8,0},{9,25... | collective-permute-start | bytes 786440 | tf_op jit(solution)/shard_map/squares0/ppermute | solution.py:37
  33.6 6.6 %collective-permute-start.17 = (bf16[64,512]{1,0:T(8,128)(2,1)S(1)}, bf16[64,512]{1,0:T(8,128)(2,1)S(1)}, u32[]{:S(2)}, u32[]{:S(2)}) collective-permute-start(bf16[64,512]{1,0:T(8,128)(2,1)S(1)} %get-tuple-element.60), channel_id=1, source_target_pairs={{0,6},{1,7},{2,4},{3,5},{4,2},{5,3},{6,0},{7,1},{8,14},{9,15},{10,... | collective-permute-start | bytes 196616 | tf_op jit(solution)/shard_map/fit3/ppermute | solution.py:29
  36.2 4.7 %collective-permute-start.19 = (bf16[64,512]{1,0:T(8,128)(2,1)S(1)}, bf16[64,512]{1,0:T(8,128)(2,1)S(1)}, u32[]{:S(2)}, u32[]{:S(2)}) collective-permute-start(bf16[64,512]{1,0:T(8,128)(2,1)S(1)} %get-tuple-element.61), channel_id=1, source_target_pairs={{0,2},{1,3},{2,0},{3,1},{4,6},{5,7},{6,4},{7,5},{8,10},{9,11},{10,... | collective-permute-start | bytes 196616 | tf_op jit(solution)/shard_map/fit1/ppermute | solution.py:29
  36.2 5.5 %collective-permute-start.18 = (bf16[64,512]{1,0:T(8,128)(2,1)S(1)}, bf16[64,512]{1,0:T(8,128)(2,1)S(1)}, u32[]{:S(2)}, u32[]{:S(2)}) collective-permute-start(bf16[64,512]{1,0:T(8,128)(2,1)S(1)} %get-tuple-element.62), channel_id=1, source_target_pairs={{0,4},{1,5},{2,6},{3,7},{4,0},{5,1},{6,2},{7,3},{8,12},{9,13},{10,... | collective-permute-start | bytes 196616 | tf_op jit(solution)/shard_map/fit2/ppermute | solution.py:29
  38.2 8.1 %collective-permute-start.15 = (bf16[256,512]{1,0:T(8,128)(2,1)S(1)}, bf16[256,512]{1,0:T(8,128)(2,1)S(1)}, u32[]{:S(2)}, u32[]{:S(2)}) collective-permute-start(bf16[256,512]{1,0:T(8,128)(2,1)S(1)} %fusion.14), channel_id=1, source_target_pairs={{0,16},{1,9},{2,18},{3,11},{4,20},{5,13},{6,22},{7,15},{8,24},{9,1... | collective-permute-start | bytes 786440 | tf_op jit(solution)/shard_map/squares1/ppermute | solution.py:37
  41.8 6.7 %collective-permute-start.22 = (bf16[64,512]{1,0:T(8,128)(2,1)S(1)}, bf16[64,512]{1,0:T(8,128)(2,1)S(1)}, u32[]{:S(2)}, u32[]{:S(2)}) collective-permute-start(bf16[64,512]{1,0:T(8,128)(2,1)S(1)} %fusion.18), channel_id=1, source_target_pairs={{0,6},{1,7},{2,4},{3,5},{4,2},{5,3},{6,0},{7,1},{8,14},{9,15},{10,... | collective-permute-start | bytes 196616 | tf_op jit(solution)/shard_map/residual3/ppermute | solution.py:29
  44.4 4.7 %collective-permute-start.21 = (bf16[64,512]{1,0:T(8,128)(2,1)S(1)}, bf16[64,512]{1,0:T(8,128)(2,1)S(1)}, u32[]{:S(2)}, u32[]{:S(2)}) collective-permute-start(bf16[64,512]{1,0:T(8,128)(2,1)S(1)} %fusion.18), channel_id=1, source_target_pairs={{0,2},{1,3},{2,0},{3,1},{4,6},{5,7},{6,4},{7,5},{8,10},{9,11},{10,... | collective-permute-start | bytes 196616 | tf_op jit(solution)/shard_map/residual1/ppermute | solution.py:29
  44.4 5.6 %collective-permute-start.20 = (bf16[64,512]{1,0:T(8,128)(2,1)S(1)}, bf16[64,512]{1,0:T(8,128)(2,1)S(1)}, u32[]{:S(2)}, u32[]{:S(2)}) collective-permute-start(bf16[64,512]{1,0:T(8,128)(2,1)S(1)} %fusion.18), channel_id=1, source_target_pairs={{0,4},{1,5},{2,6},{3,7},{4,0},{5,1},{6,2},{7,3},{8,12},{9,13},{10,... | collective-permute-start | bytes 196616 | tf_op jit(solution)/shard_map/residual2/ppermute | solution.py:29
  50.0 1.6 %collective-permute-start.23 = (bf16[256,512]{1,0:T(8,128)(2,1)S(1)}, bf16[256,512]{1,0:T(8,128)(2,1)S(1)}, u32[]{:S(2)}, u32[]{:S(2)}) collective-permute-start(bf16[256,512]{1,0:T(8,128)(2,1)S(1)} %constant_dynamic-update-slice_fusion.4), channel_id=1, source_target_pairs={{0,1},{1,0},{2,3},{3,2},{4,5},{5,4},{6,7},{7,6},{8,9},{9,8},{10,11... | collective-permute-start | bytes 786440 | tf_op jit(solution)/shard_map/residual_core/ppermute | solution.py:24
  50.4 2.3 %copy-start = (f32[256,512]{1,0:T(8,128)}, f32[256,512]{1,0:T(8,128)S(1)}, u32[]{:S(2)}) copy-start(f32[256,512]{1,0:T(8,128)S(1)} %get-tuple-element.51) | copy-start | bytes 1572868
  50.4 2.3 %copy-start.1 = (f32[256,512]{1,0:T(8,128)}, f32[256,512]{1,0:T(8,128)S(1)}, u32[]{:S(2)}) copy-start(f32[256,512]{1,0:T(8,128)S(1)} %get-tuple-element.52) | copy-start | bytes 1572868

commit v9 on v8

--- a/solution.py
+++ b/solution.py
@@ -61,13 +61,12 @@
         start = ((chip ^ k) * 2 + (core ^ side)) * mine
         return lax.dynamic_slice_in_dim(expression, start, mine, 1)
 
-    (coef_copy,) = together(coef_init.astype(bf16))
+    coef_copy, response_rows = together(coef_init.astype(bf16), responses.astype(f32))
     coef_other = core_swap(coef_copy, "coef_core")
     pairs = [jnp.stack([columns(k, 0), columns(k, 1)]) for k in range(chips)]
     for k in far_first:
         pairs[k] = chip_swap(pairs[k], k, f"cells{k}")
     weights = jnp.broadcast_to(penalty[:, None], coef_init.shape)
-    response_rows = responses.astype(f32)
 
     def fit(k):
         return dot(pairs[k][0], coef_copy) + dot(pairs[k][1], coef_other)

time: 52.9 us -> 52.3 us (0.989)
  starting transfers between devices: 30.6 us -> 31.5 us
  waiting for transfers between devices: 13.9 us -> 13.1 us
  local copies, waits for them, and re-layouts: 1.87 us -> 1.21 us
    ppermute x15, waiting for transfers between devices: 12.1 us -> 11.3 us  [chip_swap(): lax.ppermute(value, 'shard', [(i, i ^ 2 * mask) for i in range(lax.axis_s...]
    unnamed x18, local copies, waits for them, and re-layouts: 0.74 us -> 0.07 us
    ppermute x15, starting transfers between devices: 24.2 us -> 24.9 us  [chip_swap(): lax.ppermute(value, 'shard', [(i, i ^ 2 * mask) for i in range(lax.axis_s...]
where the time goes in v9:
time: 52.3 us; the launch traced here: 52.2 us
  starting transfers between devices  31.5 us (60%)
  waiting for transfers between devices  13.1 us (25%)
  matrix products  3.82 us (7%)
  other arithmetic  1.37 us (3%)
  local copies, waits for them, and re-layouts  1.21 us (2%)
  between operations  1.15 us (2%)
    ppermute x15, starting transfers between devices, chip_swap(): lax.ppermute(value, 'shard', [(i, i ^ 2 * mask) for i in range(lax.axis_s...  24.9 us
    ppermute x15, waiting for transfers between devices, chip_swap(): lax.ppermute(value, 'shard', [(i, i ^ 2 * mask) for i in range(lax.axis_s...  11.3 us
    ppermute x4, starting transfers between devices, cond_swap(): return lax.ppermute(value, ('cond', 'shard'), pairs)  6.16 us
    ppermute x5, waiting for transfers between devices, core_swap(): lax.ppermute(value, 'shard', [(i, i ^ 1) for i in range(lax.axis_size('sh...  1.77 us
    dot_general x10, matrix products, dot(): return jnp.dot(x, c, preferred_element_type=f32)  1.76 us
    dot_general x2, matrix products, shards(): lax.dot_general(across, residual_other, contract, preferred_element_type=...  1.33 us
  transfers between devices with their start and end apart: 24, of which 12 were waited for; matrix products, arithmetic and copies ran while one was open for 7% of the time, Pallas kernels for 0%

profile of v9, /device:TPU:0, one launch (start us, length us, event | category | flops | bytes accessed | tf_op | source)
XLA Modules:
  0.0 52.2 jit_solution(1018775433095785754)
XLA Ops:
  0.7 1.0 %constant_dynamic-slice_fusion = (bf16[64,256]{1,0:T(8,128)(2,1)S(1)}, bf16[1,64,256]{2,1,0:T(8,128)(2,1)S(1)}, bf16[1,64,256]{2,1,0:T(8,128)(2,1)S(1)}, bf16[1,...) fusion(bf16[64,2048]{1,0:T(8,128)(2,1)} %param.5, ...), kind=kLoop, calls=%fused_computation.65 | loop fusion | bytes 524320 | tf_op jit(solution)/shard_map/dynamic_slice | solution.py:62
  1.7 5.1 %collective-permute-start = (bf16[2,64,256]{2,1,0:T(8,128)(2,1)S(1)}, bf16[2,64,256]{2,1,0:T(8,128)(2,1)S(1)}, u32[]{:S(2)}, u32[]{:S(2)}) collective-permute-start(bf16[2,64,256]{2,1,0:T(8,128)(2,1)S(1)} %pad_maximum_fusion.2), channel_id=1, source_target_pairs={{0,6},{1,7},{2,4},{3,5},{4,2},{5,3},{6,0},{7,1},{8,14},{9,15},{10,... | collective-permute-start | bytes 196616 | tf_op jit(solution)/shard_map/cells3/ppermute | solution.py:29
  7.0 0.6 %collective-permute-start.3 = (bf16[2,64,256]{2,1,0:T(8,128)(2,1)S(1)}, bf16[2,64,256]{2,1,0:T(8,128)(2,1)S(1)}, u32[]{:S(2)}, u32[]{:S(2)}) collective-permute-start(bf16[2,64,256]{2,1,0:T(8,128)(2,1)S(1)} %pad_maximum_fusion.4), channel_id=1, source_target_pairs={{0,2},{1,3},{2,0},{3,1},{4,6},{5,7},{6,4},{7,5},{8,10},{9,11},{10,... | collective-permute-start | bytes 196616 | tf_op jit(solution)/shard_map/cells1/ppermute | solution.py:29
  7.6 0.1 multiply_convert_fusion.1
  7.8 1.8 %collective-permute-start.4 = (bf16[256,512]{1,0:T(8,128)(2,1)S(1)}, bf16[256,512]{1,0:T(8,128)(2,1)S(1)}, u32[]{:S(2)}, u32[]{:S(2)}) collective-permute-start(bf16[256,512]{1,0:T(8,128)(2,1)S(1)} %get-tuple-element.61), channel_id=1, source_target_pairs={{0,8},{1,17},{2,10},{3,19},{4,12},{5,21},{6,14},{7,23},{8,0},{9,25... | collective-permute-start | bytes 786440 | tf_op jit(solution)/shard_map/squares0/ppermute | solution.py:37
  9.6 0.2 fusion.29
  9.8 0.2 fusion.22
  9.9 0.2 fusion.6
  10.1 3.9 %collective-permute-start.7 = (bf16[64,512]{1,0:T(8,128)(2,1)S(1)}, bf16[64,512]{1,0:T(8,128)(2,1)S(1)}, u32[]{:S(2)}, u32[]{:S(2)}) collective-permute-start(bf16[64,512]{1,0:T(8,128)(2,1)S(1)} %fusion.6), channel_id=1, source_target_pairs={{0,6},{1,7},{2,4},{3,5},{4,2},{5,3},{6,0},{7,1},{8,14},{9,15},{10,... | collective-permute-start | bytes 196616 | tf_op jit(solution)/shard_map/fit3/ppermute | solution.py:29
  14.1 0.2 fusion.20
  14.2 0.2 fusion.7
  14.5 0.2 fusion.21
  14.6 0.2 fusion.8
  14.8 1.7 %collective-permute-start.9 = (bf16[64,512]{1,0:T(8,128)(2,1)S(1)}, bf16[64,512]{1,0:T(8,128)(2,1)S(1)}, u32[]{:S(2)}, u32[]{:S(2)}) collective-permute-start(bf16[64,512]{1,0:T(8,128)(2,1)S(1)} %fusion.8), channel_id=1, source_target_pairs={{0,2},{1,3},{2,0},{3,1},{4,6},{5,7},{6,4},{7,5},{8,10},{9,11},{10,... | collective-permute-start | bytes 196616 | tf_op jit(solution)/shard_map/fit1/ppermute | solution.py:29
  16.8 1.6 %collective-permute-start.5 = (bf16[256,512]{1,0:T(8,128)(2,1)S(1)}, bf16[256,512]{1,0:T(8,128)(2,1)S(1)}, u32[]{:S(2)}, u32[]{:S(2)}) collective-permute-start(bf16[256,512]{1,0:T(8,128)(2,1)S(1)} %convert_element_type.82), channel_id=1, source_target_pairs={{0,16},{1,9},{2,18},{3,11},{4,20},{5,13},{6,22},{7,15},{8,24},{9,1... | collective-permute-start | bytes 786440 | tf_op jit(solution)/shard_map/squares1/ppermute | solution.py:37
  18.4 1.5 %collective-permute-done.9 = bf16[64,512]{1,0:T(8,128)(2,1)S(1)} collective-permute-done((bf16[64,512]{1,0:T(8,128)(2,1)S(1)}, bf16[64,512]{1,0:T(8,128)(2,1)S(1)}, u32[]{:S(2)}, u32[]{:S(2)}) %collective-permute-start.9) | collective-permute-done | bytes 65568 | tf_op jit(solution)/shard_map/fit1/ppermute | solution.py:29
  19.9 0.2 fusion.9
  20.1 2.9 %collective-permute-start.12 = (bf16[64,512]{1,0:T(8,128)(2,1)S(1)}, bf16[64,512]{1,0:T(8,128)(2,1)S(1)}, u32[]{:S(2)}, u32[]{:S(2)}) collective-permute-start(bf16[64,512]{1,0:T(8,128)(2,1)S(1)} %fusion.9), channel_id=1, source_target_pairs={{0,6},{1,7},{2,4},{3,5},{4,2},{5,3},{6,0},{7,1},{8,14},{9,15},{10,... | collective-permute-start | bytes 196616 | tf_op jit(solution)/shard_map/residual3/ppermute | solution.py:29
  23.1 1.5 %collective-permute-start.10 = (bf16[64,512]{1,0:T(8,128)(2,1)S(1)}, bf16[64,512]{1,0:T(8,128)(2,1)S(1)}, u32[]{:S(2)}, u32[]{:S(2)}) collective-permute-start(bf16[64,512]{1,0:T(8,128)(2,1)S(1)} %fusion.9), channel_id=1, source_target_pairs={{0,4},{1,5},{2,6},{3,7},{4,0},{5,1},{6,2},{7,3},{8,12},{9,13},{10,... | collective-permute-start | bytes 196616 | tf_op jit(solution)/shard_map/residual2/ppermute | solution.py:29
  24.7 1.6 %collective-permute-done.12 = bf16[64,512]{1,0:T(8,128)(2,1)S(1)} collective-permute-done((bf16[64,512]{1,0:T(8,128)(2,1)S(1)}, bf16[64,512]{1,0:T(8,128)(2,1)S(1)}, u32[]{:S(2)}, u32[]{:S(2)}) %collective-permute-start.12) | collective-permute-done | bytes 65568 | tf_op jit(solution)/shard_map/residual3/ppermute | solution.py:29
  26.3 1.2 %collective-permute-done.11 = bf16[64,512]{1,0:T(8,128)(2,1)S(1)} collective-permute-done((bf16[64,512]{1,0:T(8,128)(2,1)S(1)}, bf16[64,512]{1,0:T(8,128)(2,1)S(1)}, u32[]{:S(2)}, u32[]{:S(2)}) %collective-permute-start.11) | collective-permute-done | bytes 65568 | tf_op jit(solution)/shard_map/residual1/ppermute | solution.py:29
  27.5 0.8 %collective-permute-done.10 = bf16[64,512]{1,0:T(8,128)(2,1)S(1)} collective-permute-done((bf16[64,512]{1,0:T(8,128)(2,1)S(1)}, bf16[64,512]{1,0:T(8,128)(2,1)S(1)}, u32[]{:S(2)}, u32[]{:S(2)}) %collective-permute-start.10) | collective-permute-done | bytes 65568 | tf_op jit(solution)/shard_map/residual2/ppermute | solution.py:29
  28.6 0.5 fusion.1
  29.1 0.2 fusion.19
  29.3 0.8 %collective-permute-done.13 = bf16[256,512]{1,0:T(8,128)(2,1)S(1)} collective-permute-done((bf16[256,512]{1,0:T(8,128)(2,1)S(1)}, bf16[256,512]{1,0:T(8,128)(2,1)S(1)}, u32[]{:S(2)}, u32[]{:S(2)}) %collective-permute-start.13) | collective-permute-done | bytes 262176 | tf_op jit(solution)/shard_map/residual_core/ppermute | solution.py:24
  30.1 0.3 convolution_multiply_fusion.2
  30.5 0.2 collective-permute-start.16
  30.7 0.1 multiply_convert_fusion
  30.8 1.6 %collective-permute-start.14 = (bf16[256,512]{1,0:T(8,128)(2,1)S(1)}, bf16[256,512]{1,0:T(8,128)(2,1)S(1)}, u32[]{:S(2)}, u32[]{:S(2)}) collective-permute-start(bf16[256,512]{1,0:T(8,128)(2,1)S(1)} %get-tuple-element.59), channel_id=1, source_target_pairs={{0,8},{1,17},{2,10},{3,19},{4,12},{5,21},{6,14},{7,23},{8,0},{9,25... | collective-permute-start | bytes 786440 | tf_op jit(solution)/shard_map/squares0/ppermute | solution.py:37
  32.4 0.2 fusion.23
  32.6 0.2 fusion.28
  32.9 3.2 %collective-permute-start.17 = (bf16[64,512]{1,0:T(8,128)(2,1)S(1)}, bf16[64,512]{1,0:T(8,128)(2,1)S(1)}, u32[]{:S(2)}, u32[]{:S(2)}) collective-permute-start(bf16[64,512]{1,0:T(8,128)(2,1)S(1)} %get-tuple-element.64), channel_id=1, source_target_pairs={{0,6},{1,7},{2,4},{3,5},{4,2},{5,3},{6,0},{7,1},{8,14},{9,15},{10,... | collective-permute-start | bytes 196616 | tf_op jit(solution)/shard_map/fit3/ppermute | solution.py:29
  36.1 1.3 %collective-permute-start.18 = (bf16[64,512]{1,0:T(8,128)(2,1)S(1)}, bf16[64,512]{1,0:T(8,128)(2,1)S(1)}, u32[]{:S(2)}, u32[]{:S(2)}) collective-permute-start(bf16[64,512]{1,0:T(8,128)(2,1)S(1)} %get-tuple-element.66), channel_id=1, source_target_pairs={{0,4},{1,5},{2,6},{3,7},{4,0},{5,1},{6,2},{7,3},{8,12},{9,13},{10,... | collective-permute-start | bytes 196616 | tf_op jit(solution)/shard_map/fit2/ppermute | solution.py:29
  37.4 1.3 %collective-permute-start.15 = (bf16[256,512]{1,0:T(8,128)(2,1)S(1)}, bf16[256,512]{1,0:T(8,128)(2,1)S(1)}, u32[]{:S(2)}, u32[]{:S(2)}) collective-permute-start(bf16[256,512]{1,0:T(8,128)(2,1)S(1)} %fusion.14), channel_id=1, source_target_pairs={{0,16},{1,9},{2,18},{3,11},{4,20},{5,13},{6,22},{7,15},{8,24},{9,1... | collective-permute-start | bytes 786440 | tf_op jit(solution)/shard_map/squares1/ppermute | solution.py:37
  38.6 0.7 %collective-permute-done.17 = bf16[64,512]{1,0:T(8,128)(2,1)S(1)} collective-permute-done((bf16[64,512]{1,0:T(8,128)(2,1)S(1)}, bf16[64,512]{1,0:T(8,128)(2,1)S(1)}, u32[]{:S(2)}, u32[]{:S(2)}) %collective-permute-start.17) | collective-permute-done | bytes 65568 | tf_op jit(solution)/shard_map/fit3/ppermute | solution.py:29
  39.3 1.4 %collective-permute-done.19 = bf16[64,512]{1,0:T(8,128)(2,1)S(1)} collective-permute-done((bf16[64,512]{1,0:T(8,128)(2,1)S(1)}, bf16[64,512]{1,0:T(8,128)(2,1)S(1)}, u32[]{:S(2)}, u32[]{:S(2)}) %collective-permute-start.19) | collective-permute-done | bytes 65568 | tf_op jit(solution)/shard_map/fit1/ppermute | solution.py:29
  40.8 0.9 %collective-permute-done.18 = bf16[64,512]{1,0:T(8,128)(2,1)S(1)} collective-permute-done((bf16[64,512]{1,0:T(8,128)(2,1)S(1)}, bf16[64,512]{1,0:T(8,128)(2,1)S(1)}, u32[]{:S(2)}, u32[]{:S(2)}) %collective-permute-start.18) | collective-permute-done | bytes 65568 | tf_op jit(solution)/shard_map/fit2/ppermute | solution.py:29
  41.7 2.0 %collective-permute-start.22 = (bf16[64,512]{1,0:T(8,128)(2,1)S(1)}, bf16[64,512]{1,0:T(8,128)(2,1)S(1)}, u32[]{:S(2)}, u32[]{:S(2)}) collective-permute-start(bf16[64,512]{1,0:T(8,128)(2,1)S(1)} %fusion.18), channel_id=1, source_target_pairs={{0,6},{1,7},{2,4},{3,5},{4,2},{5,3},{6,0},{7,1},{8,14},{9,15},{10,... | collective-permute-start | bytes 196616 | tf_op jit(solution)/shard_map/residual3/ppermute | solution.py:29
  43.7 0.4 collective-permute-start.21
  44.0 2.1 %collective-permute-start.20 = (bf16[64,512]{1,0:T(8,128)(2,1)S(1)}, bf16[64,512]{1,0:T(8,128)(2,1)S(1)}, u32[]{:S(2)}, u32[]{:S(2)}) collective-permute-start(bf16[64,512]{1,0:T(8,128)(2,1)S(1)} %fusion.18), channel_id=1, source_target_pairs={{0,4},{1,5},{2,6},{3,7},{4,0},{5,1},{6,2},{7,3},{8,12},{9,13},{10,... | collective-permute-start | bytes 196616 | tf_op jit(solution)/shard_map/residual2/ppermute | solution.py:29
  46.1 0.1 convert_add_fusion
  46.2 2.0 %collective-permute-done.22 = bf16[64,512]{1,0:T(8,128)(2,1)S(1)} collective-permute-done((bf16[64,512]{1,0:T(8,128)(2,1)S(1)}, bf16[64,512]{1,0:T(8,128)(2,1)S(1)}, u32[]{:S(2)}, u32[]{:S(2)}) %collective-permute-start.22) | collective-permute-done | bytes 65568 | tf_op jit(solution)/shard_map/residual3/ppermute | solution.py:29
  48.3 0.5 collective-permute-done.21
  48.8 0.7 %collective-permute-done.20 = bf16[64,512]{1,0:T(8,128)(2,1)S(1)} collective-permute-done((bf16[64,512]{1,0:T(8,128)(2,1)S(1)}, bf16[64,512]{1,0:T(8,128)(2,1)S(1)}, u32[]{:S(2)}, u32[]{:S(2)}) %collective-permute-start.20) | collective-permute-done | bytes 65568 | tf_op jit(solution)/shard_map/residual2/ppermute | solution.py:29
  49.6 0.3 fusion.24
  49.9 0.2 convolution_multiply_fusion.1
  50.1 1.0 %collective-permute-done.23 = bf16[256,512]{1,0:T(8,128)(2,1)S(1)} collective-permute-done((bf16[256,512]{1,0:T(8,128)(2,1)S(1)}, bf16[256,512]{1,0:T(8,128)(2,1)S(1)}, u32[]{:S(2)}, u32[]{:S(2)}) %collective-permute-start.23) | collective-permute-done | bytes 262176 | tf_op jit(solution)/shard_map/residual_core/ppermute | solution.py:24
  51.1 1.1 %fusion = f32[256,512]{1,0:T(8,128)} fusion(bf16[256,256]{1,0:T(8,128)(2,1)S(1)} %collective-permute-done.6, bf16[256,512]{1,0:T(8,128)(2,1)S(1)} %collective-permute-done.23, f32[256,512]{1,0:T(8,128)S(1)} %convolution_multiply_fusion.1, f32[256,512]{1,0:T(8,128)S(1)} %get-tuple-element.58, f32[256,512]{1,0:T(8,128)S(1)} %get-tuple-element.56, ...), kind=kOutput, calls=%fused_computation.1 | convolution fusion | flops 68288512 | bytes 3016704 | tf_op jit(solution)/shard_map/dot_general | solution.py:125
  (61 shorter events, 1.2 us)
Async XLA Ops:
  0.7 6.9 %copy-start.4 = (bf16[64,512]{1,0:T(8,128)(2,1)S(1)}, bf16[64,512]{1,0:T(8,128)(2,1)}, u32[]{:S(2)}) copy-start(bf16[64,512]{1,0:T(8,128)(2,1)} %param.6) | copy-start | bytes 196612
  0.7 6.9 %copy-start.2 = (f32[256,512]{1,0:T(8,128)S(1)}, f32[256,512]{1,0:T(8,128)}, u32[]{:S(2)}) copy-start(f32[256,512]{1,0:T(8,128)} %param.8) | copy-start | bytes 1572868
  0.7 6.9 %copy-start.3 = (f32[256,512]{1,0:T(8,128)S(1)}, f32[256,512]{1,0:T(8,128)}, u32[]{:S(2)}) copy-start(f32[256,512]{1,0:T(8,128)} %param.7) | copy-start | bytes 1572868
  1.7 8.0 %collective-permute-start = (bf16[2,64,256]{2,1,0:T(8,128)(2,1)S(1)}, bf16[2,64,256]{2,1,0:T(8,128)(2,1)S(1)}, u32[]{:S(2)}, u32[]{:S(2)}) collective-permute-start(bf16[2,64,256]{2,1,0:T(8,128)(2,1)S(1)} %pad_maximum_fusion.2), channel_id=1, source_target_pairs={{0,6},{1,7},{2,4},{3,5},{4,2},{5,3},{6,0},{7,1},{8,14},{9,15},{10,... | collective-permute-start | bytes 196616 | tf_op jit(solution)/shard_map/cells3/ppermute | solution.py:29
  6.9 7.2 %collective-permute-start.1 = (bf16[2,64,256]{2,1,0:T(8,128)(2,1)S(1)}, bf16[2,64,256]{2,1,0:T(8,128)(2,1)S(1)}, u32[]{:S(2)}, u32[]{:S(2)}) collective-permute-start(bf16[2,64,256]{2,1,0:T(8,128)(2,1)S(1)} %pad_maximum_fusion.3), channel_id=1, source_target_pairs={{0,4},{1,5},{2,6},{3,7},{4,0},{5,1},{6,2},{7,3},{8,12},{9,13},{10,... | collective-permute-start | bytes 196616 | tf_op jit(solution)/shard_map/cells2/ppermute | solution.py:29
  7.0 7.5 %collective-permute-start.3 = (bf16[2,64,256]{2,1,0:T(8,128)(2,1)S(1)}, bf16[2,64,256]{2,1,0:T(8,128)(2,1)S(1)}, u32[]{:S(2)}, u32[]{:S(2)}) collective-permute-start(bf16[2,64,256]{2,1,0:T(8,128)(2,1)S(1)} %pad_maximum_fusion.4), channel_id=1, source_target_pairs={{0,2},{1,3},{2,0},{3,1},{4,6},{5,7},{6,4},{7,5},{8,10},{9,11},{10,... | collective-permute-start | bytes 196616 | tf_op jit(solution)/shard_map/cells1/ppermute | solution.py:29
  7.8 2.0 %collective-permute-start.2 = (bf16[256,512]{1,0:T(8,128)(2,1)S(1)}, bf16[256,512]{1,0:T(8,128)(2,1)S(1)}, u32[]{:S(2)}, u32[]{:S(2)}) collective-permute-start(bf16[256,512]{1,0:T(8,128)(2,1)S(1)} %get-tuple-element.29), channel_id=1, source_target_pairs={{0,1},{1,0},{2,3},{3,2},{4,5},{5,4},{6,7},{7,6},{8,9},{9,8},{10,11... | collective-permute-start | bytes 786440 | tf_op jit(solution)/shard_map/coef_core/ppermute | solution.py:24
  7.8 8.7 %collective-permute-start.4 = (bf16[256,512]{1,0:T(8,128)(2,1)S(1)}, bf16[256,512]{1,0:T(8,128)(2,1)S(1)}, u32[]{:S(2)}, u32[]{:S(2)}) collective-permute-start(bf16[256,512]{1,0:T(8,128)(2,1)S(1)} %get-tuple-element.61), channel_id=1, source_target_pairs={{0,8},{1,17},{2,10},{3,19},{4,12},{5,21},{6,14},{7,23},{8,0},{9,25... | collective-permute-start | bytes 786440 | tf_op jit(solution)/shard_map/squares0/ppermute | solution.py:37
  10.1 8.3 %collective-permute-start.7 = (bf16[64,512]{1,0:T(8,128)(2,1)S(1)}, bf16[64,512]{1,0:T(8,128)(2,1)S(1)}, u32[]{:S(2)}, u32[]{:S(2)}) collective-permute-start(bf16[64,512]{1,0:T(8,128)(2,1)S(1)} %fusion.6), channel_id=1, source_target_pairs={{0,6},{1,7},{2,4},{3,5},{4,2},{5,3},{6,0},{7,1},{8,14},{9,15},{10,... | collective-permute-start | bytes 196616 | tf_op jit(solution)/shard_map/fit3/ppermute | solution.py:29
  14.4 5.5 %collective-permute-start.8 = (bf16[64,512]{1,0:T(8,128)(2,1)S(1)}, bf16[64,512]{1,0:T(8,128)(2,1)S(1)}, u32[]{:S(2)}, u32[]{:S(2)}) collective-permute-start(bf16[64,512]{1,0:T(8,128)(2,1)S(1)} %fusion.7), channel_id=1, source_target_pairs={{0,4},{1,5},{2,6},{3,7},{4,0},{5,1},{6,2},{7,3},{8,12},{9,13},{10,... | collective-permute-start | bytes 196616 | tf_op jit(solution)/shard_map/fit2/ppermute | solution.py:29
  14.8 5.1 %collective-permute-start.9 = (bf16[64,512]{1,0:T(8,128)(2,1)S(1)}, bf16[64,512]{1,0:T(8,128)(2,1)S(1)}, u32[]{:S(2)}, u32[]{:S(2)}) collective-permute-start(bf16[64,512]{1,0:T(8,128)(2,1)S(1)} %fusion.8), channel_id=1, source_target_pairs={{0,2},{1,3},{2,0},{3,1},{4,6},{5,7},{6,4},{7,5},{8,10},{9,11},{10,... | collective-permute-start | bytes 196616 | tf_op jit(solution)/shard_map/fit1/ppermute | solution.py:29
  16.7 7.9 %collective-permute-start.6 = (bf16[256,256]{1,0:T(8,128)(2,1)S(1)}, bf16[256,256]{1,0:T(8,128)(2,1)S(1)}, u32[]{:S(2)}, u32[]{:S(2)}) collective-permute-start(bf16[256,256]{1,0:T(8,128)(2,1)S(1)} %pad_maximum_fusion), channel_id=1, source_target_pairs={{0,1},{1,0},{2,3},{3,2},{4,5},{5,4},{6,7},{7,6},{8,9},{9,8},{10,11... | collective-permute-start | bytes 393224 | tf_op jit(solution)/shard_map/cells_core/ppermute | solution.py:24
  16.8 7.9 %collective-permute-start.5 = (bf16[256,512]{1,0:T(8,128)(2,1)S(1)}, bf16[256,512]{1,0:T(8,128)(2,1)S(1)}, u32[]{:S(2)}, u32[]{:S(2)}) collective-permute-start(bf16[256,512]{1,0:T(8,128)(2,1)S(1)} %convert_element_type.82), channel_id=1, source_target_pairs={{0,16},{1,9},{2,18},{3,11},{4,20},{5,13},{6,22},{7,15},{8,24},{9,1... | collective-permute-start | bytes 786440 | tf_op jit(solution)/shard_map/squares1/ppermute | solution.py:37
  20.1 6.2 %collective-permute-start.12 = (bf16[64,512]{1,0:T(8,128)(2,1)S(1)}, bf16[64,512]{1,0:T(8,128)(2,1)S(1)}, u32[]{:S(2)}, u32[]{:S(2)}) collective-permute-start(bf16[64,512]{1,0:T(8,128)(2,1)S(1)} %fusion.9), channel_id=1, source_target_pairs={{0,6},{1,7},{2,4},{3,5},{4,2},{5,3},{6,0},{7,1},{8,14},{9,15},{10,... | collective-permute-start | bytes 196616 | tf_op jit(solution)/shard_map/residual3/ppermute | solution.py:29
  23.1 4.5 %collective-permute-start.11 = (bf16[64,512]{1,0:T(8,128)(2,1)S(1)}, bf16[64,512]{1,0:T(8,128)(2,1)S(1)}, u32[]{:S(2)}, u32[]{:S(2)}) collective-permute-start(bf16[64,512]{1,0:T(8,128)(2,1)S(1)} %fusion.9), channel_id=1, source_target_pairs={{0,2},{1,3},{2,0},{3,1},{4,6},{5,7},{6,4},{7,5},{8,10},{9,11},{10,... | collective-permute-start | bytes 196616 | tf_op jit(solution)/shard_map/residual1/ppermute | solution.py:29
  23.1 5.3 %collective-permute-start.10 = (bf16[64,512]{1,0:T(8,128)(2,1)S(1)}, bf16[64,512]{1,0:T(8,128)(2,1)S(1)}, u32[]{:S(2)}, u32[]{:S(2)}) collective-permute-start(bf16[64,512]{1,0:T(8,128)(2,1)S(1)} %fusion.9), channel_id=1, source_target_pairs={{0,4},{1,5},{2,6},{3,7},{4,0},{5,1},{6,2},{7,3},{8,12},{9,13},{10,... | collective-permute-start | bytes 196616 | tf_op jit(solution)/shard_map/residual2/ppermute | solution.py:29
  24.6 3.7 %copy-start.5 = (f32[256]{0:T(256)S(1)}, f32[256]{0:T(256)}, u32[]{:S(2)}) copy-start(f32[256]{0:T(256)} %param.9) | copy-start | bytes 3076
  28.5 1.6 %collective-permute-start.13 = (bf16[256,512]{1,0:T(8,128)(2,1)S(1)}, bf16[256,512]{1,0:T(8,128)(2,1)S(1)}, u32[]{:S(2)}, u32[]{:S(2)}) collective-permute-start(bf16[256,512]{1,0:T(8,128)(2,1)S(1)} %constant_dynamic-update-slice_fusion), channel_id=1, source_target_pairs={{0,1},{1,0},{2,3},{3,2},{4,5},{5,4},{6,7},{7,6},{8,9},{9,8},{10,11... | collective-permute-start | bytes 786440 | tf_op jit(solution)/shard_map/residual_core/ppermute | solution.py:24
  30.5 2.1 %collective-permute-start.16 = (bf16[256,512]{1,0:T(8,128)(2,1)S(1)}, bf16[256,512]{1,0:T(8,128)(2,1)S(1)}, u32[]{:S(2)}, u32[]{:S(2)}) collective-permute-start(bf16[256,512]{1,0:T(8,128)(2,1)S(1)} %get-tuple-element.57), channel_id=1, source_target_pairs={{0,1},{1,0},{2,3},{3,2},{4,5},{5,4},{6,7},{7,6},{8,9},{9,8},{10,11... | collective-permute-start | bytes 786440 | tf_op jit(solution)/shard_map/coef_core/ppermute | solution.py:24
  30.8 6.5 %collective-permute-start.14 = (bf16[256,512]{1,0:T(8,128)(2,1)S(1)}, bf16[256,512]{1,0:T(8,128)(2,1)S(1)}, u32[]{:S(2)}, u32[]{:S(2)}) collective-permute-start(bf16[256,512]{1,0:T(8,128)(2,1)S(1)} %get-tuple-element.59), channel_id=1, source_target_pairs={{0,8},{1,17},{2,10},{3,19},{4,12},{5,21},{6,14},{7,23},{8,0},{9,25... | collective-permute-start | bytes 786440 | tf_op jit(solution)/shard_map/squares0/ppermute | solution.py:37
  32.9 6.5 %collective-permute-start.17 = (bf16[64,512]{1,0:T(8,128)(2,1)S(1)}, bf16[64,512]{1,0:T(8,128)(2,1)S(1)}, u32[]{:S(2)}, u32[]{:S(2)}) collective-permute-start(bf16[64,512]{1,0:T(8,128)(2,1)S(1)} %get-tuple-element.64), channel_id=1, source_target_pairs={{0,6},{1,7},{2,4},{3,5},{4,2},{5,3},{6,0},{7,1},{8,14},{9,15},{10,... | collective-permute-start | bytes 196616 | tf_op jit(solution)/shard_map/fit3/ppermute | solution.py:29
  36.0 4.7 %collective-permute-start.19 = (bf16[64,512]{1,0:T(8,128)(2,1)S(1)}, bf16[64,512]{1,0:T(8,128)(2,1)S(1)}, u32[]{:S(2)}, u32[]{:S(2)}) collective-permute-start(bf16[64,512]{1,0:T(8,128)(2,1)S(1)} %get-tuple-element.65), channel_id=1, source_target_pairs={{0,2},{1,3},{2,0},{3,1},{4,6},{5,7},{6,4},{7,5},{8,10},{9,11},{10,... | collective-permute-start | bytes 196616 | tf_op jit(solution)/shard_map/fit1/ppermute | solution.py:29
  36.1 5.6 %collective-permute-start.18 = (bf16[64,512]{1,0:T(8,128)(2,1)S(1)}, bf16[64,512]{1,0:T(8,128)(2,1)S(1)}, u32[]{:S(2)}, u32[]{:S(2)}) collective-permute-start(bf16[64,512]{1,0:T(8,128)(2,1)S(1)} %get-tuple-element.66), channel_id=1, source_target_pairs={{0,4},{1,5},{2,6},{3,7},{4,0},{5,1},{6,2},{7,3},{8,12},{9,13},{10,... | collective-permute-start | bytes 196616 | tf_op jit(solution)/shard_map/fit2/ppermute | solution.py:29
  37.4 8.7 %collective-permute-start.15 = (bf16[256,512]{1,0:T(8,128)(2,1)S(1)}, bf16[256,512]{1,0:T(8,128)(2,1)S(1)}, u32[]{:S(2)}, u32[]{:S(2)}) collective-permute-start(bf16[256,512]{1,0:T(8,128)(2,1)S(1)} %fusion.14), channel_id=1, source_target_pairs={{0,16},{1,9},{2,18},{3,11},{4,20},{5,13},{6,22},{7,15},{8,24},{9,1... | collective-permute-start | bytes 786440 | tf_op jit(solution)/shard_map/squares1/ppermute | solution.py:37
  41.7 6.6 %collective-permute-start.22 = (bf16[64,512]{1,0:T(8,128)(2,1)S(1)}, bf16[64,512]{1,0:T(8,128)(2,1)S(1)}, u32[]{:S(2)}, u32[]{:S(2)}) collective-permute-start(bf16[64,512]{1,0:T(8,128)(2,1)S(1)} %fusion.18), channel_id=1, source_target_pairs={{0,6},{1,7},{2,4},{3,5},{4,2},{5,3},{6,0},{7,1},{8,14},{9,15},{10,... | collective-permute-start | bytes 196616 | tf_op jit(solution)/shard_map/residual3/ppermute | solution.py:29
  43.7 5.1 %collective-permute-start.21 = (bf16[64,512]{1,0:T(8,128)(2,1)S(1)}, bf16[64,512]{1,0:T(8,128)(2,1)S(1)}, u32[]{:S(2)}, u32[]{:S(2)}) collective-permute-start(bf16[64,512]{1,0:T(8,128)(2,1)S(1)} %fusion.18), channel_id=1, source_target_pairs={{0,2},{1,3},{2,0},{3,1},{4,6},{5,7},{6,4},{7,5},{8,10},{9,11},{10,... | collective-permute-start | bytes 196616 | tf_op jit(solution)/shard_map/residual1/ppermute | solution.py:29
  44.0 5.4 %collective-permute-start.20 = (bf16[64,512]{1,0:T(8,128)(2,1)S(1)}, bf16[64,512]{1,0:T(8,128)(2,1)S(1)}, u32[]{:S(2)}, u32[]{:S(2)}) collective-permute-start(bf16[64,512]{1,0:T(8,128)(2,1)S(1)} %fusion.18), channel_id=1, source_target_pairs={{0,4},{1,5},{2,6},{3,7},{4,0},{5,1},{6,2},{7,3},{8,12},{9,13},{10,... | collective-permute-start | bytes 196616 | tf_op jit(solution)/shard_map/residual2/ppermute | solution.py:29
  49.5 1.6 %collective-permute-start.23 = (bf16[256,512]{1,0:T(8,128)(2,1)S(1)}, bf16[256,512]{1,0:T(8,128)(2,1)S(1)}, u32[]{:S(2)}, u32[]{:S(2)}) collective-permute-start(bf16[256,512]{1,0:T(8,128)(2,1)S(1)} %constant_dynamic-update-slice_fusion.4), channel_id=1, source_target_pairs={{0,1},{1,0},{2,3},{3,2},{4,5},{5,4},{6,7},{7,6},{8,9},{9,8},{10,11... | collective-permute-start | bytes 786440 | tf_op jit(solution)/shard_map/residual_core/ppermute | solution.py:24
  49.8 2.3 %copy-start = (f32[256,512]{1,0:T(8,128)}, f32[256,512]{1,0:T(8,128)S(1)}, u32[]{:S(2)}) copy-start(f32[256,512]{1,0:T(8,128)S(1)} %get-tuple-element.55) | copy-start | bytes 1572868
  49.9 2.3 %copy-start.1 = (f32[256,512]{1,0:T(8,128)}, f32[256,512]{1,0:T(8,128)S(1)}, u32[]{:S(2)}) copy-start(f32[256,512]{1,0:T(8,128)S(1)} %get-tuple-element.56) | copy-start | bytes 1572868
